TPU v7x, 256 devices: a whole 4x4x8 slice. The times are simulated.
256 devices in a mesh: sample: 2 (over z_hi), fsdp: 4 (over x), seq: 32 (over y, z_lo, core).
Axes of the slice: x: 4, y: 4, z: 8 (z_hi: 2, z_lo: 4; z = z_hi * 4 + z_lo), core: 2. Of those that a mesh axis runs over, the one named last changes fastest.
Arguments:
- token_act: bfloat16 [8, 4096, 768], P(('sample', 'fsdp'), 'seq'), may hold values from -40 to 40
- token_cond: bfloat16 [8, 4096, 768], P(('sample', 'fsdp'), 'seq'), may hold values from -40 to 40
- pair_bias: bfloat16 [16, 4096, 4096], P('fsdp', 'seq'), may hold values from -8 to 296
- token_mask: int32 [4096], P('seq'), may hold values 0 or 1
- ada_weights: bfloat16 [4, 768, 768], P(None, None, 'fsdp'), may hold values from -0.21875 to 0.21875
- attention_in: bfloat16 [4, 768, 768], P(None, None, 'fsdp'), may hold values from -0.21875 to 0.21875
- attention_out: bfloat16 [768, 768], P('fsdp'), may hold values from -0.21875 to 0.21875
- transition_in: bfloat16 [2, 768, 1536], P(None, None, 'fsdp'), may hold values from -0.21875 to 0.21875
- transition_out: bfloat16 [1536, 768], P('fsdp'), may hold values from -0.15625 to 0.15625
- token_vectors: float32 [3, 768], replicated, may hold values from -4 to 4
- atom_skip: bfloat16 [8, 32768, 128], P(('sample', 'fsdp'), 'seq'), may hold values from -40 to 40
- atom_cond: bfloat16 [32768, 128], P('seq'), may hold values from -40 to 40
- atom_bias: bfloat16 [4, 32768, 128], P(None, 'seq'), may hold values from -6 to 296
- window_bounds: int32 [1024, 2], P('seq'), may hold values from 0 to 32768, as said below
- atom_token: int32 [32768], P('seq'), may hold values from 0 to 4095, as said below
- atom_weights: bfloat16 [7, 128, 128], P(None, None, 'fsdp'), may hold values from -0.5 to 0.5
- token_to_atom: bfloat16 [768, 128], P('fsdp'), may hold values from -0.21875 to 0.21875
- atom_vectors: float32 [2, 128], replicated, may hold values from -4 to 4
- position_out: bfloat16 [3, 128], replicated, may hold values from -0.5 to 0.5
Outputs:
- token_out: bfloat16 [8, 4096, 768], P(('sample', 'fsdp'), 'seq')
- position_update: float32 [8, 3, 32768], P(('sample', 'fsdp'), None, 'seq')
Inputs may be any that keep to these rules, and one draw needn't show every extreme that they name: `window_bounds`: row b belongs to the atoms 32 * b to 32 * b + 31; column 0 is at least 0 and at least 32 * b - 48, and at most 32 * b; column 1 is at least 32 * b + 32, at most 32 * b + 80 and at most 32768. `atom_token`: atoms are numbered in token order: the value never falls from one atom to the next, the first atom belongs to token 0, the last to token 4095, and every token owns 1 to 24 atoms.
All inputs are finite; a program needn't handle non-finite values. No bound on the sum of `token_mask` on one device may be relied on, other than what follows from the above.
Results may differ from a plain program's by a relative error of at most 0.014.
Values may be sent and summed in bfloat16 or wider, within the bound.
No kernel may reach another device: no remote copies, remote signals or barrier semaphores. Data moves between devices by JAX's collectives and lax.ppermute only.
A program may use at most 128 MiB of HBM per device.

v0:
```python
import math

import jax
import jax.numpy as jnp
from jax import lax
from jax.experimental import pallas as pl
from jax.experimental.pallas import tpu as pltpu
from jax.sharding import PartitionSpec as P

EPS = 1e-05
FAR = -1e30
SENT = 1e30
LOG2E = 1.4426950408889634
HD = 48
HA = 4
WQ = 32
WK = 128
RIM = 48
NX = 4
NY = 4
NZ = 4
NC = 2
ROWS = 128
DIM = 768
COLS = 192
SLOTS = 4
HALF = SLOTS * COLS
HEADS = 4
ATOMS = 1024
EXT = ATOMS + 2 * RIM
CHUNK = 112
CHUNKS = EXT // CHUNK
CA = 128
F32 = jnp.float32
BF16 = jnp.bfloat16


def x_shift(a, k):
    return lax.ppermute(a, "fsdp", [(i, (i + k) % NX) for i in range(NX)])


def y_shift(a, k):
    group = NZ * NC
    pairs = [(t, ((t // group + k) % NY) * group + t % group) for t in range(NY * group)]
    return lax.ppermute(a, "seq", pairs)


def z_shift(a, k):
    group = NZ * NC
    pairs = [
        (t, (t // group) * group + ((t // NC + k) % NZ) * NC + t % NC) for t in range(NY * group)
    ]
    return lax.ppermute(a, "seq", pairs)


def y_exchange(a):
    group = NZ * NC
    groups = [[y * group + n for y in range(NY)] for n in range(group)]
    return lax.all_to_all(
        a, "seq", split_axis=0, concat_axis=0, axis_index_groups=groups, tiled=True
    )


def y_collect(a):
    group = NZ * NC
    groups = [[y * group + n for y in range(NY)] for n in range(group)]
    return lax.all_gather(a, "seq", axis=0, axis_index_groups=groups)


def c_shift(a):
    return lax.ppermute(a, "seq", [(t, t ^ 1) for t in range(NY * NZ * NC)])


def norm(values):
    center = values - jnp.mean(values, axis=-1, keepdims=True)
    spread = jnp.mean(center * center, axis=-1, keepdims=True)
    return center * lax.rsqrt(spread + EPS)


def sigmoid(v):
    return 1.0 / (1.0 + jnp.exp(-v))


def dot(a, b):
    return jnp.dot(a, b, preferred_element_type=F32)


def dot_nt(a, b):
    return lax.dot_general(a, b, (((1,), (1,)), ((), ())), preferred_element_type=F32)


def kernel_call(body, name, out_shape, args, scalars=(), scratch=(), flops=0, size=0, free=0):
    def whole(a):
        return pl.BlockSpec(
            a.shape, lambda i, n=len(a.shape): (0,) * n, pipeline_mode=pl.Buffered(1)
        )

    args = [
        a if i < free else pltpu.with_memory_space_constraint(a, pltpu.HBM)
        for i, a in enumerate(args)
    ]
    return pl.pallas_call(
        body,
        grid=(1,),
        out_shape=out_shape,
        in_specs=[pl.BlockSpec(memory_space=pltpu.SMEM)] * len(scalars) + [whole(a) for a in args],
        out_specs=jax.tree.map(whole, out_shape),
        scratch_shapes=list(scratch),
        compiler_params=pltpu.CompilerParams(
            dimension_semantics=("arbitrary",), vmem_limit_bytes=24 << 20
        ),
        cost_estimate=pl.CostEstimate(flops=flops, bytes_accessed=size, transcendentals=0),
        name=name,
    )(*scalars, *args)


def shape(dims, kind=BF16):
    return pltpu.HBM(dims, kind)


def sent_shape(dims, kind=BF16):
    return jax.ShapeDtypeStruct(dims, kind)


def prepare_body(pos, act, cond, *outs):
    f = pos[0]
    normed = norm(cond[...].astype(F32)).astype(BF16)
    hat = norm(act[...].astype(F32))
    for k in range(NX):
        dest = lax.rem(f + k, NX)
        part = hat[:, 0:COLS]
        for j in range(1, NX):
            part = jnp.where(dest == j, hat[:, j * COLS : (j + 1) * COLS], part)
        outs[k][:, 0:DIM] = normed
        outs[k][:, DIM : DIM + COLS] = part.astype(BF16)


def adaptive_body(m0, m1, m2, m3, ada, offset, maps, attend, message):
    parts = (m0, m1, m2, m3)
    normed = jnp.concatenate([m[:, 0:DIM] for m in parts], axis=0)
    hat = jnp.concatenate([m[:, DIM : DIM + COLS] for m in parts], axis=0).astype(F32)
    message[DIM:, :] = maps[...]
    for n in range(2):
        scale = sigmoid(dot(normed, ada[2 * n]) + offset[n : n + 1, :])
        result = (scale * hat + dot(normed, ada[2 * n + 1])).astype(BF16)
        wide = jnp.concatenate([result[k * ROWS : (k + 1) * ROWS] for k in range(NX)], axis=1)
        if n == 0:
            attend[...] = wide
        else:
            for i in range(DIM // 128):
                message[i * ROWS : (i + 1) * ROWS, :] = wide[:, i * 128 : (i + 1) * 128]


def gathered_rows(part, j):
    return jnp.concatenate(
        [part[:, ((r - j) % NX) * COLS : ((r - j) % NX + 1) * COLS] for r in range(NX)],
        axis=0,
    )


def project_body(pos, a0, a1, a2, a3, weights, offset, mask, q, kv, g):
    f = pos[0]
    parts = (a0, a1, a2, a3)
    sums = [None] * 4
    for j in range(NX):
        rows = gathered_rows(parts[j][...], j)
        at = pl.multiple_of(lax.rem(f + NX - j, NX) * COLS, COLS)
        for n in range(4):
            term = dot(rows, weights[n, pl.ds(at, COLS), :])
            sums[n] = term if j == 0 else sums[n] + term
    live = mask[...] > 0
    for r in range(NX):
        own = slice(r * ROWS, (r + 1) * ROWS)
        to = slice(r * COLS, (r + 1) * COLS)
        q[:, to] = ((sums[0][own] + offset[0:1, :]) * (LOG2E / math.sqrt(HD))).astype(BF16)
        kv[0:ROWS, to] = jnp.where(live, sums[1][own], SENT).astype(BF16)
        kv[ROWS:, to] = sums[2][own].astype(BF16)
        g[:, to] = sums[3][own].astype(BF16)


def hidden_body(pos, parts, w_in, w_out, out):
    f = pos[0]
    gate, up = None, None
    for j in range(NX):
        src = lax.rem(f + NX - j, NX)
        wide = jnp.concatenate(
            [parts[src, i * ROWS : (i + 1) * ROWS, :] for i in range(DIM // 128)], axis=1
        )
        rows = gathered_rows(wide, j)
        at = pl.multiple_of(src * COLS, COLS)
        gate_term = dot(rows, w_in[0, pl.ds(at, COLS), :])
        up_term = dot(rows, w_in[1, pl.ds(at, COLS), :])
        gate = gate_term if j == 0 else gate + gate_term
        up = up_term if j == 0 else up + up_term
    hidden = (gate / (1.0 + jnp.exp(-gate)) * up).astype(BF16)
    out[...] = dot(hidden, w_out[...])


KEYS = NZ * NC * ROWS


def attention_body(pos, *refs):
    q = refs[0]
    pairs = refs[1:9]
    bias = refs[9]
    out = refs[10:14]
    q_all, key_all, value_all, far_row, bias_all, stats, probs = refs[14:21]
    scores = refs[21:23]
    h = pl.program_id(0)

    @pl.when(h == 0)
    def _():
        unit = (lax.broadcasted_iota(jnp.int32, (8, 128), 1) == 0).astype(F32).astype(BF16)
        for side in range(2):
            core = pos[2] if side == 0 else 1 - pos[2]
            for n in range(NZ):
                block = pairs[side * NZ + n][0:ROWS, :]
                place = lax.rem(pos[1] + NZ - n, NZ) * NC + core
                at = pl.multiple_of(place * ROWS, ROWS)
                first = dot_nt(unit, block[:, 0:128])
                far_row[:, pl.ds(at, ROWS)] = jnp.where(first > 1e20, FAR, 0.0)
                wide = block.astype(F32)
                key_all[pl.ds(at, ROWS), :] = jnp.where(wide[:, 0:1] > 1e20, 0.0, wide).astype(BF16)
                value_all[pl.ds(at, ROWS), :] = pairs[side * NZ + n][ROWS:, :]
        for n in range(NY):
            q_all[n * ROWS : (n + 1) * ROWS, :] = q[lax.rem(pos[0] + NY - n, NY)]
        stats[...] = jnp.zeros_like(stats)

    for n in range(NY):
        part = bias[lax.rem(pos[0] + NY - n, NY), 0]
        bias_all[n] = part.astype(F32) * LOG2E + far_row[0:1, :]

    lane = lax.broadcasted_iota(jnp.int32, (NY * ROWS, 256), 1)
    slot = lax.broadcasted_iota(jnp.int32, (ROWS, 128), 1)
    windows, mines, rows = [], [], []
    for s in range(SLOTS):
        lane0 = COLS * s + HD * h
        start = jnp.minimum(lane0 // 128, (HALF - 256) // 128)
        off = lane0 - start * 128
        window = pl.ds(pl.multiple_of(start * 128, 128), 256)
        mine = (lane >= off) & (lane < off + HD)
        windows.append(window)
        mines.append(mine)
        rows.append(jnp.where(mine, q_all[:, window].astype(F32), 0.0).astype(BF16))

    tile = KEYS // NY

    def score(s, j):
        keys = slice(j * tile, (j + 1) * tile)
        scores[s % 2][:, keys] = dot_nt(rows[s], key_all[keys, windows[s]])

    for j in range(NY):
        score(0, j)
    for s in range(SLOTS):
        index = s * HEADS + h
        of_max = (lax.rem(slot, 16) == index) & (slot < 48)
        of_total = (lax.rem(slot, 16) == index) & (slot >= 48) & (slot < 96)
        totals = []
        for n in range(NY):
            if s + 1 < SLOTS:
                score(s + 1, n)
            own = slice(n * ROWS, (n + 1) * ROWS)
            part = scores[s % 2][own, :] + bias_all[n]
            top = jnp.max(part, axis=1, keepdims=True)
            part = jnp.exp2(part - top)
            total = jnp.sum(part, axis=1, keepdims=True)
            probs[own, :] = part.astype(BF16)
            totals.append(total)
            stats[n] = jnp.where(of_max, top, jnp.where(of_total, total, stats[n]))
        summed = dot(probs[...], value_all[:, windows[s]])
        for n in range(NY):
            own = slice(n * ROWS, (n + 1) * ROWS)
            scaled = summed[own] * (1.0 / totals[n])
            before = out[n][:, windows[s]].astype(F32)
            out[n][:, windows[s]] = jnp.where(mines[s][own], scaled, before).astype(BF16)

    @pl.when(h == HEADS - 1)
    def _():
        third = lax.rem(slot // 16, 3)
        for n in range(NY):
            whole = stats[n]
            high = whole.astype(BF16).astype(F32)
            rest = whole - high
            middle = rest.astype(BF16).astype(F32)
            low = rest - middle
            sent = jnp.where(third == 0, high, jnp.where(third == 1, middle, low))
            out[n][:, HALF : HALF + 128] = sent.astype(BF16)


def attention(pos, q, pairs, bias):
    once = pl.Buffered(1)
    in_specs = [pl.BlockSpec(memory_space=pltpu.SMEM)]
    in_specs += [pl.BlockSpec((NY, ROWS, DIM), lambda h: (0, 0, 0), pipeline_mode=once)]
    in_specs += [pl.BlockSpec((2 * ROWS, HALF), lambda h: (0, 0), pipeline_mode=once)] * 8
    in_specs += [pl.BlockSpec((NY, 1, ROWS, KEYS), lambda h: (0, h, 0, 0))]
    return pl.pallas_call(
        attention_body,
        grid=(HEADS,),
        out_shape=[shape((ROWS, HALF + 128))] * 4,
        in_specs=in_specs,
        out_specs=[pl.BlockSpec((ROWS, HALF + 128), lambda h: (0, 0))] * 4,
        scratch_shapes=[
            pltpu.VMEM((NY * ROWS, HALF), BF16),
            pltpu.VMEM((KEYS, HALF), BF16),
            pltpu.VMEM((KEYS, HALF), BF16),
            pltpu.VMEM((8, KEYS), F32),
            pltpu.VMEM((NY, ROWS, KEYS), F32),
            pltpu.VMEM((NY, ROWS, 128), F32),
            pltpu.VMEM((NY * ROWS, KEYS), BF16),
            pltpu.VMEM((NY * ROWS, KEYS), F32),
            pltpu.VMEM((NY * ROWS, KEYS), F32),
        ],
        compiler_params=pltpu.CompilerParams(
            dimension_semantics=("arbitrary",), vmem_limit_bytes=36 << 20
        ),
        cost_estimate=pl.CostEstimate(
            flops=SLOTS * 4 * 512 * 1024 * 512 * 2,
            bytes_accessed=6 << 20,
            transcendentals=4 << 20,
        ),
        name="attention",
    )(pos, *(pltpu.with_memory_space_constraint(a, pltpu.HBM) for a in (q, *pairs, bias)))


def combined(parts):
    tops, totals = [], []
    for o in parts:
        sent = o[:, HALF : HALF + 128].astype(F32)
        whole = sent + pltpu.roll(sent, 128 - 16, 1) + pltpu.roll(sent, 128 - 32, 1)
        tops.append(whole)
        totals.append(pltpu.roll(whole, 128 - 48, 1))
    used = lax.broadcasted_iota(jnp.int32, (ROWS, 128), 1) < SLOTS * HEADS
    tops = [jnp.where(used, t, 0.0) for t in tops]
    totals = [jnp.where(used, t, 1.0) for t in totals]
    top = jnp.maximum(jnp.maximum(tops[0], tops[1]), jnp.maximum(tops[2], tops[3]))
    shares = [n * jnp.exp2(t - top) for t, n in zip(tops, totals)]
    inverse = 1.0 / (shares[0] + shares[1] + shares[2] + shares[3])
    head = lax.broadcasted_iota(jnp.int32, (128, HALF), 0) * HD
    lane = lax.broadcasted_iota(jnp.int32, (128, HALF), 1)
    spread = ((lane >= head) & (lane < head + HD)).astype(F32).astype(BF16)
    attended = None
    for o, share in zip(parts, shares):
        share = share * inverse
        high = share.astype(BF16)
        low = (share - high.astype(F32)).astype(BF16)
        term = (dot(high, spread) + dot(low, spread)) * o[:, 0:HALF].astype(F32)
        attended = term if attended is None else attended + term
    return attended


def combine_body(*refs):
    gate, ffn, w_out, w_atom, act = refs[4:9]
    outs = refs[9:]
    attended = combined(refs[0:4])
    gated = (attended * sigmoid(gate[...].astype(F32))).astype(BF16)
    for r in range(NX):
        part = dot(gated[:, r * COLS : (r + 1) * COLS], w_out[...]) + ffn[r * ROWS : (r + 1) * ROWS]
        small = part.astype(BF16)
        rows = dot(small, w_atom[...])
        if r == 0:
            outs[0][...] = part + act[...].astype(F32)
            outs[4][...] = rows + dot(act[...], w_atom[...])
        else:
            outs[r][...] = small
            outs[4 + r][...] = rows.astype(BF16)


def atom_first_body(starts, maps, cond, tokens, offset, *outs):
    weights, project, scale, shift, select = outs
    for src in range(NX):
        project[src * COLS : (src + 1) * COLS, :] = maps[src, DIM : DIM + COLS, :]
        for i in range(7):
            line = DIM + COLS + i * 32
            weights[i, src * 32 : (src + 1) * 32, :] = maps[src, line : line + 32, :]
    normed = norm(cond[...].astype(F32)).astype(BF16)
    scale[...] = sigmoid(dot_nt(normed, weights[0]) + offset[0:1, :])
    shift[...] = dot_nt(normed, weights[1])
    row = lax.broadcasted_iota(jnp.int32, (128, CHUNK), 0)
    for i in range(CHUNKS):
        hit = ((row + starts[i]) == tokens[i : i + 1, :]).astype(F32)
        select[i * CHUNK : (i + 1) * CHUNK, :] = hit.T.astype(BF16)


def atom_body(pos, starts, bounds, near, far, before, own_skip, after, *refs):
    scale, shift, select, weights, offset, bias, spots, out = refs[0:8]
    table, skip, state, xs, qs, ks, vs, gs, at_all = refs[8:]
    skip[0:RIM, :] = before[0:RIM, :]
    skip[RIM : RIM + ATOMS, :] = own_skip[...]
    skip[RIM + ATOMS :, :] = after[0:RIM, :]
    y, z, c = pos[0], pos[1], pos[2]
    for ky in range(NY):
        for kz in range(NZ):
            place = lax.rem(y + NY - ky, NY) * (NZ * NC) + lax.rem(z + NZ - kz, NZ) * NC
            n = (kz * NY + ky) * ROWS
            own = pl.multiple_of((place + c) * ROWS, ROWS)
            other = pl.multiple_of((place + 1 - c) * ROWS, ROWS)
            table[pl.ds(own, ROWS), :] = near[n : n + ROWS, :]
            table[pl.ds(other, ROWS), :] = far[n : n + ROWS, :]
    for i in range(CHUNKS):
        rows = slice(i * CHUNK, (i + 1) * CHUNK)
        taken = table[pl.ds(pl.multiple_of(starts[i], 16), 128), :]
        now = skip[rows, :].astype(F32) + dot(select[rows, :], taken)
        state[rows, :] = now
        xs[rows, :] = (scale[rows, :] * norm(now) + shift[rows, :]).astype(BF16)
    x = xs[...]
    own = slice(RIM, RIM + ATOMS)
    mine = xs[own, :]
    qs[...] = (
        (dot_nt(mine, weights[2]) + offset[1:2, :]) * (LOG2E / math.sqrt(CA // HA))
    ).astype(BF16)
    ks[...] = dot_nt(x, weights[3]).astype(BF16)
    vs[...] = dot_nt(x, weights[4]).astype(BF16)
    gs[...] = sigmoid(dot_nt(mine, weights[5]).astype(BF16).astype(F32))
    width = CA // HA
    head_of_row = lax.broadcasted_iota(jnp.int32, (HA * WQ, CA), 0) // WQ
    head_of_lane = lax.broadcasted_iota(jnp.int32, (HA * WQ, CA), 1) // width
    same = head_of_row == head_of_lane
    lane_head = lax.broadcasted_iota(jnp.int32, (WQ, CA), 1) // width
    key_slot = lax.broadcasted_iota(jnp.int32, (HA * WQ, WK), 1)

    def window(b):
        rows = pl.ds(pl.multiple_of(b * WQ, WQ), WQ)
        span = pl.ds(pl.multiple_of(b * WQ, WQ), WK)
        one = qs[rows, :].astype(F32)
        four = jnp.where(same, jnp.concatenate([one] * HA, axis=0), 0.0).astype(BF16)
        extra = jnp.concatenate([bias[i, rows, :] for i in range(HA)], axis=0).astype(F32)
        scores = dot_nt(four, ks[span, :]) + extra * LOG2E
        base = pos[3] + b * WQ - RIM
        low = bounds[0, b] - base
        high = bounds[1, b] - base
        scores = jnp.where((key_slot >= low) & (key_slot < high), scores, FAR)
        probs = jnp.exp2(scores - jnp.max(scores, axis=1, keepdims=True))
        total = jnp.sum(probs, axis=1, keepdims=True)
        summed = dot(probs.astype(BF16), vs[span, :]) * (1.0 / total)
        picked = summed[0:WQ]
        for i in range(1, HA):
            picked = jnp.where(lane_head == i, summed[i * WQ : (i + 1) * WQ], picked)
        at_all[rows, :] = picked

    def windows(step, carry):
        for i in range(8):
            window(step * 8 + i)
        return carry

    lax.fori_loop(0, ATOMS // WQ // 8, windows, 0)
    gated = (at_all[...] * gs[...]).astype(BF16)
    new = state[own, :] + dot_nt(gated, weights[6])
    final = norm(new).astype(BF16)
    update = dot_nt(spots[...], final)
    for i in range(3):
        out[i] = update[i : i + 1, :]


def per_device(
    token_act,
    token_cond,
    pair_bias,
    token_mask,
    ada_weights,
    attention_in,
    attention_out,
    transition_in,
    transition_out,
    token_vectors,
    atom_skip,
    atom_cond,
    atom_bias,
    window_bounds,
    atom_token,
    atom_weights,
    token_to_atom,
    atom_vectors,
    position_out,
):
    f = lax.axis_index("fsdp").astype(jnp.int32)
    t = lax.axis_index("seq").astype(jnp.int32)
    y, z, c = t // (NZ * NC), (t // NC) % NZ, t % NC
    f_pos = f.reshape(1)
    act = token_act[0]

    sent = kernel_call(
        prepare_body,
        "prepare",
        [sent_shape((ROWS, DIM + COLS))] * 4,
        (act, token_cond[0]),
        (f_pos,),
        size=2 << 20,
    )
    normed = [sent[0]] + [x_shift(sent[k], k) for k in (1, 2, 3)]
    edge_skip, edge_cond, edge_token, _ = lax.optimization_barrier(
        (atom_skip[0], atom_cond, atom_token, sent[0])
    )

    turned = jnp.swapaxes(atom_weights, 1, 2).reshape(7 * 32, CA)
    own_maps = jnp.concatenate([token_to_atom, turned], axis=0)
    skip = atom_skip[0]
    coded = jnp.stack([edge_token // 64, edge_token % 64]).astype(BF16)

    def edge(lo, hi):
        codes = jnp.pad(coded[:, lo:hi], ((0, 14), (0, CA - RIM)))
        return jnp.concatenate([edge_skip[lo:hi], edge_cond[lo:hi], codes], axis=0)

    size = lax.axis_size("seq")
    up = [(i, i + 1) for i in range(size - 1)]
    before = lax.ppermute(edge(ATOMS - RIM, ATOMS), "seq", up)
    after = lax.ppermute(edge(0, RIM), "seq", [(j, i) for i, j in up])

    span = pair_bias.shape[2] // NY
    cut = jnp.stack([pair_bias[:, :, i * span : (i + 1) * span] for i in range(NY)])
    bias = y_exchange(cut)

    def decoded(side):
        pair = side[2 * RIM : 2 * RIM + 2, 0:RIM].astype(jnp.int32)
        return pair[0] * 64 + pair[1]

    cond_ext = jnp.concatenate([before[RIM : 2 * RIM], atom_cond, after[RIM : 2 * RIM]], axis=0)
    token_ext = jnp.concatenate([decoded(before), atom_token, decoded(after)])
    by_chunk = token_ext.reshape(CHUNKS, CHUNK)
    token_count = size * ROWS
    starts = jnp.minimum((by_chunk[:, 0] // 16) * 16, token_count - 128)

    offsets = lax.dynamic_slice_in_dim(token_vectors, f * COLS, COLS, 1)
    attend, message = kernel_call(
        adaptive_body,
        "adaptive",
        [sent_shape((ROWS, DIM)), shape((DIM + COLS + 7 * 32, CA))],
        (*normed, ada_weights, offsets[0:2], own_maps),
        free=4,
        flops=4 * 2 * 512 * 768 * 192,
        size=3 << 20,
    )
    attend_all = [attend] + [x_shift(attend, k) for k in (1, 2, 3)]
    q, kv, gate = kernel_call(
        project_body,
        "project",
        [sent_shape((ROWS, DIM)), sent_shape((2 * ROWS, DIM)), shape((ROWS, DIM))],
        free=4,
        args=(*attend_all, attention_in, offsets[2:3], token_mask.reshape(ROWS, 1)),
        scalars=(f_pos,),
        flops=4 * 2 * 512 * 768 * 192,
        size=4 << 20,
    )
    near = [kv] + [z_shift(kv, k) for k in (1, 2, 3)]
    pairs = near + [c_shift(a) for a in near]
    q, _ = lax.optimization_barrier((q, pairs[NZ]))
    q_all = y_collect(q)

    message, _ = lax.optimization_barrier((message, q))
    messages = lax.all_gather(message, "fsdp", axis=0)
    ffn = kernel_call(
        hidden_body,
        "hidden",
        shape((NX * ROWS, DIM), F32),
        (messages, transition_in, transition_out),
        (f_pos,),
        flops=3 * 2 * 512 * 768 * 384,
        size=6 << 20,
    )
    atom_maps, project_full, scale, shift, select = kernel_call(
        atom_first_body,
        "atom_first",
        [
            shape((7, CA, CA)),
            shape((DIM, CA)),
            shape((EXT, CA), F32),
            shape((EXT, CA), F32),
            shape((EXT, 128)),
        ],
        (messages, cond_ext, by_chunk, atom_vectors),
        (starts,),
        flops=4 * EXT * CA * CA,
        size=3 << 20,
    )

    place = jnp.stack([y, z, c])
    out = attention(place, q_all, pairs, bias)
    parts = [out[0]] + [y_shift(out[k], NY - k) for k in (1, 2, 3)]
    sums = kernel_call(
        combine_body,
        "combine",
        [shape((ROWS, DIM), F32)]
        + [sent_shape((ROWS, DIM))] * 3
        + [sent_shape((ROWS, CA), F32)]
        + [sent_shape((ROWS, CA))] * 3,
        (*parts, gate, ffn, attention_out, project_full, act),
        free=4,
        flops=4 * 2 * 128 * 768 * (192 + 128) + 8 * 2 * 128 * 128 * 768,
        size=5 << 20,
    )
    arrived = [x_shift(sums[4 + k], NX - k) for k in (1, 2, 3)]
    rows = (
        sums[4] + arrived[0].astype(F32) + arrived[1].astype(F32) + arrived[2].astype(F32)
    ).astype(BF16)

    turns = [y_shift(rows, k) for k in (1, 2, 3)]
    by_y = jnp.concatenate([rows] + turns, axis=0)
    _, *partial = lax.optimization_barrier((by_y, *sums[1:4]))
    main = [x_shift(partial[k - 1], NX - k) for k in (1, 2, 3)]
    turns = [z_shift(by_y, k) for k in (1, 2, 3)]
    turns, main = lax.optimization_barrier((turns, main))
    by_z = jnp.concatenate([by_y] + turns, axis=0)
    token_result = (
        sums[0] + main[0].astype(F32) + main[1].astype(F32) + main[2].astype(F32)
    ).astype(BF16)
    by_c = c_shift(by_z)
    by_c, token_result = lax.optimization_barrier((by_c, token_result))

    scalars = (jnp.stack([y, z, c, t * ATOMS]), starts, window_bounds.T)
    update = kernel_call(
        atom_body,
        "atoms",
        shape((3, 1, ATOMS), F32),
        (
            by_z,
            by_c,
            before,
            skip,
            after,
            scale,
            shift,
            select,
            atom_maps,
            atom_vectors,
            atom_bias,
            position_out,
        ),
        scalars,
        free=2,
        scratch=[
            pltpu.VMEM((token_count, CA), BF16),
            pltpu.VMEM((EXT, CA), BF16),
            pltpu.VMEM((EXT, CA), F32),
            pltpu.VMEM((EXT, CA), BF16),
            pltpu.VMEM((ATOMS, CA), BF16),
            pltpu.VMEM((EXT, CA), BF16),
            pltpu.VMEM((EXT, CA), BF16),
            pltpu.VMEM((ATOMS, CA), F32),
            pltpu.VMEM((ATOMS, CA), F32),
        ],
        flops=2 * 1120 * 128 * 128 * 10,
        size=6 << 20,
    )
    return (token_result[None], jnp.swapaxes(update, 0, 1))


def solution(mesh):
    in_specs = (
        P(("sample", "fsdp"), "seq", None),
        P(("sample", "fsdp"), "seq", None),
        P("fsdp", "seq", None),
        P("seq"),
        P(None, None, "fsdp"),
        P(None, None, "fsdp"),
        P("fsdp", None),
        P(None, None, "fsdp"),
        P("fsdp", None),
        P(),
        P(("sample", "fsdp"), "seq", None),
        P("seq", None),
        P(None, "seq", None),
        P("seq", None),
        P("seq"),
        P(None, None, "fsdp"),
        P("fsdp", None),
        P(),
        P(),
    )
    out_specs = (P(("sample", "fsdp"), "seq", None), P(("sample", "fsdp"), None, "seq"))
    return jax.shard_map(
        per_device, mesh=mesh, in_specs=in_specs, out_specs=out_specs, check_vma=False
    )
```

profile of v0, /device:TPU:1, one launch (start us, length us, event | category | flops | bytes accessed | tf_op | source)
XLA Modules:
  0.0 203.0 jit_solution(7631267380548004374)
XLA Ops:
  7.2 2.8 %slice_bitcast_fusion.3 = (bf16[1,4,128,1024]{3,2,1,0:T(8,128)(2,1)S(1)}, bf16[1,4,128,1024]{3,2,1,0:T(8,128)(2,1)S(1)}, bf16[1,4,128,1024]{3,2,1,0:T(8,128)(2,1)S(1)}, bf16[1,4,128,1024]{3,2,1,0:T(8,128)(2,1)S(1)}) fusion(bf16[4,128,4096]{2,1,0:T(8,128)(2,1)} %param.21), kind=kLoop, calls=%fused_computation.4 | loop fusion | bytes 8388608 | tf_op jit(solution)/shard_map/stack | solution.py:509
  10.0 2.3 %pad_maximum_fusion = bf16[4,4,128,1024]{3,2,1,0:T(8,128)(2,1)} fusion(bf16[1,4,128,1024]{3,2,1,0:T(8,128)(2,1)S(1)} %get-tuple-element.90, bf16[1,4,128,1024]{3,2,1,0:T(8,128)(2,1)S(1)} %get-tuple-element.91, bf16[1,4,128,1024]{3,2,1,0:T(8,128)(2,1)S(1)} %get-tuple-element.89, bf16[1,4,128,1024]{3,2,1,0:T(8,128)(2,1)S(1)} %get-tuple-element.88), kind=kLoop, calls=%fused_computation | loop fusion | flops 6291456 | bytes 8388608 | tf_op jit(solution)/shard_map/stack | solution.py:509
  12.2 5.1 %all-to-all-start = ((bf16[4,4,128,1024]{3,2,1,0:T(8,128)(2,1)}), bf16[4,4,128,1024]{3,2,1,0:T(8,128)(2,1)}, u32[]{:S(2)}, u32[]{:S(2)}) async-start(bf16[4,4,128,1024]{3,2,1,0:T(8,128)(2,1)} %pad_maximum_fusion), calls=%async_computation | async-start | bytes 8388608 | tf_op jit(solution)/shard_map/all_to_all | solution.py:59
  17.4 1.6 prepare.1
  19.1 2.0 %collective-permute-start = (bf16[128,960]{1,0:T(8,128)(2,1)S(1)}, bf16[128,960]{1,0:T(8,128)(2,1)S(1)}, u32[]{:S(2)}, u32[]{:S(2)}) collective-permute-start(bf16[128,960]{1,0:T(8,128)(2,1)S(1)} %get-tuple-element.45), channel_id=1, source_target_pairs={{0,32},{32,64},{64,96},{96,0},{1,33},{33,65},{65,97},{97,1},{2,34}... | collective-permute-start | bytes 737288 | tf_op jit(solution)/shard_map/ppermute | solution.py:39
  21.2 2.5 %collective-permute-start.1 = (bf16[128,960]{1,0:T(8,128)(2,1)S(1)}, bf16[128,960]{1,0:T(8,128)(2,1)S(1)}, u32[]{:S(2)}, u32[]{:S(2)}) collective-permute-start(bf16[128,960]{1,0:T(8,128)(2,1)S(1)} %get-tuple-element.46), channel_id=1, source_target_pairs={{0,64},{32,96},{64,0},{96,32},{1,65},{33,97},{65,1},{97,33},{2,66}... | collective-permute-start | bytes 737288 | tf_op jit(solution)/shard_map/ppermute | solution.py:39
  23.6 1.2 collective-permute-start.2
  24.9 0.7 fusion.15
  25.6 4.9 %collective-permute-start.16 = (bf16[112,128]{1,0:T(8,128)(2,1)S(1)}, bf16[112,128]{1,0:T(8,128)(2,1)S(1)}, u32[]{:S(2)}, u32[]{:S(2)}) collective-permute-start(bf16[112,128]{1,0:T(8,128)(2,1)S(1)} %pad_maximum_fusion.4), channel_id=1, source_target_pairs={{0,1},{1,2},{2,3},{3,4},{4,5},{5,6},{6,7},{7,8},{8,9},{9,10},{10,1... | collective-permute-start | bytes 86024 | tf_op jit(solution)/shard_map/ppermute | solution.py:505
  30.6 1.9 collective-permute-start.17
  32.6 1.5 copy.24.ada
  34.2 2.5 %copy.25.weights = bf16[4,768,192]{2,1,0:T(8,128)(2,1)} copy(bf16[4,768,192]{1,2,0:T(8,128)(2,1)} %param.24) | data formatting | bytes 2359296 | tf_op args[5]
  36.7 0.7 copy.26.mask
  37.4 1.3 dynamic-slice.1.offset
  38.8 1.3 constant_dynamic-slice_fusion.offset
  40.1 0.7 pad_maximum_fusion.3.maps
  40.8 3.2 %adaptive.1 = (bf16[128,768]{1,0:T(8,128)(2,1)S(1)}, bf16[1184,128]{1,0:T(8,128)(2,1)}) custom-call(bf16[128,960]{1,0:T(8,128)(2,1)S(1)} %get-tuple-element.44.m0, bf16[128,960]{1,0:T(8,128)(2,1)S(1)} %collective-permute-done.m1, bf16[128,960]{1,0:T(8,128)(2,1)S(1)} %collective-permute-done.1.m2, bf16[128,960]{1,0:T(8,128)(2,1)S(1)} %collective-permute-done.2.m3, ...), custom_call_target="tpu_custom_call" | custom-call | flops 603979776 | bytes 3145728 | tf_op jit(solution)/shard_map/adaptive/pallas_call | solution.py:102
  44.0 0.3 collective-permute-start.3
  44.4 0.6 collective-permute-start.4
  44.9 1.8 collective-permute-start.5
  46.8 7.4 %collective-permute-done.3.a1 = bf16[128,768]{1,0:T(8,128)(2,1)S(1)} collective-permute-done((bf16[128,768]{1,0:T(8,128)(2,1)S(1)}, bf16[128,768]{1,0:T(8,128)(2,1)S(1)}, u32[]{:S(2)}, u32[]{:S(2)}) %collective-permute-start.3) | collective-permute-done | bytes 196640 | tf_op jit(solution)/shard_map/ppermute | solution.py:39
  54.2 0.9 collective-permute-done.5.a3
  55.0 3.5 %project.1 = (bf16[128,768]{1,0:T(8,128)(2,1)S(1)}, bf16[256,768]{1,0:T(8,128)(2,1)S(1)}, bf16[128,768]{1,0:T(8,128)(2,1)}) custom-call(s32[1]{0:T(128)} %bitcast.3.pos, bf16[128,768]{1,0:T(8,128)(2,1)S(1)} %get-tuple-element.48.a0, bf16[128,768]{1,0:T(8,128)(2,1)S(1)} %collective-permute-done.3.a1, bf16[128,768]{1,0:T(8,128)(2,1)S(1)} %collective-permute-done.4.a2, ...), custom_call_target="tpu_custom_call" | custom-call | flops 603979776 | bytes 4194304 | tf_op jit(solution)/shard_map/project/pallas_call | solution.py:102
  58.6 4.1 %collective-permute-start.7 = (bf16[256,768]{1,0:T(8,128)(2,1)S(1)}, bf16[256,768]{1,0:T(8,128)(2,1)S(1)}, u32[]{:S(2)}, u32[]{:S(2)}) collective-permute-start(bf16[256,768]{1,0:T(8,128)(2,1)S(1)} %get-tuple-element.50.refs_1_), channel_id=1, source_target_pairs={{0,2},{1,3},{2,4},{3,5},{4,6},{5,7},{6,0},{7,1},{8,10},{9,11},{10,... | collective-permute-start | bytes 1179656 | tf_op jit(solution)/shard_map/ppermute | solution.py:53
  62.7 1.6 collective-permute-start.8
  64.3 2.1 %collective-permute-start.9 = (bf16[256,768]{1,0:T(8,128)(2,1)S(1)}, bf16[256,768]{1,0:T(8,128)(2,1)S(1)}, u32[]{:S(2)}, u32[]{:S(2)}) collective-permute-start(bf16[256,768]{1,0:T(8,128)(2,1)S(1)} %get-tuple-element.50.refs_1_), channel_id=1, source_target_pairs={{0,6},{1,7},{2,0},{3,1},{4,2},{5,3},{6,4},{7,5},{8,14},{9,15},{10,... | collective-permute-start | bytes 1179656 | tf_op jit(solution)/shard_map/ppermute | solution.py:53
  66.6 0.7 pad_maximum_fusion.1.cond
  67.3 6.2 %collective-permute-done.7.refs_2_ = bf16[256,768]{1,0:T(8,128)(2,1)S(1)} collective-permute-done((bf16[256,768]{1,0:T(8,128)(2,1)S(1)}, bf16[256,768]{1,0:T(8,128)(2,1)S(1)}, u32[]{:S(2)}, u32[]{:S(2)}) %collective-permute-start.7) | collective-permute-done | bytes 393248 | tf_op jit(solution)/shard_map/ppermute | solution.py:53
  73.6 0.8 collective-permute-start.10
  74.4 16.2 %collective-permute-done.8.refs_3_ = bf16[256,768]{1,0:T(8,128)(2,1)S(1)} collective-permute-done((bf16[256,768]{1,0:T(8,128)(2,1)S(1)}, bf16[256,768]{1,0:T(8,128)(2,1)S(1)}, u32[]{:S(2)}, u32[]{:S(2)}) %collective-permute-start.8) | collective-permute-done | bytes 393248 | tf_op jit(solution)/shard_map/ppermute | solution.py:53
  90.6 0.4 collective-permute-start.11
  91.1 0.1 slice_reduce_fusion
  91.2 13.2 %all-gather = bf16[512,768]{1,0:T(8,128)(2,1)} all-gather(bf16[128,768]{1,0:T(8,128)(2,1)S(1)} %get-tuple-element.51), channel_id=2, replica_groups={{0,8,16,24},{1,9,17,25},{2,10,18,26},{3,11,19,27},{4,12,20,28},{5,13,21..., dimensions={0}, use_global_device_ids=true | all-gather | bytes 983040 | tf_op jit(solution)/shard_map/all_gather | solution.py:67
  104.4 0.8 copy-done.17
  105.3 19.7 %attention.1 = (bf16[128,896]{1,0:T(8,128)(2,1)}, bf16[128,896]{1,0:T(8,128)(2,1)}, bf16[128,896]{1,0:T(8,128)(2,1)}, bf16[128,896]{1,0:T(8,128)(2,1)}) custom-call(s32[3]{0:T(128)S(1)} %pad_add_fusion.pos, bf16[4,128,768]{2,1,0:T(8,128)(2,1)} %bitcast.34, bf16[256,768]{1,0:T(8,128)(2,1)} %copy-done.2, bf16[256,768]{1,0:T(8,128)(2,1)} %copy-done.13, ...), custom_call_target="tpu_custom_call" | custom-call | flops 8589934592 | bytes 6291456 | tf_op jit(solution)/shard_map/attention/pallas_call | solution.py:296
  125.0 1.7 collective-permute-start.13
  126.7 0.6 collective-permute-start.14
  127.5 3.2 %atom_first.1 = (bf16[7,128,128]{2,1,0:T(8,128)(2,1)}, bf16[768,128]{1,0:T(8,128)(2,1)}, f32[1120,128]{1,0:T(8,128)}, f32[1120,128]{1,0:T(8,128)}, bf16[1120,128]{1,0:T(8,128)(2,1)}) custom-call(s32[10]{0:T(128)S(1)} %multiply_minimum_fusion.starts, bf16[4,1184,128]{2,1,0:T(8,128)(2,1)} %bitcast.30, bf16[1120,128]{1,0:T(8,128)(2,1)} %pad_maximum_fusion.1.cond, ...), custom_call_target="tpu_custom_call" | custom-call | flops 73400320 | bytes 3145728 | tf_op jit(solution)/shard_map/atom_first/pallas_call | solution.py:102
  130.7 4.9 %hidden.1.refs_5_ = f32[512,768]{1,0:T(8,128)} custom-call(s32[1]{0:T(128)} %bitcast.3.pos, bf16[4,1184,128]{2,1,0:T(8,128)(2,1)} %bitcast.31, bf16[2,768,384]{2,1,0:T(8,128)(2,1)} %w_in.1, bf16[384,768]{1,0:T(8,128)(2,1)} %w_out.1), custom_call_target="tpu_custom_call" | custom-call | flops 905969664 | bytes 6291456 | tf_op jit(solution)/shard_map/hidden/pallas_call | solution.py:102
  135.6 0.8 collective-permute-done.15.refs_3_
  136.4 3.4 %combine.1 = (f32[128,768]{1,0:T(8,128)}, bf16[128,768]{1,0:T(8,128)(2,1)S(1)}, bf16[128,768]{1,0:T(8,128)(2,1)S(1)}, bf16[128,768]{1,0:T(8,128)(2,1)S(1)}, f32[...) custom-call(bf16[128,896]{1,0:T(8,128)(2,1)S(1)} %copy-done, ...), custom_call_target="tpu_custom_call" | custom-call | flops 452984832 | bytes 5242880 | tf_op jit(solution)/shard_map/combine/pallas_call | solution.py:102
  139.8 0.8 collective-permute-start.20
  140.5 2.8 %collective-permute-start.19 = (bf16[128,128]{1,0:T(8,128)(2,1)S(1)}, bf16[128,128]{1,0:T(8,128)(2,1)S(1)}, u32[]{:S(2)}, u32[]{:S(2)}) collective-permute-start(bf16[128,128]{1,0:T(8,128)(2,1)S(1)} %get-tuple-element.65), channel_id=1, source_target_pairs={{0,64},{32,96},{64,0},{96,32},{1,65},{33,97},{65,1},{97,33},{2,66}... | collective-permute-start | bytes 98312 | tf_op jit(solution)/shard_map/ppermute | solution.py:39
  143.3 0.4 collective-permute-done.20
  143.7 1.3 collective-permute-done.19
  145.0 1.1 collective-permute-done.18
  146.1 1.3 collective-permute-start.21
  147.4 1.8 collective-permute-start.22
  149.2 1.0 collective-permute-start.23
  150.2 0.2 collective-permute-done.21
  150.5 1.2 collective-permute-done.22
  151.7 0.5 collective-permute-done.23
  152.3 11.6 %collective-permute-start.24 = (bf16[512,128]{1,0:T(8,128)(2,1)S(1)}, bf16[512,128]{1,0:T(8,128)(2,1)S(1)}, u32[]{:S(2)}, u32[]{:S(2)}) collective-permute-start(bf16[512,128]{1,0:T(8,128)(2,1)S(1)} %pad_maximum_fusion.2), channel_id=1, source_target_pairs={{0,2},{1,3},{2,4},{3,5},{4,6},{5,7},{6,0},{7,1},{8,10},{9,11},{10,... | collective-permute-start | bytes 393224 | tf_op jit(solution)/shard_map/ppermute | solution.py:53
  163.8 2.2 %collective-permute-start.26 = (bf16[512,128]{1,0:T(8,128)(2,1)S(1)}, bf16[512,128]{1,0:T(8,128)(2,1)S(1)}, u32[]{:S(2)}, u32[]{:S(2)}) collective-permute-start(bf16[512,128]{1,0:T(8,128)(2,1)S(1)} %pad_maximum_fusion.2), channel_id=1, source_target_pairs={{0,6},{1,7},{2,0},{3,1},{4,2},{5,3},{6,4},{7,5},{8,14},{9,15},{10,... | collective-permute-start | bytes 393224 | tf_op jit(solution)/shard_map/ppermute | solution.py:53
  166.0 0.9 collective-permute-start.27
  167.0 0.3 collective-permute-start.28
  167.3 0.9 collective-permute-start.29
  168.2 1.5 collective-permute-done.25
  169.8 0.8 collective-permute-done.27
  170.5 2.6 %collective-permute-done.28 = bf16[128,768]{1,0:T(8,128)(2,1)S(1)} collective-permute-done((bf16[128,768]{1,0:T(8,128)(2,1)S(1)}, bf16[128,768]{1,0:T(8,128)(2,1)S(1)}, u32[]{:S(2)}, u32[]{:S(2)}) %collective-permute-start.28) | collective-permute-done | bytes 196640 | tf_op jit(solution)/shard_map/ppermute | solution.py:39
  173.1 2.1 %collective-permute-done.29 = bf16[128,768]{1,0:T(8,128)(2,1)S(1)} collective-permute-done((bf16[128,768]{1,0:T(8,128)(2,1)S(1)}, bf16[128,768]{1,0:T(8,128)(2,1)S(1)}, u32[]{:S(2)}, u32[]{:S(2)}) %collective-permute-start.29) | collective-permute-done | bytes 196640 | tf_op jit(solution)/shard_map/ppermute | solution.py:39
  175.3 6.7 %collective-permute-start.30 = (bf16[2048,128]{1,0:T(8,128)(2,1)S(1)}, bf16[2048,128]{1,0:T(8,128)(2,1)S(1)}, u32[]{:S(2)}, u32[]{:S(2)}) collective-permute-start(bf16[2048,128]{1,0:T(8,128)(2,1)S(1)} %constant_dynamic-update-slice_fusion.near), channel_id=1, source_target_pairs={{0,1},{1,0},{2,3},{3,2},{4,5},{5,4},{6,7},{7,6},{8,9},{9,8},{10,11... | collective-permute-start | bytes 1572872 | tf_op jit(solution)/shard_map/ppermute | solution.py:71
  182.1 1.8 add_convert_fusion
  183.8 12.3 %atoms.1 = f32[3,1,1024]{2,1,0:T(1,128)} custom-call(s32[4]{0:T(128)S(1)} %pad_add_fusion.1.pos, s32[10]{0:T(128)S(1)} %multiply_minimum_fusion.starts, s32[2,32]{1,0:T(2,128)S(1)} %bitcast.29, bf16[2048,128]{1,0:T(8,128)(2,1)S(1)} %constant_dynamic-update-slice_fusion.near, bf16[2048,128]{1,0:T(8,128)(2,1)S(1)} %collective-permute-done.30.far, ...), custom_call_target="tpu_custom_call" | custom-call | flops 367001600 | bytes 6291456 | tf_op jit(solution)/shard_map/atoms/pallas_call | solution.py:102
  (85 shorter events, 1.0 us)
Async XLA Ops:
  12.2 12.5 %copy-start.10 = (s32[1024]{0:T(1024)S(1)}, s32[1024]{0:T(1024)}, u32[]{:S(2)}) copy-start(s32[1024]{0:T(1024)} %param.33) | copy-start | bytes 12292
  12.2 12.6 %copy-start.4 = (bf16[1024,128]{1,0:T(8,128)(2,1)S(1)}, bf16[1024,128]{1,0:T(8,128)(2,1)}, u32[]{:S(2)}) copy-start(bf16[1024,128]{1,0:T(8,128)(2,1)} %param.30) | copy-start | bytes 786436
  12.2 20.4 %copy-start.3 = (bf16[4,768,192]{1,2,0:T(8,128)(2,1)S(1)}, bf16[4,768,192]{1,2,0:T(8,128)(2,1)}, u32[]{:S(2)}) copy-start(bf16[4,768,192]{1,2,0:T(8,128)(2,1)} %param.23) | copy-start | bytes 3538948
  12.2 93.0 %all-to-all-start = ((bf16[4,4,128,1024]{3,2,1,0:T(8,128)(2,1)}), bf16[4,4,128,1024]{3,2,1,0:T(8,128)(2,1)}, u32[]{:S(2)}, u32[]{:S(2)}) async-start(bf16[4,4,128,1024]{3,2,1,0:T(8,128)(2,1)} %pad_maximum_fusion), calls=%async_computation | async-start | bytes 8388608 | tf_op jit(solution)/shard_map/all_to_all | solution.py:59
  17.4 19.3 %copy-start.11 = (s32[128]{0:T(128)S(1)}, s32[128]{0:T(128)}, u32[]{:S(2)}) copy-start(s32[128]{0:T(128)} %param.22) | copy-start | bytes 1540
  17.4 22.7 %copy-start.8 = (bf16[7,128,32]{1,2,0:T(8,128)(2,1)S(1)}, bf16[7,128,32]{1,2,0:T(8,128)(2,1)}, u32[]{:S(2)}) copy-start(bf16[7,128,32]{1,2,0:T(8,128)(2,1)} %param.34) | copy-start | bytes 172036
  17.4 22.7 %copy-start.9 = (bf16[192,128]{1,0:T(8,128)(2,1)S(1)}, bf16[192,128]{1,0:T(8,128)(2,1)}, u32[]{:S(2)}) copy-start(bf16[192,128]{1,0:T(8,128)(2,1)} %param.35) | copy-start | bytes 147460
  17.4 110.1 %all-gather.4.cloned.1.call-start = ((), (), s32[]{:S(2)}) async-start(), calls=%async_computation.1 | async-start | bytes 1515520 | tf_op jit(solution)/shard_map/all_gather | solution.py:549
  19.1 21.7 %collective-permute-start = (bf16[128,960]{1,0:T(8,128)(2,1)S(1)}, bf16[128,960]{1,0:T(8,128)(2,1)S(1)}, u32[]{:S(2)}, u32[]{:S(2)}) collective-permute-start(bf16[128,960]{1,0:T(8,128)(2,1)S(1)} %get-tuple-element.45), channel_id=1, source_target_pairs={{0,32},{32,64},{64,96},{96,0},{1,33},{33,65},{65,97},{97,1},{2,34}... | collective-permute-start | bytes 737288 | tf_op jit(solution)/shard_map/ppermute | solution.py:39
  21.2 19.6 %collective-permute-start.1 = (bf16[128,960]{1,0:T(8,128)(2,1)S(1)}, bf16[128,960]{1,0:T(8,128)(2,1)S(1)}, u32[]{:S(2)}, u32[]{:S(2)}) collective-permute-start(bf16[128,960]{1,0:T(8,128)(2,1)S(1)} %get-tuple-element.46), channel_id=1, source_target_pairs={{0,64},{32,96},{64,0},{96,32},{1,65},{33,97},{65,1},{97,33},{2,66}... | collective-permute-start | bytes 737288 | tf_op jit(solution)/shard_map/ppermute | solution.py:39
  23.6 17.2 %collective-permute-start.2 = (bf16[128,960]{1,0:T(8,128)(2,1)S(1)}, bf16[128,960]{1,0:T(8,128)(2,1)S(1)}, u32[]{:S(2)}, u32[]{:S(2)}) collective-permute-start(bf16[128,960]{1,0:T(8,128)(2,1)S(1)} %get-tuple-element.47), channel_id=1, source_target_pairs={{0,96},{32,0},{64,32},{96,64},{1,97},{33,1},{65,33},{97,65},{2,98}... | collective-permute-start | bytes 737288 | tf_op jit(solution)/shard_map/ppermute | solution.py:39
  25.6 21.1 %collective-permute-start.16 = (bf16[112,128]{1,0:T(8,128)(2,1)S(1)}, bf16[112,128]{1,0:T(8,128)(2,1)S(1)}, u32[]{:S(2)}, u32[]{:S(2)}) collective-permute-start(bf16[112,128]{1,0:T(8,128)(2,1)S(1)} %pad_maximum_fusion.4), channel_id=1, source_target_pairs={{0,1},{1,2},{2,3},{3,4},{4,5},{5,6},{6,7},{7,8},{8,9},{9,10},{10,1... | collective-permute-start | bytes 86024 | tf_op jit(solution)/shard_map/ppermute | solution.py:505
  30.6 28.0 %collective-permute-start.17 = (bf16[112,128]{1,0:T(8,128)(2,1)S(1)}, bf16[112,128]{1,0:T(8,128)(2,1)S(1)}, u32[]{:S(2)}, u32[]{:S(2)}) collective-permute-start(bf16[112,128]{1,0:T(8,128)(2,1)S(1)} %pad_maximum_fusion.5), channel_id=1, source_target_pairs={{1,0},{2,1},{3,2},{4,3},{5,4},{6,5},{7,6},{8,7},{9,8},{10,9},{11,1... | collective-permute-start | bytes 86024 | tf_op jit(solution)/shard_map/ppermute | solution.py:506
  44.0 10.1 %collective-permute-start.3 = (bf16[128,768]{1,0:T(8,128)(2,1)S(1)}, bf16[128,768]{1,0:T(8,128)(2,1)S(1)}, u32[]{:S(2)}, u32[]{:S(2)}) collective-permute-start(bf16[128,768]{1,0:T(8,128)(2,1)S(1)} %get-tuple-element.48.a0), channel_id=1, source_target_pairs={{0,32},{32,64},{64,96},{96,0},{1,33},{33,65},{65,97},{97,1},{2,34}... | collective-permute-start | bytes 589832 | tf_op jit(solution)/shard_map/ppermute | solution.py:39
  44.4 9.8 %collective-permute-start.4 = (bf16[128,768]{1,0:T(8,128)(2,1)S(1)}, bf16[128,768]{1,0:T(8,128)(2,1)S(1)}, u32[]{:S(2)}, u32[]{:S(2)}) collective-permute-start(bf16[128,768]{1,0:T(8,128)(2,1)S(1)} %get-tuple-element.48.a0), channel_id=1, source_target_pairs={{0,64},{32,96},{64,0},{96,32},{1,65},{33,97},{65,1},{97,33},{2,66}... | collective-permute-start | bytes 589832 | tf_op jit(solution)/shard_map/ppermute | solution.py:39
  44.9 10.1 %collective-permute-start.5 = (bf16[128,768]{1,0:T(8,128)(2,1)S(1)}, bf16[128,768]{1,0:T(8,128)(2,1)S(1)}, u32[]{:S(2)}, u32[]{:S(2)}) collective-permute-start(bf16[128,768]{1,0:T(8,128)(2,1)S(1)} %get-tuple-element.48.a0), channel_id=1, source_target_pairs={{0,96},{32,0},{64,32},{96,64},{1,97},{33,1},{65,33},{97,65},{2,98}... | collective-permute-start | bytes 589832 | tf_op jit(solution)/shard_map/ppermute | solution.py:39
  46.8 78.2 %copy-start.6 = (bf16[112,128]{1,0:T(8,128)(2,1)}, bf16[112,128]{1,0:T(8,128)(2,1)S(1)}, u32[]{:S(2)}) copy-start(bf16[112,128]{1,0:T(8,128)(2,1)S(1)} %collective-permute-done.16.before) | copy-start | bytes 86020
  58.6 46.7 %copy-start.2 = (bf16[256,768]{1,0:T(8,128)(2,1)}, bf16[256,768]{1,0:T(8,128)(2,1)S(1)}, u32[]{:S(2)}) copy-start(bf16[256,768]{1,0:T(8,128)(2,1)S(1)} %get-tuple-element.50.refs_1_) | copy-start | bytes 1179652
  58.6 7.8 %collective-permute-start.6 = (bf16[256,768]{1,0:T(8,128)(2,1)S(1)}, bf16[256,768]{1,0:T(8,128)(2,1)S(1)}, u32[]{:S(2)}, u32[]{:S(2)}) collective-permute-start(bf16[256,768]{1,0:T(8,128)(2,1)S(1)} %get-tuple-element.50.refs_1_), channel_id=1, source_target_pairs={{0,1},{1,0},{2,3},{3,2},{4,5},{5,4},{6,7},{7,6},{8,9},{9,8},{10,11... | collective-permute-start | bytes 1179656 | tf_op jit(solution)/shard_map/ppermute | solution.py:71
  58.6 66.4 %copy-start.7 = (bf16[112,128]{1,0:T(8,128)(2,1)}, bf16[112,128]{1,0:T(8,128)(2,1)S(1)}, u32[]{:S(2)}) copy-start(bf16[112,128]{1,0:T(8,128)(2,1)S(1)} %collective-permute-done.17.after) | copy-start | bytes 86020
  58.6 14.9 %collective-permute-start.7 = (bf16[256,768]{1,0:T(8,128)(2,1)S(1)}, bf16[256,768]{1,0:T(8,128)(2,1)S(1)}, u32[]{:S(2)}, u32[]{:S(2)}) collective-permute-start(bf16[256,768]{1,0:T(8,128)(2,1)S(1)} %get-tuple-element.50.refs_1_), channel_id=1, source_target_pairs={{0,2},{1,3},{2,4},{3,5},{4,6},{5,7},{6,0},{7,1},{8,10},{9,11},{10,... | collective-permute-start | bytes 1179656 | tf_op jit(solution)/shard_map/ppermute | solution.py:53
  62.7 27.9 %collective-permute-start.8 = (bf16[256,768]{1,0:T(8,128)(2,1)S(1)}, bf16[256,768]{1,0:T(8,128)(2,1)S(1)}, u32[]{:S(2)}, u32[]{:S(2)}) collective-permute-start(bf16[256,768]{1,0:T(8,128)(2,1)S(1)} %get-tuple-element.50.refs_1_), channel_id=1, source_target_pairs={{0,4},{1,5},{2,6},{3,7},{4,0},{5,1},{6,2},{7,3},{8,12},{9,13},{10,... | collective-permute-start | bytes 1179656 | tf_op jit(solution)/shard_map/ppermute | solution.py:53
  64.3 26.8 %collective-permute-start.9 = (bf16[256,768]{1,0:T(8,128)(2,1)S(1)}, bf16[256,768]{1,0:T(8,128)(2,1)S(1)}, u32[]{:S(2)}, u32[]{:S(2)}) collective-permute-start(bf16[256,768]{1,0:T(8,128)(2,1)S(1)} %get-tuple-element.50.refs_1_), channel_id=1, source_target_pairs={{0,6},{1,7},{2,0},{3,1},{4,2},{5,3},{6,4},{7,5},{8,14},{9,15},{10,... | collective-permute-start | bytes 1179656 | tf_op jit(solution)/shard_map/ppermute | solution.py:53
  66.4 38.9 %copy-start.12 = (bf16[256,768]{1,0:T(8,128)(2,1)}, bf16[256,768]{1,0:T(8,128)(2,1)S(1)}, u32[]{:S(2)}) copy-start(bf16[256,768]{1,0:T(8,128)(2,1)S(1)} %collective-permute-done.6.refs_5_) | copy-start | bytes 1179652
  66.6 58.4 %copy-start.5 = (s32[10,112]{1,0:T(8,128)}, s32[10,112]{1,0:T(8,128)S(1)}, u32[]{:S(2)}) copy-start(s32[10,112]{1,0:T(8,128)S(1)} %reshape.25.tokens) | copy-start | bytes 13444
  73.6 31.7 %copy-start.13 = (bf16[256,768]{1,0:T(8,128)(2,1)}, bf16[256,768]{1,0:T(8,128)(2,1)S(1)}, u32[]{:S(2)}) copy-start(bf16[256,768]{1,0:T(8,128)(2,1)S(1)} %collective-permute-done.7.refs_2_) | copy-start | bytes 1179652
  73.6 30.9 %collective-permute-start.10 = (bf16[256,768]{1,0:T(8,128)(2,1)S(1)}, bf16[256,768]{1,0:T(8,128)(2,1)S(1)}, u32[]{:S(2)}, u32[]{:S(2)}) collective-permute-start(bf16[256,768]{1,0:T(8,128)(2,1)S(1)} %collective-permute-done.7.refs_2_), channel_id=1, source_target_pairs={{0,1},{1,0},{2,3},{3,2},{4,5},{5,4},{6,7},{7,6},{8,9},{9,8},{10,11... | collective-permute-start | bytes 1179656 | tf_op jit(solution)/shard_map/ppermute | solution.py:71
  90.6 14.7 %copy-start.14 = (bf16[256,768]{1,0:T(8,128)(2,1)}, bf16[256,768]{1,0:T(8,128)(2,1)S(1)}, u32[]{:S(2)}) copy-start(bf16[256,768]{1,0:T(8,128)(2,1)S(1)} %collective-permute-done.8.refs_3_) | copy-start | bytes 1179652
  90.6 13.8 %collective-permute-start.11 = (bf16[256,768]{1,0:T(8,128)(2,1)S(1)}, bf16[256,768]{1,0:T(8,128)(2,1)S(1)}, u32[]{:S(2)}, u32[]{:S(2)}) collective-permute-start(bf16[256,768]{1,0:T(8,128)(2,1)S(1)} %collective-permute-done.8.refs_3_), channel_id=1, source_target_pairs={{0,1},{1,0},{2,3},{3,2},{4,5},{5,4},{6,7},{7,6},{8,9},{9,8},{10,11... | collective-permute-start | bytes 1179656 | tf_op jit(solution)/shard_map/ppermute | solution.py:71
  91.0 14.2 %copy-start.15 = (bf16[256,768]{1,0:T(8,128)(2,1)}, bf16[256,768]{1,0:T(8,128)(2,1)S(1)}, u32[]{:S(2)}) copy-start(bf16[256,768]{1,0:T(8,128)(2,1)S(1)} %collective-permute-done.9.refs_4_) | copy-start | bytes 1179652
  91.0 14.2 %collective-permute-start.12 = (bf16[256,768]{1,0:T(8,128)(2,1)S(1)}, bf16[256,768]{1,0:T(8,128)(2,1)}, u32[]{:S(2)}, u32[]{:S(2)}) collective-permute-start(bf16[256,768]{1,0:T(8,128)(2,1)S(1)} %collective-permute-done.9.refs_4_), channel_id=1, source_target_pairs={{0,1},{1,0},{2,3},{3,2},{4,5},{5,4},{6,7},{7,6},{8,9},{9,8},{10,11... | collective-permute-start | bytes 1179656 | tf_op jit(solution)/shard_map/ppermute | solution.py:71
  104.4 0.9 copy-start.16
  104.4 0.8 copy-start.17
  125.0 11.4 %copy-start = (bf16[128,896]{1,0:T(8,128)(2,1)S(1)}, bf16[128,896]{1,0:T(8,128)(2,1)}, u32[]{:S(2)}) copy-start(bf16[128,896]{1,0:T(8,128)(2,1)} %get-tuple-element.52.refs_0_) | copy-start | bytes 688132
  125.0 10.6 %collective-permute-start.13 = (bf16[128,896]{1,0:T(8,128)(2,1)}, bf16[128,896]{1,0:T(8,128)(2,1)S(1)}, u32[]{:S(2)}, u32[]{:S(2)}) collective-permute-start(bf16[128,896]{1,0:T(8,128)(2,1)} %get-tuple-element.53), channel_id=1, source_target_pairs={{0,24},{1,25},{2,26},{3,27},{4,28},{5,29},{6,30},{7,31},{8,0},{9,1... | collective-permute-start | bytes 688136 | tf_op jit(solution)/shard_map/ppermute | solution.py:45
  126.7 8.9 %collective-permute-start.14 = (bf16[128,896]{1,0:T(8,128)(2,1)}, bf16[128,896]{1,0:T(8,128)(2,1)S(1)}, u32[]{:S(2)}, u32[]{:S(2)}) collective-permute-start(bf16[128,896]{1,0:T(8,128)(2,1)} %get-tuple-element.54), channel_id=1, source_target_pairs={{0,16},{1,17},{2,18},{3,19},{4,20},{5,21},{6,22},{7,23},{8,24},{9,... | collective-permute-start | bytes 688136 | tf_op jit(solution)/shard_map/ppermute | solution.py:45
  127.3 9.0 %collective-permute-start.15 = (bf16[128,896]{1,0:T(8,128)(2,1)}, bf16[128,896]{1,0:T(8,128)(2,1)S(1)}, u32[]{:S(2)}, u32[]{:S(2)}) collective-permute-start(bf16[128,896]{1,0:T(8,128)(2,1)} %get-tuple-element.55), channel_id=1, source_target_pairs={{0,8},{1,9},{2,10},{3,11},{4,12},{5,13},{6,14},{7,15},{8,16},{9,17... | collective-permute-start | bytes 688136 | tf_op jit(solution)/shard_map/ppermute | solution.py:45
  130.7 53.1 %copy-start.1 = (s32[32,2]{0,1:T(2,128)S(1)}, s32[32,2]{0,1:T(2,128)}, u32[]{:S(2)}) copy-start(s32[32,2]{0,1:T(2,128)} %param.32) | copy-start | bytes 772
  139.8 4.0 %collective-permute-start.20 = (bf16[128,128]{1,0:T(8,128)(2,1)S(1)}, bf16[128,128]{1,0:T(8,128)(2,1)S(1)}, u32[]{:S(2)}, u32[]{:S(2)}) collective-permute-start(bf16[128,128]{1,0:T(8,128)(2,1)S(1)} %get-tuple-element.66), channel_id=1, source_target_pairs={{0,32},{32,64},{64,96},{96,0},{1,33},{33,65},{65,97},{97,1},{2,34}... | collective-permute-start | bytes 98312 | tf_op jit(solution)/shard_map/ppermute | solution.py:39
  140.5 4.4 %collective-permute-start.19 = (bf16[128,128]{1,0:T(8,128)(2,1)S(1)}, bf16[128,128]{1,0:T(8,128)(2,1)S(1)}, u32[]{:S(2)}, u32[]{:S(2)}) collective-permute-start(bf16[128,128]{1,0:T(8,128)(2,1)S(1)} %get-tuple-element.65), channel_id=1, source_target_pairs={{0,64},{32,96},{64,0},{96,32},{1,65},{33,97},{65,1},{97,33},{2,66}... | collective-permute-start | bytes 98312 | tf_op jit(solution)/shard_map/ppermute | solution.py:39
  143.3 2.8 %collective-permute-start.18 = (bf16[128,128]{1,0:T(8,128)(2,1)S(1)}, bf16[128,128]{1,0:T(8,128)(2,1)S(1)}, u32[]{:S(2)}, u32[]{:S(2)}) collective-permute-start(bf16[128,128]{1,0:T(8,128)(2,1)S(1)} %get-tuple-element.64), channel_id=1, source_target_pairs={{0,96},{32,0},{64,32},{96,64},{1,97},{33,1},{65,33},{97,65},{2,98}... | collective-permute-start | bytes 98312 | tf_op jit(solution)/shard_map/ppermute | solution.py:39
  146.1 4.3 %collective-permute-start.21 = (bf16[128,128]{1,0:T(8,128)(2,1)S(1)}, bf16[128,128]{1,0:T(8,128)(2,1)S(1)}, u32[]{:S(2)}, u32[]{:S(2)}) collective-permute-start(bf16[128,128]{1,0:T(8,128)(2,1)S(1)} %get-tuple-element.87), channel_id=1, source_target_pairs={{0,8},{1,9},{2,10},{3,11},{4,12},{5,13},{6,14},{7,15},{8,16},{9,17... | collective-permute-start | bytes 98312 | tf_op jit(solution)/shard_map/ppermute | solution.py:45
  147.4 4.3 %collective-permute-start.22 = (bf16[128,128]{1,0:T(8,128)(2,1)S(1)}, bf16[128,128]{1,0:T(8,128)(2,1)S(1)}, u32[]{:S(2)}, u32[]{:S(2)}) collective-permute-start(bf16[128,128]{1,0:T(8,128)(2,1)S(1)} %get-tuple-element.87), channel_id=1, source_target_pairs={{0,16},{1,17},{2,18},{3,19},{4,20},{5,21},{6,22},{7,23},{8,24},{9,... | collective-permute-start | bytes 98312 | tf_op jit(solution)/shard_map/ppermute | solution.py:45
  149.2 3.1 %collective-permute-start.23 = (bf16[128,128]{1,0:T(8,128)(2,1)S(1)}, bf16[128,128]{1,0:T(8,128)(2,1)S(1)}, u32[]{:S(2)}, u32[]{:S(2)}) collective-permute-start(bf16[128,128]{1,0:T(8,128)(2,1)S(1)} %get-tuple-element.87), channel_id=1, source_target_pairs={{0,24},{1,25},{2,26},{3,27},{4,28},{5,29},{6,30},{7,31},{8,0},{9,1... | collective-permute-start | bytes 98312 | tf_op jit(solution)/shard_map/ppermute | solution.py:45
  152.3 15.0 %collective-permute-start.24 = (bf16[512,128]{1,0:T(8,128)(2,1)S(1)}, bf16[512,128]{1,0:T(8,128)(2,1)S(1)}, u32[]{:S(2)}, u32[]{:S(2)}) collective-permute-start(bf16[512,128]{1,0:T(8,128)(2,1)S(1)} %pad_maximum_fusion.2), channel_id=1, source_target_pairs={{0,2},{1,3},{2,4},{3,5},{4,6},{5,7},{6,0},{7,1},{8,10},{9,11},{10,... | collective-permute-start | bytes 393224 | tf_op jit(solution)/shard_map/ppermute | solution.py:53
  163.8 5.9 %collective-permute-start.25 = (bf16[512,128]{1,0:T(8,128)(2,1)S(1)}, bf16[512,128]{1,0:T(8,128)(2,1)S(1)}, u32[]{:S(2)}, u32[]{:S(2)}) collective-permute-start(bf16[512,128]{1,0:T(8,128)(2,1)S(1)} %pad_maximum_fusion.2), channel_id=1, source_target_pairs={{0,4},{1,5},{2,6},{3,7},{4,0},{5,1},{6,2},{7,3},{8,12},{9,13},{10,... | collective-permute-start | bytes 393224 | tf_op jit(solution)/shard_map/ppermute | solution.py:53
  163.8 5.9 %collective-permute-start.26 = (bf16[512,128]{1,0:T(8,128)(2,1)S(1)}, bf16[512,128]{1,0:T(8,128)(2,1)S(1)}, u32[]{:S(2)}, u32[]{:S(2)}) collective-permute-start(bf16[512,128]{1,0:T(8,128)(2,1)S(1)} %pad_maximum_fusion.2), channel_id=1, source_target_pairs={{0,6},{1,7},{2,0},{3,1},{4,2},{5,3},{6,4},{7,5},{8,14},{9,15},{10,... | collective-permute-start | bytes 393224 | tf_op jit(solution)/shard_map/ppermute | solution.py:53
  166.0 4.5 %collective-permute-start.27 = (bf16[128,768]{1,0:T(8,128)(2,1)S(1)}, bf16[128,768]{1,0:T(8,128)(2,1)S(1)}, u32[]{:S(2)}, u32[]{:S(2)}) collective-permute-start(bf16[128,768]{1,0:T(8,128)(2,1)S(1)} %get-tuple-element.70), channel_id=1, source_target_pairs={{0,96},{32,0},{64,32},{96,64},{1,97},{33,1},{65,33},{97,65},{2,98}... | collective-permute-start | bytes 589832 | tf_op jit(solution)/shard_map/ppermute | solution.py:39
  167.0 6.1 %collective-permute-start.28 = (bf16[128,768]{1,0:T(8,128)(2,1)S(1)}, bf16[128,768]{1,0:T(8,128)(2,1)S(1)}, u32[]{:S(2)}, u32[]{:S(2)}) collective-permute-start(bf16[128,768]{1,0:T(8,128)(2,1)S(1)} %get-tuple-element.71), channel_id=1, source_target_pairs={{0,64},{32,96},{64,0},{96,32},{1,65},{33,97},{65,1},{97,33},{2,66}... | collective-permute-start | bytes 589832 | tf_op jit(solution)/shard_map/ppermute | solution.py:39
  167.3 8.0 %collective-permute-start.29 = (bf16[128,768]{1,0:T(8,128)(2,1)S(1)}, bf16[128,768]{1,0:T(8,128)(2,1)S(1)}, u32[]{:S(2)}, u32[]{:S(2)}) collective-permute-start(bf16[128,768]{1,0:T(8,128)(2,1)S(1)} %get-tuple-element.72), channel_id=1, source_target_pairs={{0,32},{32,64},{64,96},{96,0},{1,33},{33,65},{65,97},{97,1},{2,34}... | collective-permute-start | bytes 589832 | tf_op jit(solution)/shard_map/ppermute | solution.py:39
  175.3 8.5 %collective-permute-start.30 = (bf16[2048,128]{1,0:T(8,128)(2,1)S(1)}, bf16[2048,128]{1,0:T(8,128)(2,1)S(1)}, u32[]{:S(2)}, u32[]{:S(2)}) collective-permute-start(bf16[2048,128]{1,0:T(8,128)(2,1)S(1)} %constant_dynamic-update-slice_fusion.near), channel_id=1, source_target_pairs={{0,1},{1,0},{2,3},{3,2},{4,5},{5,4},{6,7},{7,6},{8,9},{9,8},{10,11... | collective-permute-start | bytes 1572872 | tf_op jit(solution)/shard_map/ppermute | solution.py:71
Sparse Core Ops, SparseCore 0:
  66.5 26.2 all-gather.3
where the time goes:
time: 204 us; the launch traced here: 203 us
  starting transfers between devices  62.2 us (30%)
  Pallas kernels  51.9 us (25%)
  waiting for transfers between devices  43.3 us (21%)
  between operations  14.3 us (7%)
  blocking collectives  13.2 us (6%)
  local copies, waits for them, and re-layouts  12.3 us (6%)
  other arithmetic  5.75 us (3%)
    pallas_call x7, Pallas kernels, kernel_call(): pl.pallas_call(body, grid=(1,), out_shape=out_shape, in_specs=[pl.BlockSp...  32.2 us
    ppermute x6, waiting for transfers between devices, z_shift(): return lax.ppermute(a, 'seq', pairs)  24 us
    ppermute x6, starting transfers between devices, z_shift(): return lax.ppermute(a, 'seq', pairs)  21.5 us
    pallas_call x1, Pallas kernels, attention(): pl.pallas_call(attention_body, grid=(HEADS,), out_shape=[shape((ROWS, HAL...  19.7 us
    ppermute x12, waiting for transfers between devices, x_shift(): return lax.ppermute(a, 'fsdp', [(i, (i + k) % NX) for i in range(NX)])  16.5 us
    ppermute x12, starting transfers between devices, x_shift(): return lax.ppermute(a, 'fsdp', [(i, (i + k) % NX) for i in range(NX)])  14.1 us
    all_gather x1, blocking collectives, y_collect(): return lax.all_gather(a, 'seq', axis=0, axis_index_groups=groups)  13.2 us
    ppermute x5, starting transfers between devices, c_shift(): return lax.ppermute(a, 'seq', [(t, t ^ 1) for t in range(NY * NZ * NC)])  8.06 us
  transfers between devices with their start and end apart: 33, of which 15 were waited for; matrix products, arithmetic and copies ran while one was open for 6% of the time, Pallas kernels for 18%

commit v1 on v0

--- a/solution.py
+++ b/solution.py
@@ -1,3 +1,4 @@
+import functools
 import math
 
 import jax
@@ -23,8 +24,6 @@
 ROWS = 128
 DIM = 768
 COLS = 192
-SLOTS = 4
-HALF = SLOTS * COLS
 HEADS = 4
 ATOMS = 1024
 EXT = ATOMS + 2 * RIM
@@ -51,6 +50,10 @@
         (t, (t // group) * group + ((t // NC + k) % NZ) * NC + t % NC) for t in range(NY * group)
     ]
     return lax.ppermute(a, "seq", pairs)
+
+
+def z_swap(a, k):
+    return lax.ppermute(a, "seq", [(t, t ^ (NC * k)) for t in range(NY * NZ * NC)])
 
 
 def y_exchange(a):
@@ -122,7 +125,14 @@
     return jax.ShapeDtypeStruct(dims, kind)
 
 
-def prepare_body(pos, act, cond, *outs):
+def prepare_body(pos, act, cond, bias, *refs):
+    outs, cut, sems = refs[0:4], refs[4], refs[5]
+    copies = []
+    for i in range(NY):
+        copies.append(
+            pltpu.make_async_copy(bias.at[:, :, pl.ds(i * KEYS, KEYS)], cut.at[i], sems.at[i])
+        )
+        copies[i].start()
     f = pos[0]
     normed = norm(cond[...].astype(F32)).astype(BF16)
     hat = norm(act[...].astype(F32))
@@ -133,6 +143,8 @@
             part = jnp.where(dest == j, hat[:, j * COLS : (j + 1) * COLS], part)
         outs[k][:, 0:DIM] = normed
         outs[k][:, DIM : DIM + COLS] = part.astype(BF16)
+    for copy in copies:
+        copy.wait()
 
 
 def adaptive_body(m0, m1, m2, m3, ada, offset, maps, attend, message):
@@ -178,7 +190,7 @@
         g[:, to] = sums[3][own].astype(BF16)
 
 
-def hidden_body(pos, parts, w_in, w_out, out):
+def hidden_body(pos, w_in, w_out, parts, out):
     f = pos[0]
     gate, up = None, None
     for j in range(NX):
@@ -197,45 +209,63 @@
 
 
 KEYS = NZ * NC * ROWS
-
-
-def attention_body(pos, *refs):
-    q = refs[0]
-    pairs = refs[1:9]
-    bias = refs[9]
-    out = refs[10:14]
-    q_all, key_all, value_all, far_row, bias_all, stats, probs = refs[14:21]
-    scores = refs[21:23]
+PART = KEYS // 2
+
+
+def spread_heads(first):
+    head = (lax.broadcasted_iota(jnp.int32, (128, DIM), 0) - first) * HD
+    lane = lax.broadcasted_iota(jnp.int32, (128, DIM), 1)
+    return ((lane >= head) & (lane < head + HD)).astype(F32).astype(BF16)
+
+
+def spread_rows(share, spread):
+    high = share.astype(BF16)
+    low = (share - high.astype(F32)).astype(BF16)
+    return dot(high, spread) + dot(low, spread)
+
+
+def attention_body(merge, pos, q, *refs):
+    pairs = refs[0:4]
+    bias = refs[4]
+    refs = refs[5:]
+    if merge:
+        earlier, earlier_stats, refs = refs[0:4], refs[4:8], refs[8:]
+        out, refs = refs[0:4], refs[4:]
+    else:
+        out, out_stats, refs = refs[0:4], refs[4:8], refs[8:]
+    q_all, key_all, value_all, far_row, bias_all, stats, probs, total_all = refs[0:8]
+    scores = refs[8:10]
     h = pl.program_id(0)
+    y = pos[0]
 
     @pl.when(h == 0)
     def _():
         unit = (lax.broadcasted_iota(jnp.int32, (8, 128), 1) == 0).astype(F32).astype(BF16)
-        for side in range(2):
-            core = pos[2] if side == 0 else 1 - pos[2]
-            for n in range(NZ):
-                block = pairs[side * NZ + n][0:ROWS, :]
-                place = lax.rem(pos[1] + NZ - n, NZ) * NC + core
-                at = pl.multiple_of(place * ROWS, ROWS)
-                first = dot_nt(unit, block[:, 0:128])
-                far_row[:, pl.ds(at, ROWS)] = jnp.where(first > 1e20, FAR, 0.0)
-                wide = block.astype(F32)
-                key_all[pl.ds(at, ROWS), :] = jnp.where(wide[:, 0:1] > 1e20, 0.0, wide).astype(BF16)
-                value_all[pl.ds(at, ROWS), :] = pairs[side * NZ + n][ROWS:, :]
+        for i in range(4):
+            at = slice(i * ROWS, (i + 1) * ROWS)
+            block = pairs[i][0:ROWS, :]
+            first = dot_nt(unit, block[:, 0:128])
+            far_row[:, at] = jnp.where(first > 1e20, FAR, 0.0)
+            wide = block.astype(F32)
+            key_all[at, :] = jnp.where(wide[:, 0:1] > 1e20, 0.0, wide).astype(BF16)
+            value_all[at, :] = pairs[i][ROWS:, :]
         for n in range(NY):
-            q_all[n * ROWS : (n + 1) * ROWS, :] = q[lax.rem(pos[0] + NY - n, NY)]
+            q_all[n * ROWS : (n + 1) * ROWS, :] = q[lax.rem(y + NY - n, NY)]
         stats[...] = jnp.zeros_like(stats)
 
     for n in range(NY):
-        part = bias[lax.rem(pos[0] + NY - n, NY), 0]
-        bias_all[n] = part.astype(F32) * LOG2E + far_row[0:1, :]
+        src = lax.rem(y + NY - n, NY)
+        for i in range(4):
+            at = slice(i * ROWS, (i + 1) * ROWS)
+            part = bias[src, 0, :, pl.ds(pl.multiple_of(pos[1 + i] * ROWS, ROWS), ROWS)]
+            bias_all[n, :, at] = part.astype(F32) * LOG2E + far_row[0:1, at]
 
     lane = lax.broadcasted_iota(jnp.int32, (NY * ROWS, 256), 1)
     slot = lax.broadcasted_iota(jnp.int32, (ROWS, 128), 1)
     windows, mines, rows = [], [], []
-    for s in range(SLOTS):
+    for s in range(NX):
         lane0 = COLS * s + HD * h
-        start = jnp.minimum(lane0 // 128, (HALF - 256) // 128)
+        start = jnp.minimum(lane0 // 128, (DIM - 256) // 128)
         off = lane0 - start * 128
         window = pl.ds(pl.multiple_of(start * 128, 128), 256)
         mine = (lane >= off) & (lane < off + HD)
@@ -243,21 +273,19 @@
         mines.append(mine)
         rows.append(jnp.where(mine, q_all[:, window].astype(F32), 0.0).astype(BF16))
 
-    tile = KEYS // NY
-
     def score(s, j):
-        keys = slice(j * tile, (j + 1) * tile)
+        keys = slice(j * 256, (j + 1) * 256)
         scores[s % 2][:, keys] = dot_nt(rows[s], key_all[keys, windows[s]])
 
-    for j in range(NY):
+    for j in range(PART // 256):
         score(0, j)
-    for s in range(SLOTS):
+    for s in range(NX):
         index = s * HEADS + h
         of_max = (lax.rem(slot, 16) == index) & (slot < 48)
         of_total = (lax.rem(slot, 16) == index) & (slot >= 48) & (slot < 96)
         totals = []
         for n in range(NY):
-            if s + 1 < SLOTS:
+            if s + 1 < NX and n < PART // 256:
                 score(s + 1, n)
             own = slice(n * ROWS, (n + 1) * ROWS)
             part = scores[s % 2][own, :] + bias_all[n]
@@ -271,79 +299,100 @@
         for n in range(NY):
             own = slice(n * ROWS, (n + 1) * ROWS)
             scaled = summed[own] * (1.0 / totals[n])
-            before = out[n][:, windows[s]].astype(F32)
-            out[n][:, windows[s]] = jnp.where(mines[s][own], scaled, before).astype(BF16)
+            before = total_all[own, windows[s]]
+            total_all[own, windows[s]] = jnp.where(mines[s][own], scaled, before)
 
     @pl.when(h == HEADS - 1)
     def _():
         third = lax.rem(slot // 16, 3)
+        spread = spread_heads(48)
         for n in range(NY):
+            own = slice(n * ROWS, (n + 1) * ROWS)
             whole = stats[n]
+            if not merge:
+                out[n][...] = total_all[own, :].astype(BF16)
+                out_stats[n][...] = whole
+                continue
+            other = earlier_stats[n][...]
+            top = jnp.maximum(whole, other)
+            top_there = pltpu.roll(top, 48, 1)
+            now = whole * jnp.exp2(jnp.minimum(pltpu.roll(whole, 48, 1) - top_there, 0.0))
+            then = other * jnp.exp2(jnp.minimum(pltpu.roll(other, 48, 1) - top_there, 0.0))
+            both = now + then
+            used = (slot >= 48) & (slot < 64)
+            share_now = jnp.where(used, now / both, 0.0)
+            share_then = jnp.where(used, then / both, 0.0)
+            merged = spread_rows(share_now, spread) * total_all[own, :]
+            merged += spread_rows(share_then, spread) * earlier[n][...].astype(F32)
+            out[n][:, 0:DIM] = merged.astype(BF16)
+            whole = jnp.where(slot < 48, top, jnp.where(slot < 96, both, 0.0))
             high = whole.astype(BF16).astype(F32)
             rest = whole - high
             middle = rest.astype(BF16).astype(F32)
             low = rest - middle
             sent = jnp.where(third == 0, high, jnp.where(third == 1, middle, low))
-            out[n][:, HALF : HALF + 128] = sent.astype(BF16)
-
-
-def attention(pos, q, pairs, bias):
+            out[n][:, DIM : DIM + 128] = sent.astype(BF16)
+
+
+def attention(pos, q, pairs, bias, earlier=None):
     once = pl.Buffered(1)
-    in_specs = [pl.BlockSpec(memory_space=pltpu.SMEM)]
-    in_specs += [pl.BlockSpec((NY, ROWS, DIM), lambda h: (0, 0, 0), pipeline_mode=once)]
-    in_specs += [pl.BlockSpec((2 * ROWS, HALF), lambda h: (0, 0), pipeline_mode=once)] * 8
+
+    def whole(dims):
+        return pl.BlockSpec(dims, lambda h, n=len(dims): (0,) * n, pipeline_mode=once)
+
+    merge = earlier is not None
+    in_specs = [pl.BlockSpec(memory_space=pltpu.SMEM), whole((NY, ROWS, DIM))]
+    in_specs += [whole((2 * ROWS, DIM))] * 4
     in_specs += [pl.BlockSpec((NY, 1, ROWS, KEYS), lambda h: (0, h, 0, 0))]
+    args = [q, *pairs, bias]
+    if merge:
+        in_specs += [whole((ROWS, DIM))] * 4 + [whole((ROWS, 128))] * 4
+        args += earlier
+        outs = [sent_shape((ROWS, DIM + 128))] * 4
+    else:
+        outs = [shape((ROWS, DIM))] * 4 + [shape((ROWS, 128), F32)] * 4
     return pl.pallas_call(
-        attention_body,
+        functools.partial(attention_body, merge),
         grid=(HEADS,),
-        out_shape=[shape((ROWS, HALF + 128))] * 4,
+        out_shape=outs,
         in_specs=in_specs,
-        out_specs=[pl.BlockSpec((ROWS, HALF + 128), lambda h: (0, 0))] * 4,
+        out_specs=[whole(o.shape) for o in outs],
         scratch_shapes=[
-            pltpu.VMEM((NY * ROWS, HALF), BF16),
-            pltpu.VMEM((KEYS, HALF), BF16),
-            pltpu.VMEM((KEYS, HALF), BF16),
-            pltpu.VMEM((8, KEYS), F32),
-            pltpu.VMEM((NY, ROWS, KEYS), F32),
+            pltpu.VMEM((NY * ROWS, DIM), BF16),
+            pltpu.VMEM((PART, DIM), BF16),
+            pltpu.VMEM((PART, DIM), BF16),
+            pltpu.VMEM((8, PART), F32),
+            pltpu.VMEM((NY, ROWS, PART), F32),
             pltpu.VMEM((NY, ROWS, 128), F32),
-            pltpu.VMEM((NY * ROWS, KEYS), BF16),
-            pltpu.VMEM((NY * ROWS, KEYS), F32),
-            pltpu.VMEM((NY * ROWS, KEYS), F32),
+            pltpu.VMEM((NY * ROWS, PART), BF16),
+            pltpu.VMEM((NY * ROWS, DIM), F32),
+            pltpu.VMEM((NY * ROWS, PART), F32),
+            pltpu.VMEM((NY * ROWS, PART), F32),
         ],
         compiler_params=pltpu.CompilerParams(
-            dimension_semantics=("arbitrary",), vmem_limit_bytes=36 << 20
+            dimension_semantics=("arbitrary",), vmem_limit_bytes=32 << 20
         ),
-        cost_estimate=pl.CostEstimate(
-            flops=SLOTS * 4 * 512 * 1024 * 512 * 2,
-            bytes_accessed=6 << 20,
-            transcendentals=4 << 20,
-        ),
-        name="attention",
-    )(pos, *(pltpu.with_memory_space_constraint(a, pltpu.HBM) for a in (q, *pairs, bias)))
+        name="attention_last" if merge else "attention_first",
+    )(pos, *(pltpu.with_memory_space_constraint(a, pltpu.HBM) for a in args))
 
 
 def combined(parts):
     tops, totals = [], []
     for o in parts:
-        sent = o[:, HALF : HALF + 128].astype(F32)
+        sent = o[:, DIM : DIM + 128].astype(F32)
         whole = sent + pltpu.roll(sent, 128 - 16, 1) + pltpu.roll(sent, 128 - 32, 1)
         tops.append(whole)
         totals.append(pltpu.roll(whole, 128 - 48, 1))
-    used = lax.broadcasted_iota(jnp.int32, (ROWS, 128), 1) < SLOTS * HEADS
+    used = lax.broadcasted_iota(jnp.int32, (ROWS, 128), 1) < NX * HEADS
     tops = [jnp.where(used, t, 0.0) for t in tops]
     totals = [jnp.where(used, t, 1.0) for t in totals]
     top = jnp.maximum(jnp.maximum(tops[0], tops[1]), jnp.maximum(tops[2], tops[3]))
     shares = [n * jnp.exp2(t - top) for t, n in zip(tops, totals)]
     inverse = 1.0 / (shares[0] + shares[1] + shares[2] + shares[3])
-    head = lax.broadcasted_iota(jnp.int32, (128, HALF), 0) * HD
-    lane = lax.broadcasted_iota(jnp.int32, (128, HALF), 1)
-    spread = ((lane >= head) & (lane < head + HD)).astype(F32).astype(BF16)
+    spread = spread_heads(0)
     attended = None
     for o, share in zip(parts, shares):
-        share = share * inverse
-        high = share.astype(BF16)
-        low = (share - high.astype(F32)).astype(BF16)
-        term = (dot(high, spread) + dot(low, spread)) * o[:, 0:HALF].astype(F32)
+        term = spread_rows(share * inverse, spread) * o[:, 0:DIM].astype(F32)
         attended = term if attended is None else attended + term
     return attended
 
@@ -478,13 +527,28 @@
     f_pos = f.reshape(1)
     act = token_act[0]
 
-    sent = kernel_call(
+    block = pl.BlockSpec((ROWS, DIM), lambda i: (0, 0), pipeline_mode=pl.Buffered(1))
+    wide = pl.BlockSpec((ROWS, DIM + COLS), lambda i: (0, 0), pipeline_mode=pl.Buffered(1))
+    *sent, cut = pl.pallas_call(
         prepare_body,
-        "prepare",
-        [sent_shape((ROWS, DIM + COLS))] * 4,
-        (act, token_cond[0]),
-        (f_pos,),
-        size=2 << 20,
+        grid=(1,),
+        out_shape=[sent_shape((ROWS, DIM + COLS))] * 4 + [shape((NY, HEADS, ROWS, KEYS))],
+        in_specs=[
+            pl.BlockSpec(memory_space=pltpu.SMEM),
+            block,
+            block,
+            pl.BlockSpec(memory_space=pltpu.HBM),
+        ],
+        out_specs=[wide] * 4 + [pl.BlockSpec(memory_space=pltpu.HBM)],
+        scratch_shapes=[pltpu.SemaphoreType.DMA((NY,))],
+        compiler_params=pltpu.CompilerParams(dimension_semantics=("arbitrary",)),
+        cost_estimate=pl.CostEstimate(flops=1 << 20, bytes_accessed=10 << 20, transcendentals=0),
+        name="prepare",
+    )(
+        f_pos,
+        pltpu.with_memory_space_constraint(act, pltpu.HBM),
+        pltpu.with_memory_space_constraint(token_cond[0], pltpu.HBM),
+        pair_bias,
     )
     normed = [sent[0]] + [x_shift(sent[k], k) for k in (1, 2, 3)]
     edge_skip, edge_cond, edge_token, _ = lax.optimization_barrier(
@@ -505,8 +569,6 @@
     before = lax.ppermute(edge(ATOMS - RIM, ATOMS), "seq", up)
     after = lax.ppermute(edge(0, RIM), "seq", [(j, i) for i, j in up])
 
-    span = pair_bias.shape[2] // NY
-    cut = jnp.stack([pair_bias[:, :, i * span : (i + 1) * span] for i in range(NY)])
     bias = y_exchange(cut)
 
     def decoded(side):
@@ -525,7 +587,7 @@
         "adaptive",
         [sent_shape((ROWS, DIM)), shape((DIM + COLS + 7 * 32, CA))],
         (*normed, ada_weights, offsets[0:2], own_maps),
-        free=4,
+        free=7,
         flops=4 * 2 * 512 * 768 * 192,
         size=3 << 20,
     )
@@ -534,16 +596,18 @@
         project_body,
         "project",
         [sent_shape((ROWS, DIM)), sent_shape((2 * ROWS, DIM)), shape((ROWS, DIM))],
-        free=4,
+        free=7,
         args=(*attend_all, attention_in, offsets[2:3], token_mask.reshape(ROWS, 1)),
         scalars=(f_pos,),
         flops=4 * 2 * 512 * 768 * 192,
         size=4 << 20,
     )
-    near = [kv] + [z_shift(kv, k) for k in (1, 2, 3)]
-    pairs = near + [c_shift(a) for a in near]
-    q, _ = lax.optimization_barrier((q, pairs[NZ]))
+    near = [kv] + [z_swap(kv, k) for k in (1, 2, 3)]
+    across = c_shift(kv)
+    q, _ = lax.optimization_barrier((q, across))
     q_all = y_collect(q)
+    q_all, near_1 = lax.optimization_barrier((q_all, near[1]))
+    early = [kv, near_1, across, c_shift(near_1)]
 
     message, _ = lax.optimization_barrier((message, q))
     messages = lax.all_gather(message, "fsdp", axis=0)
@@ -551,8 +615,9 @@
         hidden_body,
         "hidden",
         shape((NX * ROWS, DIM), F32),
-        (messages, transition_in, transition_out),
+        (transition_in, transition_out, messages),
         (f_pos,),
+        free=2,
         flops=3 * 2 * 512 * 768 * 384,
         size=6 << 20,
     )
@@ -572,8 +637,14 @@
         size=3 << 20,
     )
 
-    place = jnp.stack([y, z, c])
-    out = attention(place, q_all, pairs, bias)
+    def places(n):
+        at = [(z ^ n) * NC + c, (z ^ (n + 1)) * NC + c]
+        return jnp.stack([y, *at, at[0] ^ 1, at[1] ^ 1])
+
+    first = attention(places(0), q_all, early, bias)
+    _, near_2, near_3 = lax.optimization_barrier((first[0], near[2], near[3]))
+    late = [near_2, near_3, c_shift(near_2), c_shift(near_3)]
+    out = attention(places(2), q_all, late, bias, first)
     parts = [out[0]] + [y_shift(out[k], NY - k) for k in (1, 2, 3)]
     sums = kernel_call(
         combine_body,

time: 204 us -> 311 us (1.52)
  Pallas kernels: 51.9 us -> 182 us
  waiting for transfers between devices: 43.3 us -> 36.4 us
  starting transfers between devices: 62.2 us -> 56.1 us
  local copies, waits for them, and re-layouts: 12.3 us -> 6.84 us
  other arithmetic: 5.75 us -> 2.54 us
    pallas_call x1 -> x3, Pallas kernels: 19.7 us -> 154 us  [the longest x1 130 us: per_device(): pl.pallas_call(prepare_body, grid=(1,), out_shape=[sent_shape((ROWS, DIM...]
    ppermute x6 -> x3, waiting for transfers between devices: 24 us -> 1.87 us  [z_shift(): return lax.ppermute(a, 'seq', pairs)]
    ppermute x6 -> x3, starting transfers between devices: 21.5 us -> 7.71 us  [z_shift(): return lax.ppermute(a, 'seq', pairs)]
    ppermute x6, waiting for transfers between devices: 2.79 us -> 7.65 us  [y_shift(): return lax.ppermute(a, 'seq', pairs)]
    ppermute x12, waiting for transfers between devices: 16.5 us -> 21.2 us  [x_shift(): return lax.ppermute(a, 'fsdp', [(i, (i + k) % NX) for i in range(NX)])]
    ppermute x5, starting transfers between devices: 8.06 us -> 12.7 us  [c_shift(): return lax.ppermute(a, 'seq', [(t, t ^ 1) for t in range(NY * NZ * NC)])]
    ppermute x0 -> x3, starting transfers between devices: none -> 4.37 us  [z_swap(): lax.ppermute(a, 'seq', [(t, t ^ NC * k) for t in range(NY * NZ * NC)])]
    pallas_call x7 -> x6, Pallas kernels: 32.2 us -> 28.3 us  [kernel_call(): pl.pallas_call(body, grid=(1,), out_shape=out_shape, in_specs=[pl.BlockSp...]
  transfers between devices with their start and end apart: 33 -> 33, of which waited for: 15 -> 19; matrix products, arithmetic and copies ran while one was open for 6% -> 2% of each run, Pallas kernels for 18% -> 12%
where the time goes in v1:
time: 311 us
  Pallas kernels  182 us (59%)
  starting transfers between devices  56.1 us (18%)
  waiting for transfers between devices  36.4 us (12%)
  between operations  14.4 us (5%)
  blocking collectives  12.1 us (4%)
  local copies, waits for them, and re-layouts  6.84 us (2%)
    pallas_call x1, Pallas kernels, per_device(): pl.pallas_call(prepare_body, grid=(1,), out_shape=[sent_shape((ROWS, DIM...  130 us
    pallas_call x6, Pallas kernels, kernel_call(): pl.pallas_call(body, grid=(1,), out_shape=out_shape, in_specs=[pl.BlockSp...  28.3 us
    pallas_call x2, Pallas kernels, attention(): pl.pallas_call(functools.partial(attention_body, merge), grid=(HEADS,), o...  23.6 us
    ppermute x12, waiting for transfers between devices, x_shift(): return lax.ppermute(a, 'fsdp', [(i, (i + k) % NX) for i in range(NX)])  21.2 us
    ppermute x12, starting transfers between devices, x_shift(): return lax.ppermute(a, 'fsdp', [(i, (i + k) % NX) for i in range(NX)])  15 us
    ppermute x5, starting transfers between devices, c_shift(): return lax.ppermute(a, 'seq', [(t, t ^ 1) for t in range(NY * NZ * NC)])  12.7 us
    all_gather x1, blocking collectives, y_collect(): return lax.all_gather(a, 'seq', axis=0, axis_index_groups=groups)  12.1 us
    ppermute x3, starting transfers between devices, z_shift(): return lax.ppermute(a, 'seq', pairs)  7.71 us
  transfers between devices with their start and end apart: 33, of which 19 were waited for; matrix products, arithmetic and copies ran while one was open for 2% of the time, Pallas kernels for 12%

profile of v1, /device:TPU:1, one launch (start us, length us, event | category | flops | bytes accessed | tf_op | source)
XLA Modules:
  0.0 310.5 jit_solution(1113891281518067231)
XLA Ops:
  7.2 130.2 %prepare.1 = (bf16[128,960]{1,0:T(8,128)(2,1)}, bf16[128,960]{1,0:T(8,128)(2,1)}, bf16[128,960]{1,0:T(8,128)(2,1)}, bf16[128,960]{1,0:T(8,128)(2,1)}, bf16[4,4,128,1024]{3,2,1,0:T(8,128)(2,1)}) custom-call(s32[1]{0:T(128)} %bitcast.5.pos, bf16[128,768]{1,0:T(8,128)(2,1)} %bitcast.34, bf16[128,768]{1,0:T(8,128)(2,1)} %bitcast.38, bf16[4,128,4096]{2,1,0:T(8,128)(2,1)} %bias.1), custom_call_target="tpu_custom_call" | custom-call | flops 1048576 | bytes 10485760 | tf_op jit(solution)/shard_map/prepare/pallas_call | solution.py:532
  137.4 5.2 %all-to-all-start = ((bf16[4,4,128,1024]{3,2,1,0:T(8,128)(2,1)}), bf16[4,4,128,1024]{3,2,1,0:T(8,128)(2,1)}, u32[]{:S(2)}, u32[]{:S(2)}) async-start(bf16[4,4,128,1024]{3,2,1,0:T(8,128)(2,1)} %get-tuple-element.67), calls=%async_computation | async-start | bytes 8388608 | tf_op jit(solution)/shard_map/all_to_all | solution.py:62
  142.5 2.1 collective-permute-start
  144.6 2.5 collective-permute-start.1
  147.0 1.2 collective-permute-start.2
  148.2 0.7 copy.24.ada
  148.9 1.7 copy.25.weights
  150.7 0.8 dynamic-slice.1.offset
  151.5 0.8 constant_dynamic-slice_fusion.offset
  152.3 0.8 pad_maximum_fusion.2.maps
  153.1 5.6 %collective-permute-done.1.m2 = bf16[128,960]{1,0:T(8,128)(2,1)} collective-permute-done((bf16[128,960]{1,0:T(8,128)(2,1)}, bf16[128,960]{1,0:T(8,128)(2,1)}, u32[]{:S(2)}, u32[]{:S(2)}) %collective-permute-start.1) | collective-permute-done | bytes 245792 | tf_op jit(solution)/shard_map/ppermute | solution.py:38
  158.7 3.0 adaptive.1
  161.6 1.2 collective-permute-start.3
  162.8 2.3 collective-permute-start.4
  165.1 0.7 collective-permute-start.5
  165.8 1.9 collective-permute-done.3.a1
  167.8 5.4 %collective-permute-done.4.a2 = bf16[128,768]{1,0:T(8,128)(2,1)S(1)} collective-permute-done((bf16[128,768]{1,0:T(8,128)(2,1)S(1)}, bf16[128,768]{1,0:T(8,128)(2,1)S(1)}, u32[]{:S(2)}, u32[]{:S(2)}) %collective-permute-start.4) | collective-permute-done | bytes 196640 | tf_op jit(solution)/shard_map/ppermute | solution.py:38
  173.2 2.1 project.1
  175.3 2.0 collective-permute-start.6
  177.4 0.7 fusion.15
  178.1 4.2 %collective-permute-start.16 = (bf16[112,128]{1,0:T(8,128)(2,1)S(1)}, bf16[112,128]{1,0:T(8,128)(2,1)S(1)}, u32[]{:S(2)}, u32[]{:S(2)}) collective-permute-start(bf16[112,128]{1,0:T(8,128)(2,1)S(1)} %pad_maximum_fusion.3), channel_id=1, source_target_pairs={{0,1},{1,2},{2,3},{3,4},{4,5},{5,6},{6,7},{7,8},{8,9},{9,10},{10,1... | collective-permute-start | bytes 86024 | tf_op jit(solution)/shard_map/ppermute | solution.py:569
  182.4 1.9 collective-permute-start.17
  184.6 1.7 collective-permute-start.7
  186.2 2.0 collective-permute-start.9
  188.2 0.7 collective-permute-start.10
  188.9 12.1 %all-gather = bf16[512,768]{1,0:T(8,128)(2,1)} all-gather(bf16[128,768]{1,0:T(8,128)(2,1)S(1)} %get-tuple-element.64), channel_id=2, replica_groups={{0,8,16,24},{1,9,17,25},{2,10,18,26},{3,11,19,27},{4,12,20,28},{5,13,21..., dimensions={0}, use_global_device_ids=true | all-gather | bytes 983040 | tf_op jit(solution)/shard_map/all_gather | solution.py:70
  201.0 2.8 collective-permute-done.7.refs_1_
  203.9 4.0 %collective-permute-start.8 = (bf16[256,768]{1,0:T(8,128)(2,1)S(1)}, bf16[256,768]{1,0:T(8,128)(2,1)S(1)}, u32[]{:S(2)}, u32[]{:S(2)}) collective-permute-start(bf16[256,768]{1,0:T(8,128)(2,1)S(1)} %collective-permute-done.7.refs_1_), channel_id=1, source_target_pairs={{0,1},{1,0},{2,3},{3,2},{4,5},{5,4},{6,7},{7,6},{8,9},{9,8},{10,11... | collective-permute-start | bytes 1179656 | tf_op jit(solution)/shard_map/ppermute | solution.py:74
  207.9 1.3 collective-permute-done.8.refs_3_
  209.2 0.7 copy-done.13
  210.0 11.5 %attention_first.1 = (bf16[128,768]{1,0:T(8,128)(2,1)}, bf16[128,768]{1,0:T(8,128)(2,1)}, bf16[128,768]{1,0:T(8,128)(2,1)}, bf16[128,768]{1,0:T(8,128)(2,1)}, f3...) custom-call(s32[5]{0:T(128)S(1)} %stack.69.pos, ...), custom_call_target="tpu_custom_call" | custom-call | tf_op jit(solution)/shard_map/attention_first/pallas_call | solution.py:354
  221.6 0.5 collective-permute-start.11
  222.5 0.7 pad_maximum_fusion.cond
  223.4 0.6 collective-permute-done.12.refs_3_
  223.9 0.7 copy-done.12
  224.7 12.1 %attention_last.1 = (bf16[128,896]{1,0:T(8,128)(2,1)S(1)}, bf16[128,896]{1,0:T(8,128)(2,1)S(1)}, bf16[128,896]{1,0:T(8,128)(2,1)S(1)}, bf16[128,896]{1,0:T(8,128)(2,1)S(1)}) custom-call(s32[5]{0:T(128)S(1)} %stack.64.pos, bf16[4,128,768]{2,1,0:T(8,128)(2,1)} %bitcast.31, bf16[256,768]{1,0:T(8,128)(2,1)} %copy-done.8, bf16[256,768]{1,0:T(8,128)(2,1)} %copy-done.9, ...), custom_call_target="tpu_custom_call" | custom-call | tf_op jit(solution)/shard_map/attention_last/pallas_call | solution.py:354
  236.8 1.4 collective-permute-start.13
  238.3 0.7 collective-permute-start.14
  239.0 3.3 %atom_first.1 = (bf16[7,128,128]{2,1,0:T(8,128)(2,1)}, bf16[768,128]{1,0:T(8,128)(2,1)}, f32[1120,128]{1,0:T(8,128)}, f32[1120,128]{1,0:T(8,128)}, bf16[1120,128]{1,0:T(8,128)(2,1)}) custom-call(s32[10]{0:T(128)S(1)} %multiply_minimum_fusion.starts, bf16[4,1184,128]{2,1,0:T(8,128)(2,1)} %bitcast.32, bf16[1120,128]{1,0:T(8,128)(2,1)} %pad_maximum_fusion.cond, ...), custom_call_target="tpu_custom_call" | custom-call | flops 73400320 | bytes 3145728 | tf_op jit(solution)/shard_map/atom_first/pallas_call | solution.py:105
  242.3 4.4 %hidden.1.refs_5_ = f32[512,768]{1,0:T(8,128)} custom-call(s32[1]{0:T(128)} %bitcast.5.pos, bf16[2,768,384]{2,1,0:T(8,128)(2,1)S(1)} %copy-done, bf16[384,768]{1,0:T(8,128)(2,1)S(1)} %copy-done.1, bf16[4,1184,128]{2,1,0:T(8,128)(2,1)} %bitcast.33), custom_call_target="tpu_custom_call" | custom-call | flops 905969664 | bytes 6291456 | tf_op jit(solution)/shard_map/hidden/pallas_call | solution.py:105
  246.7 5.5 %collective-permute-done.15.refs_3_ = bf16[128,896]{1,0:T(8,128)(2,1)S(1)} collective-permute-done((bf16[128,896]{1,0:T(8,128)(2,1)S(1)}, bf16[128,896]{1,0:T(8,128)(2,1)S(1)}, u32[]{:S(2)}, u32[]{:S(2)}) %collective-permute-start.15) | collective-permute-done | bytes 229408 | tf_op jit(solution)/shard_map/ppermute | solution.py:44
  252.2 3.3 %combine.1 = (f32[128,768]{1,0:T(8,128)}, bf16[128,768]{1,0:T(8,128)(2,1)S(1)}, bf16[128,768]{1,0:T(8,128)(2,1)S(1)}, bf16[128,768]{1,0:T(8,128)(2,1)S(1)}, f32[...) custom-call(bf16[128,896]{1,0:T(8,128)(2,1)S(1)} %get-tuple-element., ...), custom_call_target="tpu_custom_call" | custom-call | flops 452984832 | bytes 5242880 | tf_op jit(solution)/shard_map/combine/pallas_call | solution.py:105
  255.8 2.7 collective-permute-start.19
  258.5 1.0 collective-permute-done.20
  259.5 0.7 collective-permute-done.19
  260.2 1.5 collective-permute-done.18
  261.8 0.8 collective-permute-start.22
  262.6 2.0 collective-permute-start.23
  264.5 1.2 collective-permute-done.21
  265.7 0.4 collective-permute-done.22
  266.1 0.5 collective-permute-done.23
  266.7 3.8 %collective-permute-start.24 = (bf16[512,128]{1,0:T(8,128)(2,1)S(1)}, bf16[512,128]{1,0:T(8,128)(2,1)S(1)}, u32[]{:S(2)}, u32[]{:S(2)}) collective-permute-start(bf16[512,128]{1,0:T(8,128)(2,1)S(1)} %pad_maximum_fusion.1), channel_id=1, source_target_pairs={{0,2},{1,3},{2,4},{3,5},{4,6},{5,7},{6,0},{7,1},{8,10},{9,11},{10,... | collective-permute-start | bytes 393224 | tf_op jit(solution)/shard_map/ppermute | solution.py:52
  270.4 1.7 collective-permute-start.25
  272.1 2.3 collective-permute-start.26
  274.4 1.1 collective-permute-start.27
  275.5 1.0 collective-permute-start.28
  276.6 1.9 collective-permute-done.25
  278.5 0.7 collective-permute-done.27
  279.2 2.4 collective-permute-done.28
  281.6 2.0 collective-permute-done.29
  283.7 6.2 %collective-permute-start.30 = (bf16[2048,128]{1,0:T(8,128)(2,1)S(1)}, bf16[2048,128]{1,0:T(8,128)(2,1)S(1)}, u32[]{:S(2)}, u32[]{:S(2)}) collective-permute-start(bf16[2048,128]{1,0:T(8,128)(2,1)S(1)} %constant_dynamic-update-slice_fusion.near), channel_id=1, source_target_pairs={{0,1},{1,0},{2,3},{3,2},{4,5},{5,4},{6,7},{7,6},{8,9},{9,8},{10,11... | collective-permute-start | bytes 1572872 | tf_op jit(solution)/shard_map/ppermute | solution.py:74
  289.9 0.8 add_convert_fusion
  290.7 0.7 collective-permute-done.30.far
  291.4 12.3 %atoms.1 = f32[3,1,1024]{2,1,0:T(1,128)} custom-call(s32[4]{0:T(128)S(1)} %pad_add_fusion.pos, s32[10]{0:T(128)S(1)} %multiply_minimum_fusion.starts, s32[2,32]{1,0:T(2,128)S(1)} %bitcast.29, bf16[2048,128]{1,0:T(8,128)(2,1)S(1)} %constant_dynamic-update-slice_fusion.near, bf16[2048,128]{1,0:T(8,128)(2,1)S(1)} %collective-permute-done.30.far, ...), custom_call_target="tpu_custom_call" | custom-call | flops 367001600 | bytes 6291456 | tf_op jit(solution)/shard_map/atoms/pallas_call | solution.py:105
  (91 shorter events, 1.8 us)
Async XLA Ops:
  137.4 10.8 %copy-start.5 = (bf16[4,768,192]{1,2,0:T(8,128)(2,1)S(1)}, bf16[4,768,192]{1,2,0:T(8,128)(2,1)}, u32[]{:S(2)}) copy-start(bf16[4,768,192]{1,2,0:T(8,128)(2,1)} %param.23) | copy-start | bytes 3538948
  137.4 71.9 %all-to-all-start = ((bf16[4,4,128,1024]{3,2,1,0:T(8,128)(2,1)}), bf16[4,4,128,1024]{3,2,1,0:T(8,128)(2,1)}, u32[]{:S(2)}, u32[]{:S(2)}) async-start(bf16[4,4,128,1024]{3,2,1,0:T(8,128)(2,1)} %get-tuple-element.67), calls=%async_computation | async-start | bytes 8388608 | tf_op jit(solution)/shard_map/all_to_all | solution.py:62
  142.5 96.5 %all-gather.4.cloned.1.call-start = ((), (), s32[]{:S(2)}) async-start(), calls=%async_computation.1 | async-start | bytes 1515520 | tf_op jit(solution)/shard_map/all_gather | solution.py:613
  142.5 10.5 %collective-permute-start = (bf16[128,960]{1,0:T(8,128)(2,1)}, bf16[128,960]{1,0:T(8,128)(2,1)}, u32[]{:S(2)}, u32[]{:S(2)}) collective-permute-start(bf16[128,960]{1,0:T(8,128)(2,1)} %get-tuple-element.58), channel_id=1, source_target_pairs={{0,32},{32,64},{64,96},{96,0},{1,33},{33,65},{65,97},{97,1},{2,34}... | collective-permute-start | bytes 737288 | tf_op jit(solution)/shard_map/ppermute | solution.py:38
  144.6 14.1 %collective-permute-start.1 = (bf16[128,960]{1,0:T(8,128)(2,1)}, bf16[128,960]{1,0:T(8,128)(2,1)}, u32[]{:S(2)}, u32[]{:S(2)}) collective-permute-start(bf16[128,960]{1,0:T(8,128)(2,1)} %get-tuple-element.59), channel_id=1, source_target_pairs={{0,64},{32,96},{64,0},{96,32},{1,65},{33,97},{65,1},{97,33},{2,66}... | collective-permute-start | bytes 737288 | tf_op jit(solution)/shard_map/ppermute | solution.py:38
  147.0 11.6 %collective-permute-start.2 = (bf16[128,960]{1,0:T(8,128)(2,1)}, bf16[128,960]{1,0:T(8,128)(2,1)}, u32[]{:S(2)}, u32[]{:S(2)}) collective-permute-start(bf16[128,960]{1,0:T(8,128)(2,1)} %get-tuple-element.60), channel_id=1, source_target_pairs={{0,96},{32,0},{64,32},{96,64},{1,97},{33,1},{65,33},{97,65},{2,98}... | collective-permute-start | bytes 737288 | tf_op jit(solution)/shard_map/ppermute | solution.py:38
  148.9 1.7 copy-start.20
  148.9 3.4 %copy-start.18 = (bf16[7,128,32]{1,2,0:T(8,128)(2,1)S(1)}, bf16[7,128,32]{1,2,0:T(8,128)(2,1)}, u32[]{:S(2)}) copy-start(bf16[7,128,32]{1,2,0:T(8,128)(2,1)} %param.34) | copy-start | bytes 172036
  148.9 9.8 %copy-start.3 = (bf16[128,960]{1,0:T(8,128)(2,1)S(1)}, bf16[128,960]{1,0:T(8,128)(2,1)}, u32[]{:S(2)}) copy-start(bf16[128,960]{1,0:T(8,128)(2,1)} %get-tuple-element.57.m0) | copy-start | bytes 737284
  150.6 15.2 %copy-start.19 = (s32[1024]{0:T(1024)S(1)}, s32[1024]{0:T(1024)}, u32[]{:S(2)}) copy-start(s32[1024]{0:T(1024)} %param.33) | copy-start | bytes 12292
  161.6 15.7 %copy-start.14 = (bf16[1024,128]{1,0:T(8,128)(2,1)S(1)}, bf16[1024,128]{1,0:T(8,128)(2,1)}, u32[]{:S(2)}) copy-start(bf16[1024,128]{1,0:T(8,128)(2,1)} %param.30) | copy-start | bytes 786436
  161.6 6.2 %collective-permute-start.3 = (bf16[128,768]{1,0:T(8,128)(2,1)S(1)}, bf16[128,768]{1,0:T(8,128)(2,1)S(1)}, u32[]{:S(2)}, u32[]{:S(2)}) collective-permute-start(bf16[128,768]{1,0:T(8,128)(2,1)S(1)} %get-tuple-element.61.a0), channel_id=1, source_target_pairs={{0,32},{32,64},{64,96},{96,0},{1,33},{33,65},{65,97},{97,1},{2,34}... | collective-permute-start | bytes 589832 | tf_op jit(solution)/shard_map/ppermute | solution.py:38
  162.8 10.4 %collective-permute-start.4 = (bf16[128,768]{1,0:T(8,128)(2,1)S(1)}, bf16[128,768]{1,0:T(8,128)(2,1)S(1)}, u32[]{:S(2)}, u32[]{:S(2)}) collective-permute-start(bf16[128,768]{1,0:T(8,128)(2,1)S(1)} %get-tuple-element.61.a0), channel_id=1, source_target_pairs={{0,64},{32,96},{64,0},{96,32},{1,65},{33,97},{65,1},{97,33},{2,66}... | collective-permute-start | bytes 589832 | tf_op jit(solution)/shard_map/ppermute | solution.py:38
  165.1 8.1 %collective-permute-start.5 = (bf16[128,768]{1,0:T(8,128)(2,1)S(1)}, bf16[128,768]{1,0:T(8,128)(2,1)S(1)}, u32[]{:S(2)}, u32[]{:S(2)}) collective-permute-start(bf16[128,768]{1,0:T(8,128)(2,1)S(1)} %get-tuple-element.61.a0), channel_id=1, source_target_pairs={{0,96},{32,0},{64,32},{96,64},{1,97},{33,1},{65,33},{97,65},{2,98}... | collective-permute-start | bytes 589832 | tf_op jit(solution)/shard_map/ppermute | solution.py:38
  175.3 33.9 %copy-start.2 = (bf16[256,768]{1,0:T(8,128)(2,1)}, bf16[256,768]{1,0:T(8,128)(2,1)S(1)}, u32[]{:S(2)}) copy-start(bf16[256,768]{1,0:T(8,128)(2,1)S(1)} %get-tuple-element.63.refs_0_) | copy-start | bytes 1179652
  175.3 7.0 %collective-permute-start.6 = (bf16[256,768]{1,0:T(8,128)(2,1)S(1)}, bf16[256,768]{1,0:T(8,128)(2,1)S(1)}, u32[]{:S(2)}, u32[]{:S(2)}) collective-permute-start(bf16[256,768]{1,0:T(8,128)(2,1)S(1)} %get-tuple-element.63.refs_0_), channel_id=1, source_target_pairs={{0,1},{1,0},{2,3},{3,2},{4,5},{5,4},{6,7},{7,6},{8,9},{9,8},{10,11... | collective-permute-start | bytes 1179656 | tf_op jit(solution)/shard_map/ppermute | solution.py:74
  178.1 8.1 %collective-permute-start.16 = (bf16[112,128]{1,0:T(8,128)(2,1)S(1)}, bf16[112,128]{1,0:T(8,128)(2,1)S(1)}, u32[]{:S(2)}, u32[]{:S(2)}) collective-permute-start(bf16[112,128]{1,0:T(8,128)(2,1)S(1)} %pad_maximum_fusion.3), channel_id=1, source_target_pairs={{0,1},{1,2},{2,3},{3,4},{4,5},{5,6},{6,7},{7,8},{8,9},{9,10},{10,1... | collective-permute-start | bytes 86024 | tf_op jit(solution)/shard_map/ppermute | solution.py:569
  182.4 26.9 %copy-start.7 = (bf16[256,768]{1,0:T(8,128)(2,1)}, bf16[256,768]{1,0:T(8,128)(2,1)S(1)}, u32[]{:S(2)}) copy-start(bf16[256,768]{1,0:T(8,128)(2,1)S(1)} %collective-permute-done.6.refs_2_) | copy-start | bytes 1179652
  182.4 25.5 %collective-permute-start.17 = (bf16[112,128]{1,0:T(8,128)(2,1)S(1)}, bf16[112,128]{1,0:T(8,128)(2,1)S(1)}, u32[]{:S(2)}, u32[]{:S(2)}) collective-permute-start(bf16[112,128]{1,0:T(8,128)(2,1)S(1)} %pad_maximum_fusion.4), channel_id=1, source_target_pairs={{1,0},{2,1},{3,2},{4,3},{5,4},{6,5},{7,6},{8,7},{9,8},{10,9},{11,1... | collective-permute-start | bytes 86024 | tf_op jit(solution)/shard_map/ppermute | solution.py:570
  184.6 19.3 %collective-permute-start.7 = (bf16[256,768]{1,0:T(8,128)(2,1)S(1)}, bf16[256,768]{1,0:T(8,128)(2,1)S(1)}, u32[]{:S(2)}, u32[]{:S(2)}) collective-permute-start(bf16[256,768]{1,0:T(8,128)(2,1)S(1)} %get-tuple-element.63.refs_0_), channel_id=1, source_target_pairs={{0,2},{1,3},{2,0},{3,1},{4,6},{5,7},{6,4},{7,5},{8,10},{9,11},{10,... | collective-permute-start | bytes 1179656 | tf_op jit(solution)/shard_map/ppermute | solution.py:56
  186.2 36.1 %copy-start.16 = (bf16[112,128]{1,0:T(8,128)(2,1)}, bf16[112,128]{1,0:T(8,128)(2,1)S(1)}, u32[]{:S(2)}) copy-start(bf16[112,128]{1,0:T(8,128)(2,1)S(1)} %collective-permute-done.16.before) | copy-start | bytes 86020
  186.2 35.3 %collective-permute-start.9 = (bf16[256,768]{1,0:T(8,128)(2,1)S(1)}, bf16[256,768]{1,0:T(8,128)(2,1)S(1)}, u32[]{:S(2)}, u32[]{:S(2)}) collective-permute-start(bf16[256,768]{1,0:T(8,128)(2,1)S(1)} %get-tuple-element.63.refs_0_), channel_id=1, source_target_pairs={{0,4},{1,5},{2,6},{3,7},{4,0},{5,1},{6,2},{7,3},{8,12},{9,13},{10,... | collective-permute-start | bytes 1179656 | tf_op jit(solution)/shard_map/ppermute | solution.py:56
  188.2 33.3 %collective-permute-start.10 = (bf16[256,768]{1,0:T(8,128)(2,1)S(1)}, bf16[256,768]{1,0:T(8,128)(2,1)S(1)}, u32[]{:S(2)}, u32[]{:S(2)}) collective-permute-start(bf16[256,768]{1,0:T(8,128)(2,1)S(1)} %get-tuple-element.63.refs_0_), channel_id=1, source_target_pairs={{0,6},{1,7},{2,4},{3,5},{4,2},{5,3},{6,0},{7,1},{8,14},{9,15},{10,... | collective-permute-start | bytes 1179656 | tf_op jit(solution)/shard_map/ppermute | solution.py:56
  203.9 5.4 %copy-start.10 = (bf16[256,768]{1,0:T(8,128)(2,1)}, bf16[256,768]{1,0:T(8,128)(2,1)S(1)}, u32[]{:S(2)}) copy-start(bf16[256,768]{1,0:T(8,128)(2,1)S(1)} %collective-permute-done.7.refs_1_) | copy-start | bytes 1179652
  203.9 5.4 %collective-permute-start.8 = (bf16[256,768]{1,0:T(8,128)(2,1)S(1)}, bf16[256,768]{1,0:T(8,128)(2,1)S(1)}, u32[]{:S(2)}, u32[]{:S(2)}) collective-permute-start(bf16[256,768]{1,0:T(8,128)(2,1)S(1)} %collective-permute-done.7.refs_1_), channel_id=1, source_target_pairs={{0,1},{1,0},{2,3},{3,2},{4,5},{5,4},{6,7},{7,6},{8,9},{9,8},{10,11... | collective-permute-start | bytes 1179656 | tf_op jit(solution)/shard_map/ppermute | solution.py:74
  207.9 28.9 %copy-start.17 = (bf16[112,128]{1,0:T(8,128)(2,1)}, bf16[112,128]{1,0:T(8,128)(2,1)S(1)}, u32[]{:S(2)}) copy-start(bf16[112,128]{1,0:T(8,128)(2,1)S(1)} %collective-permute-done.17.after) | copy-start | bytes 86020
  209.2 0.8 copy-start.13
  221.5 3.2 %copy-start.8 = (bf16[256,768]{1,0:T(8,128)(2,1)}, bf16[256,768]{1,0:T(8,128)(2,1)S(1)}, u32[]{:S(2)}) copy-start(bf16[256,768]{1,0:T(8,128)(2,1)S(1)} %collective-permute-done.9.refs_0_) | copy-start | bytes 1179652
  221.5 3.1 %copy-start.9 = (bf16[256,768]{1,0:T(8,128)(2,1)}, bf16[256,768]{1,0:T(8,128)(2,1)S(1)}, u32[]{:S(2)}) copy-start(bf16[256,768]{1,0:T(8,128)(2,1)S(1)} %collective-permute-done.10.refs_1_) | copy-start | bytes 1179652
  221.6 1.8 collective-permute-start.11
  222.0 1.9 collective-permute-start.12
  222.3 14.5 %copy-start.15 = (s32[10,112]{1,0:T(8,128)}, s32[10,112]{1,0:T(8,128)S(1)}, u32[]{:S(2)}) copy-start(s32[10,112]{1,0:T(8,128)S(1)} %reshape.25.tokens) | copy-start | bytes 13444
  223.4 1.3 copy-start.11
  223.9 0.7 copy-start.12
  224.7 17.6 %copy-start.1 = (bf16[384,768]{1,0:T(8,128)(2,1)S(1)}, bf16[384,768]{1,0:T(8,128)(2,1)}, u32[]{:S(2)}) copy-start(bf16[384,768]{1,0:T(8,128)(2,1)} %w_out.1) | copy-start | bytes 1769476
  236.8 5.5 %copy-start = (bf16[2,768,384]{2,1,0:T(8,128)(2,1)S(1)}, bf16[2,768,384]{2,1,0:T(8,128)(2,1)}, u32[]{:S(2)}) copy-start(bf16[2,768,384]{2,1,0:T(8,128)(2,1)} %w_in.1) | copy-start | bytes 3538948
  236.8 9.9 %collective-permute-start.13 = (bf16[128,896]{1,0:T(8,128)(2,1)S(1)}, bf16[128,896]{1,0:T(8,128)(2,1)S(1)}, u32[]{:S(2)}, u32[]{:S(2)}) collective-permute-start(bf16[128,896]{1,0:T(8,128)(2,1)S(1)} %get-tuple-element.79), channel_id=1, source_target_pairs={{0,24},{1,25},{2,26},{3,27},{4,28},{5,29},{6,30},{7,31},{8,0},{9,1... | collective-permute-start | bytes 688136 | tf_op jit(solution)/shard_map/ppermute | solution.py:44
  238.3 8.4 %collective-permute-start.14 = (bf16[128,896]{1,0:T(8,128)(2,1)S(1)}, bf16[128,896]{1,0:T(8,128)(2,1)S(1)}, u32[]{:S(2)}, u32[]{:S(2)}) collective-permute-start(bf16[128,896]{1,0:T(8,128)(2,1)S(1)} %get-tuple-element.80), channel_id=1, source_target_pairs={{0,16},{1,17},{2,18},{3,19},{4,20},{5,21},{6,22},{7,23},{8,24},{9,... | collective-permute-start | bytes 688136 | tf_op jit(solution)/shard_map/ppermute | solution.py:44
  239.0 13.2 %collective-permute-start.15 = (bf16[128,896]{1,0:T(8,128)(2,1)S(1)}, bf16[128,896]{1,0:T(8,128)(2,1)S(1)}, u32[]{:S(2)}, u32[]{:S(2)}) collective-permute-start(bf16[128,896]{1,0:T(8,128)(2,1)S(1)} %get-tuple-element.81), channel_id=1, source_target_pairs={{0,8},{1,9},{2,10},{3,11},{4,12},{5,13},{6,14},{7,15},{8,16},{9,17... | collective-permute-start | bytes 688136 | tf_op jit(solution)/shard_map/ppermute | solution.py:44
  255.5 34.4 %copy-start.6 = (f32[128,768]{1,0:T(8,128)S(1)}, f32[128,768]{1,0:T(8,128)}, u32[]{:S(2)}) copy-start(f32[128,768]{1,0:T(8,128)} %get-tuple-element.102) | copy-start | bytes 1179652
  255.5 35.9 %copy-start.4 = (s32[32,2]{0,1:T(2,128)S(1)}, s32[32,2]{0,1:T(2,128)}, u32[]{:S(2)}) copy-start(s32[32,2]{0,1:T(2,128)} %param.32) | copy-start | bytes 772
  255.5 4.0 %collective-permute-start.20 = (bf16[128,128]{1,0:T(8,128)(2,1)S(1)}, bf16[128,128]{1,0:T(8,128)(2,1)S(1)}, u32[]{:S(2)}, u32[]{:S(2)}) collective-permute-start(bf16[128,128]{1,0:T(8,128)(2,1)S(1)} %get-tuple-element.92), channel_id=1, source_target_pairs={{0,32},{32,64},{64,96},{96,0},{1,33},{33,65},{65,97},{97,1},{2,34}... | collective-permute-start | bytes 98312 | tf_op jit(solution)/shard_map/ppermute | solution.py:38
  255.8 4.3 %collective-permute-start.19 = (bf16[128,128]{1,0:T(8,128)(2,1)S(1)}, bf16[128,128]{1,0:T(8,128)(2,1)S(1)}, u32[]{:S(2)}, u32[]{:S(2)}) collective-permute-start(bf16[128,128]{1,0:T(8,128)(2,1)S(1)} %get-tuple-element.91), channel_id=1, source_target_pairs={{0,64},{32,96},{64,0},{96,32},{1,65},{33,97},{65,1},{97,33},{2,66}... | collective-permute-start | bytes 98312 | tf_op jit(solution)/shard_map/ppermute | solution.py:38
  258.5 3.1 %collective-permute-start.18 = (bf16[128,128]{1,0:T(8,128)(2,1)S(1)}, bf16[128,128]{1,0:T(8,128)(2,1)S(1)}, u32[]{:S(2)}, u32[]{:S(2)}) collective-permute-start(bf16[128,128]{1,0:T(8,128)(2,1)S(1)} %get-tuple-element.90), channel_id=1, source_target_pairs={{0,96},{32,0},{64,32},{96,64},{1,97},{33,1},{65,33},{97,65},{2,98}... | collective-permute-start | bytes 98312 | tf_op jit(solution)/shard_map/ppermute | solution.py:38
  261.7 4.1 %collective-permute-start.21 = (bf16[128,128]{1,0:T(8,128)(2,1)S(1)}, bf16[128,128]{1,0:T(8,128)(2,1)S(1)}, u32[]{:S(2)}, u32[]{:S(2)}) collective-permute-start(bf16[128,128]{1,0:T(8,128)(2,1)S(1)} %get-tuple-element.113), channel_id=1, source_target_pairs={{0,8},{1,9},{2,10},{3,11},{4,12},{5,13},{6,14},{7,15},{8,16},{9,17... | collective-permute-start | bytes 98312 | tf_op jit(solution)/shard_map/ppermute | solution.py:44
  261.8 4.4 %collective-permute-start.22 = (bf16[128,128]{1,0:T(8,128)(2,1)S(1)}, bf16[128,128]{1,0:T(8,128)(2,1)S(1)}, u32[]{:S(2)}, u32[]{:S(2)}) collective-permute-start(bf16[128,128]{1,0:T(8,128)(2,1)S(1)} %get-tuple-element.113), channel_id=1, source_target_pairs={{0,16},{1,17},{2,18},{3,19},{4,20},{5,21},{6,22},{7,23},{8,24},{9,... | collective-permute-start | bytes 98312 | tf_op jit(solution)/shard_map/ppermute | solution.py:44
  262.6 4.1 %collective-permute-start.23 = (bf16[128,128]{1,0:T(8,128)(2,1)S(1)}, bf16[128,128]{1,0:T(8,128)(2,1)S(1)}, u32[]{:S(2)}, u32[]{:S(2)}) collective-permute-start(bf16[128,128]{1,0:T(8,128)(2,1)S(1)} %get-tuple-element.113), channel_id=1, source_target_pairs={{0,24},{1,25},{2,26},{3,27},{4,28},{5,29},{6,30},{7,31},{8,0},{9,1... | collective-permute-start | bytes 98312 | tf_op jit(solution)/shard_map/ppermute | solution.py:44
  266.7 9.8 %collective-permute-start.24 = (bf16[512,128]{1,0:T(8,128)(2,1)S(1)}, bf16[512,128]{1,0:T(8,128)(2,1)S(1)}, u32[]{:S(2)}, u32[]{:S(2)}) collective-permute-start(bf16[512,128]{1,0:T(8,128)(2,1)S(1)} %pad_maximum_fusion.1), channel_id=1, source_target_pairs={{0,2},{1,3},{2,4},{3,5},{4,6},{5,7},{6,0},{7,1},{8,10},{9,11},{10,... | collective-permute-start | bytes 393224 | tf_op jit(solution)/shard_map/ppermute | solution.py:52
  270.4 8.0 %collective-permute-start.25 = (bf16[512,128]{1,0:T(8,128)(2,1)S(1)}, bf16[512,128]{1,0:T(8,128)(2,1)S(1)}, u32[]{:S(2)}, u32[]{:S(2)}) collective-permute-start(bf16[512,128]{1,0:T(8,128)(2,1)S(1)} %pad_maximum_fusion.1), channel_id=1, source_target_pairs={{0,4},{1,5},{2,6},{3,7},{4,0},{5,1},{6,2},{7,3},{8,12},{9,13},{10,... | collective-permute-start | bytes 393224 | tf_op jit(solution)/shard_map/ppermute | solution.py:52
  272.1 6.4 %collective-permute-start.26 = (bf16[512,128]{1,0:T(8,128)(2,1)S(1)}, bf16[512,128]{1,0:T(8,128)(2,1)S(1)}, u32[]{:S(2)}, u32[]{:S(2)}) collective-permute-start(bf16[512,128]{1,0:T(8,128)(2,1)S(1)} %pad_maximum_fusion.1), channel_id=1, source_target_pairs={{0,6},{1,7},{2,0},{3,1},{4,2},{5,3},{6,4},{7,5},{8,14},{9,15},{10,... | collective-permute-start | bytes 393224 | tf_op jit(solution)/shard_map/ppermute | solution.py:52
  274.4 4.8 %collective-permute-start.27 = (bf16[128,768]{1,0:T(8,128)(2,1)S(1)}, bf16[128,768]{1,0:T(8,128)(2,1)S(1)}, u32[]{:S(2)}, u32[]{:S(2)}) collective-permute-start(bf16[128,768]{1,0:T(8,128)(2,1)S(1)} %get-tuple-element.96), channel_id=1, source_target_pairs={{0,96},{32,0},{64,32},{96,64},{1,97},{33,1},{65,33},{97,65},{2,98}... | collective-permute-start | bytes 589832 | tf_op jit(solution)/shard_map/ppermute | solution.py:38
  275.5 6.1 %collective-permute-start.28 = (bf16[128,768]{1,0:T(8,128)(2,1)S(1)}, bf16[128,768]{1,0:T(8,128)(2,1)S(1)}, u32[]{:S(2)}, u32[]{:S(2)}) collective-permute-start(bf16[128,768]{1,0:T(8,128)(2,1)S(1)} %get-tuple-element.97), channel_id=1, source_target_pairs={{0,64},{32,96},{64,0},{96,32},{1,65},{33,97},{65,1},{97,33},{2,66}... | collective-permute-start | bytes 589832 | tf_op jit(solution)/shard_map/ppermute | solution.py:38
  276.5 7.1 %collective-permute-start.29 = (bf16[128,768]{1,0:T(8,128)(2,1)S(1)}, bf16[128,768]{1,0:T(8,128)(2,1)S(1)}, u32[]{:S(2)}, u32[]{:S(2)}) collective-permute-start(bf16[128,768]{1,0:T(8,128)(2,1)S(1)} %get-tuple-element.98), channel_id=1, source_target_pairs={{0,32},{32,64},{64,96},{96,0},{1,33},{33,65},{65,97},{97,1},{2,34}... | collective-permute-start | bytes 589832 | tf_op jit(solution)/shard_map/ppermute | solution.py:38
  283.7 7.7 %collective-permute-start.30 = (bf16[2048,128]{1,0:T(8,128)(2,1)S(1)}, bf16[2048,128]{1,0:T(8,128)(2,1)S(1)}, u32[]{:S(2)}, u32[]{:S(2)}) collective-permute-start(bf16[2048,128]{1,0:T(8,128)(2,1)S(1)} %constant_dynamic-update-slice_fusion.near), channel_id=1, source_target_pairs={{0,1},{1,0},{2,3},{3,2},{4,5},{5,4},{6,7},{7,6},{8,9},{9,8},{10,11... | collective-permute-start | bytes 1572872 | tf_op jit(solution)/shard_map/ppermute | solution.py:74
Sparse Core Ops, SparseCore 0:
  182.5 26.8 all-gather.3

commit v2 on v1

--- a/solution.py
+++ b/solution.py
@@ -92,7 +92,7 @@
     return lax.dot_general(a, b, (((1,), (1,)), ((), ())), preferred_element_type=F32)
 
 
-def kernel_call(body, name, out_shape, args, scalars=(), scratch=(), flops=0, size=0, free=0):
+def kernel_call(body, name, out_shape, args, scalars=(), scratch=(), flops=0, size=0, free=0, late=0):
     def whole(a):
         return pl.BlockSpec(
             a.shape, lambda i, n=len(a.shape): (0,) * n, pipeline_mode=pl.Buffered(1)
@@ -106,7 +106,9 @@
         body,
         grid=(1,),
         out_shape=out_shape,
-        in_specs=[pl.BlockSpec(memory_space=pltpu.SMEM)] * len(scalars) + [whole(a) for a in args],
+        in_specs=[pl.BlockSpec(memory_space=pltpu.SMEM)] * len(scalars)
+        + [whole(a) for a in args[: len(args) - late]]
+        + [pl.BlockSpec(memory_space=pltpu.HBM)] * late,
         out_specs=jax.tree.map(whole, out_shape),
         scratch_shapes=list(scratch),
         compiler_params=pltpu.CompilerParams(
@@ -126,25 +128,21 @@
 
 
 def prepare_body(pos, act, cond, bias, *refs):
-    outs, cut, sems = refs[0:4], refs[4], refs[5]
-    copies = []
-    for i in range(NY):
-        copies.append(
-            pltpu.make_async_copy(bias.at[:, :, pl.ds(i * KEYS, KEYS)], cut.at[i], sems.at[i])
-        )
-        copies[i].start()
-    f = pos[0]
-    normed = norm(cond[...].astype(F32)).astype(BF16)
-    hat = norm(act[...].astype(F32))
-    for k in range(NX):
-        dest = lax.rem(f + k, NX)
-        part = hat[:, 0:COLS]
-        for j in range(1, NX):
-            part = jnp.where(dest == j, hat[:, j * COLS : (j + 1) * COLS], part)
-        outs[k][:, 0:DIM] = normed
-        outs[k][:, DIM : DIM + COLS] = part.astype(BF16)
-    for copy in copies:
-        copy.wait()
+    outs, cut = refs[0:4], refs[4]
+    cut[0] = bias[...]
+
+    @pl.when(pl.program_id(0) == 0)
+    def _():
+        f = pos[0]
+        normed = norm(cond[...].astype(F32)).astype(BF16)
+        hat = norm(act[...].astype(F32))
+        for k in range(NX):
+            dest = lax.rem(f + k, NX)
+            part = hat[:, 0:COLS]
+            for j in range(1, NX):
+                part = jnp.where(dest == j, hat[:, j * COLS : (j + 1) * COLS], part)
+            outs[k][:, 0:DIM] = normed
+            outs[k][:, DIM : DIM + COLS] = part.astype(BF16)
 
 
 def adaptive_body(m0, m1, m2, m3, ada, offset, maps, attend, message):
@@ -430,9 +428,15 @@
         select[i * CHUNK : (i + 1) * CHUNK, :] = hit.T.astype(BF16)
 
 
-def atom_body(pos, starts, bounds, near, far, before, own_skip, after, *refs):
-    scale, shift, select, weights, offset, bias, spots, out = refs[0:8]
-    table, skip, state, xs, qs, ks, vs, gs, at_all = refs[8:]
+def atom_body(pos, starts, bounds, near, far, before, own_skip, after, offset, spots, *refs):
+    out = refs[5]
+    table, skip, state, xs, qs, ks, vs, gs, at_all = refs[6:15]
+    select, scale, shift, weights, bias = refs[15:20]
+    sems = refs[20]
+    copies = []
+    for i, there in enumerate(refs[0:5]):
+        copies.append(pltpu.make_async_copy(there, refs[15 + i], sems.at[i]))
+        copies[i].start()
     skip[0:RIM, :] = before[0:RIM, :]
     skip[RIM : RIM + ATOMS, :] = own_skip[...]
     skip[RIM + ATOMS :, :] = after[0:RIM, :]
@@ -445,12 +449,15 @@
             other = pl.multiple_of((place + 1 - c) * ROWS, ROWS)
             table[pl.ds(own, ROWS), :] = near[n : n + ROWS, :]
             table[pl.ds(other, ROWS), :] = far[n : n + ROWS, :]
+    for i in range(3):
+        copies[i].wait()
     for i in range(CHUNKS):
         rows = slice(i * CHUNK, (i + 1) * CHUNK)
         taken = table[pl.ds(pl.multiple_of(starts[i], 16), 128), :]
         now = skip[rows, :].astype(F32) + dot(select[rows, :], taken)
         state[rows, :] = now
         xs[rows, :] = (scale[rows, :] * norm(now) + shift[rows, :]).astype(BF16)
+    copies[3].wait()
     x = xs[...]
     own = slice(RIM, RIM + ATOMS)
     mine = xs[own, :]
@@ -485,6 +492,8 @@
         for i in range(1, HA):
             picked = jnp.where(lane_head == i, summed[i * WQ : (i + 1) * WQ], picked)
         at_all[rows, :] = picked
+
+    copies[4].wait()
 
     def windows(step, carry):
         for i in range(8):
@@ -531,24 +540,24 @@
     wide = pl.BlockSpec((ROWS, DIM + COLS), lambda i: (0, 0), pipeline_mode=pl.Buffered(1))
     *sent, cut = pl.pallas_call(
         prepare_body,
-        grid=(1,),
+        grid=(NY,),
         out_shape=[sent_shape((ROWS, DIM + COLS))] * 4 + [shape((NY, HEADS, ROWS, KEYS))],
         in_specs=[
             pl.BlockSpec(memory_space=pltpu.SMEM),
             block,
             block,
-            pl.BlockSpec(memory_space=pltpu.HBM),
+            pl.BlockSpec((HEADS, ROWS, KEYS), lambda i: (0, 0, i)),
         ],
-        out_specs=[wide] * 4 + [pl.BlockSpec(memory_space=pltpu.HBM)],
-        scratch_shapes=[pltpu.SemaphoreType.DMA((NY,))],
-        compiler_params=pltpu.CompilerParams(dimension_semantics=("arbitrary",)),
-        cost_estimate=pl.CostEstimate(flops=1 << 20, bytes_accessed=10 << 20, transcendentals=0),
+        out_specs=[wide] * 4 + [pl.BlockSpec((1, HEADS, ROWS, KEYS), lambda i: (i, 0, 0, 0))],
+        compiler_params=pltpu.CompilerParams(
+            dimension_semantics=("arbitrary",), vmem_limit_bytes=24 << 20
+        ),
         name="prepare",
     )(
         f_pos,
         pltpu.with_memory_space_constraint(act, pltpu.HBM),
         pltpu.with_memory_space_constraint(token_cond[0], pltpu.HBM),
-        pair_bias,
+        pltpu.with_memory_space_constraint(pair_bias, pltpu.HBM),
     )
     normed = [sent[0]] + [x_shift(sent[k], k) for k in (1, 2, 3)]
     edge_skip, edge_cond, edge_token, _ = lax.optimization_barrier(
@@ -592,6 +601,7 @@
         size=3 << 20,
     )
     attend_all = [attend] + [x_shift(attend, k) for k in (1, 2, 3)]
+    attend_all[3], before, after = lax.optimization_barrier((attend_all[3], before, after))
     q, kv, gate = kernel_call(
         project_body,
         "project",
@@ -604,7 +614,6 @@
     )
     near = [kv] + [z_swap(kv, k) for k in (1, 2, 3)]
     across = c_shift(kv)
-    q, _ = lax.optimization_barrier((q, across))
     q_all = y_collect(q)
     q_all, near_1 = lax.optimization_barrier((q_all, near[1]))
     early = [kv, near_1, across, c_shift(near_1)]
@@ -665,16 +674,11 @@
 
     turns = [y_shift(rows, k) for k in (1, 2, 3)]
     by_y = jnp.concatenate([rows] + turns, axis=0)
-    _, *partial = lax.optimization_barrier((by_y, *sums[1:4]))
+    turns = [z_shift(by_y, k) for k in (1, 2, 3)]
+    by_z = jnp.concatenate([by_y] + turns, axis=0)
+    by_c = c_shift(by_z)
+    _, *partial = lax.optimization_barrier((by_z, *sums[1:4]))
     main = [x_shift(partial[k - 1], NX - k) for k in (1, 2, 3)]
-    turns = [z_shift(by_y, k) for k in (1, 2, 3)]
-    turns, main = lax.optimization_barrier((turns, main))
-    by_z = jnp.concatenate([by_y] + turns, axis=0)
-    token_result = (
-        sums[0] + main[0].astype(F32) + main[1].astype(F32) + main[2].astype(F32)
-    ).astype(BF16)
-    by_c = c_shift(by_z)
-    by_c, token_result = lax.optimization_barrier((by_c, token_result))
 
     scalars = (jnp.stack([y, z, c, t * ATOMS]), starts, window_bounds.T)
     update = kernel_call(
@@ -687,13 +691,13 @@
             before,
             skip,
             after,
+            atom_vectors,
+            position_out,
+            select,
             scale,
             shift,
-            select,
             atom_maps,
-            atom_vectors,
             atom_bias,
-            position_out,
         ),
         scalars,
         free=2,
@@ -707,10 +711,21 @@
             pltpu.VMEM((EXT, CA), BF16),
             pltpu.VMEM((ATOMS, CA), F32),
             pltpu.VMEM((ATOMS, CA), F32),
+            pltpu.VMEM((EXT, 128), BF16),
+            pltpu.VMEM((EXT, CA), F32),
+            pltpu.VMEM((EXT, CA), F32),
+            pltpu.VMEM((7, CA, CA), BF16),
+            pltpu.VMEM((HA, ATOMS, WK), BF16),
+            pltpu.SemaphoreType.DMA((5,)),
         ],
+        late=5,
         flops=2 * 1120 * 128 * 128 * 10,
         size=6 << 20,
     )
+    update, *main = lax.optimization_barrier((update, *main))
+    token_result = (
+        sums[0] + main[0].astype(F32) + main[1].astype(F32) + main[2].astype(F32)
+    ).astype(BF16)
     return (token_result[None], jnp.swapaxes(update, 0, 1))
 
 

time: 311 us -> 178 us (0.57)
  Pallas kernels: 182 us -> 57.1 us
  waiting for transfers between devices: 36.4 us -> 26.7 us
  blocking collectives: 12.1 us -> 17.1 us
  starting transfers between devices: 56.1 us -> 51.4 us
    pallas_call x1, Pallas kernels: 130 us -> 5.64 us  [per_device(): pl.pallas_call(prepare_body, grid=(NY,), out_shape=[sent_shape((ROWS, DIM...]
    ppermute x12, waiting for transfers between devices: 21.2 us -> 9.05 us  [x_shift(): return lax.ppermute(a, 'fsdp', [(i, (i + k) % NX) for i in range(NX)])]
    ppermute x5, starting transfers between devices: 12.7 us -> 5.74 us  [c_shift(): return lax.ppermute(a, 'seq', [(t, t ^ 1) for t in range(NY * NZ * NC)])]
    ppermute x3, waiting for transfers between devices: 1.87 us -> 7.83 us  [z_shift(): return lax.ppermute(a, 'seq', pairs)]
    all_gather x1, blocking collectives: 12.1 us -> 17.1 us  [y_collect(): return lax.all_gather(a, 'seq', axis=0, axis_index_groups=groups)]
  transfers between devices with their start and end apart: 33 -> 33, of which waited for: 19 -> 11; matrix products, arithmetic and copies ran while one was open for 2% -> 4% of each run, Pallas kernels for 12% -> 27%
where the time goes in v2:
time: 178 us; the launch traced here: 177 us
  Pallas kernels  57.1 us (32%)
  starting transfers between devices  51.4 us (29%)
  waiting for transfers between devices  26.7 us (15%)
  blocking collectives  17.1 us (10%)
  between operations  14.4 us (8%)
  local copies, waits for them, and re-layouts  8.6 us (5%)
    pallas_call x6, Pallas kernels, kernel_call(): pl.pallas_call(body, grid=(1,), out_shape=out_shape, in_specs=[pl.BlockSp...  27.8 us
    pallas_call x2, Pallas kernels, attention(): pl.pallas_call(functools.partial(attention_body, merge), grid=(HEADS,), o...  23.6 us
    ppermute x12, starting transfers between devices, x_shift(): return lax.ppermute(a, 'fsdp', [(i, (i + k) % NX) for i in range(NX)])  17.3 us
    all_gather x1, blocking collectives, y_collect(): return lax.all_gather(a, 'seq', axis=0, axis_index_groups=groups)  17.1 us
    ppermute x12, waiting for transfers between devices, x_shift(): return lax.ppermute(a, 'fsdp', [(i, (i + k) % NX) for i in range(NX)])  9.05 us
    ppermute x3, waiting for transfers between devices, z_shift(): return lax.ppermute(a, 'seq', pairs)  7.83 us
    ppermute x6, waiting for transfers between devices, y_shift(): return lax.ppermute(a, 'seq', pairs)  7.26 us
    ppermute x1, starting transfers between devices, per_device(): before = lax.ppermute(edge(ATOMS - RIM, ATOMS), 'seq', up)  5.98 us
  transfers between devices with their start and end apart: 33, of which 11 were waited for; matrix products, arithmetic and copies ran while one was open for 4% of the time, Pallas kernels for 27%

profile of v2, /device:TPU:1, one launch (start us, length us, event | category | flops | bytes accessed | tf_op | source)
XLA Modules:
  0.0 177.0 jit_solution(8921047245242796572)
XLA Ops:
  7.2 5.6 %prepare.1 = (bf16[128,960]{1,0:T(8,128)(2,1)S(1)}, bf16[128,960]{1,0:T(8,128)(2,1)}, bf16[128,960]{1,0:T(8,128)(2,1)S(1)}, bf16[128,960]{1,0:T(8,128)(2,1)S(1)}, bf16[4,4,128,1024]{3,2,1,0:T(8,128)(2,1)}) custom-call(s32[1]{0:T(128)} %bitcast.5.pos, bf16[128,768]{1,0:T(8,128)(2,1)} %bitcast.35, bf16[128,768]{1,0:T(8,128)(2,1)} %bitcast.39, ...), custom_call_target="tpu_custom_call" | custom-call | tf_op jit(solution)/shard_map/prepare/pallas_call | solution.py:541
  12.8 5.2 %all-to-all-start = ((bf16[4,4,128,1024]{3,2,1,0:T(8,128)(2,1)}), bf16[4,4,128,1024]{3,2,1,0:T(8,128)(2,1)}, u32[]{:S(2)}, u32[]{:S(2)}) async-start(bf16[4,4,128,1024]{3,2,1,0:T(8,128)(2,1)} %get-tuple-element.68), calls=%async_computation | async-start | bytes 8388608 | tf_op jit(solution)/shard_map/all_to_all | solution.py:62
  18.0 2.1 %collective-permute-start = (bf16[128,960]{1,0:T(8,128)(2,1)}, bf16[128,960]{1,0:T(8,128)(2,1)S(1)}, u32[]{:S(2)}, u32[]{:S(2)}) collective-permute-start(bf16[128,960]{1,0:T(8,128)(2,1)} %get-tuple-element.56), channel_id=1, source_target_pairs={{0,32},{32,64},{64,96},{96,0},{1,33},{33,65},{65,97},{97,1},{2,34}... | collective-permute-start | bytes 737288 | tf_op jit(solution)/shard_map/ppermute | solution.py:38
  20.0 2.5 %collective-permute-start.1 = (bf16[128,960]{1,0:T(8,128)(2,1)S(1)}, bf16[128,960]{1,0:T(8,128)(2,1)S(1)}, u32[]{:S(2)}, u32[]{:S(2)}) collective-permute-start(bf16[128,960]{1,0:T(8,128)(2,1)S(1)} %get-tuple-element.57), channel_id=1, source_target_pairs={{0,64},{32,96},{64,0},{96,32},{1,65},{33,97},{65,1},{97,33},{2,66}... | collective-permute-start | bytes 737288 | tf_op jit(solution)/shard_map/ppermute | solution.py:38
  22.5 1.2 collective-permute-start.2
  23.8 0.8 constant_dynamic-slice_fusion.offset
  24.6 1.6 copy.24.ada
  26.2 0.8 fusion.16
  27.0 7.1 %collective-permute-done.1.m2 = bf16[128,960]{1,0:T(8,128)(2,1)S(1)} collective-permute-done((bf16[128,960]{1,0:T(8,128)(2,1)S(1)}, bf16[128,960]{1,0:T(8,128)(2,1)S(1)}, u32[]{:S(2)}, u32[]{:S(2)}) %collective-permute-start.1) | collective-permute-done | bytes 245792 | tf_op jit(solution)/shard_map/ppermute | solution.py:38
  34.0 1.9 %adaptive.1 = (bf16[128,768]{1,0:T(8,128)(2,1)S(1)}, bf16[1184,128]{1,0:T(8,128)(2,1)}) custom-call(bf16[128,960]{1,0:T(8,128)(2,1)S(1)} %get-tuple-element.55.m0, bf16[128,960]{1,0:T(8,128)(2,1)S(1)} %collective-permute-done.m1, bf16[128,960]{1,0:T(8,128)(2,1)S(1)} %collective-permute-done.1.m2, bf16[128,960]{1,0:T(8,128)(2,1)S(1)} %collective-permute-done.2.m3, ...), custom_call_target="tpu_custom_call" | custom-call | flops 603979776 | bytes 3145728 | tf_op jit(solution)/shard_map/adaptive/pallas_call | solution.py:105
  35.9 1.1 collective-permute-start.3
  37.0 2.3 %collective-permute-start.4 = (bf16[128,768]{1,0:T(8,128)(2,1)S(1)}, bf16[128,768]{1,0:T(8,128)(2,1)S(1)}, u32[]{:S(2)}, u32[]{:S(2)}) collective-permute-start(bf16[128,768]{1,0:T(8,128)(2,1)S(1)} %get-tuple-element.59.a0), channel_id=1, source_target_pairs={{0,64},{32,96},{64,0},{96,32},{1,65},{33,97},{65,1},{97,33},{2,66}... | collective-permute-start | bytes 589832 | tf_op jit(solution)/shard_map/ppermute | solution.py:38
  39.3 0.7 collective-permute-start.5
  40.0 6.0 %collective-permute-start.6 = (bf16[112,128]{1,0:T(8,128)(2,1)S(1)}, bf16[112,128]{1,0:T(8,128)(2,1)S(1)}, u32[]{:S(2)}, u32[]{:S(2)}) collective-permute-start(bf16[112,128]{1,0:T(8,128)(2,1)S(1)} %pad_maximum_fusion.3), channel_id=1, source_target_pairs={{0,1},{1,2},{2,3},{3,4},{4,5},{5,6},{6,7},{7,8},{8,9},{9,10},{10,1... | collective-permute-start | bytes 86024 | tf_op jit(solution)/shard_map/ppermute | solution.py:578
  46.0 1.9 %collective-permute-start.7 = (bf16[112,128]{1,0:T(8,128)(2,1)S(1)}, bf16[112,128]{1,0:T(8,128)(2,1)S(1)}, u32[]{:S(2)}, u32[]{:S(2)}) collective-permute-start(bf16[112,128]{1,0:T(8,128)(2,1)S(1)} %pad_maximum_fusion.4), channel_id=1, source_target_pairs={{1,0},{2,1},{3,2},{4,3},{5,4},{6,5},{7,6},{8,7},{9,8},{10,9},{11,1... | collective-permute-start | bytes 86024 | tf_op jit(solution)/shard_map/ppermute | solution.py:579
  47.9 1.6 copy.25.weights
  49.5 0.8 dynamic-slice.1.offset
  50.3 0.1 copy.26.mask
  50.4 1.1 collective-permute-done.7.after
  51.6 2.1 %project.1 = (bf16[128,768]{1,0:T(8,128)(2,1)S(1)}, bf16[256,768]{1,0:T(8,128)(2,1)S(1)}, bf16[128,768]{1,0:T(8,128)(2,1)}) custom-call(s32[1]{0:T(128)} %bitcast.5.pos, bf16[128,768]{1,0:T(8,128)(2,1)S(1)} %get-tuple-element.59.a0, bf16[128,768]{1,0:T(8,128)(2,1)S(1)} %collective-permute-done.3.a1, bf16[128,768]{1,0:T(8,128)(2,1)S(1)} %collective-permute-done.4.a2, ...), custom_call_target="tpu_custom_call" | custom-call | flops 603979776 | bytes 4194304 | tf_op jit(solution)/shard_map/project/pallas_call | solution.py:105
  53.8 0.1 stack.64.pos
  53.9 0.1 stack.72.pos
  53.9 1.7 collective-permute-start.8
  55.6 3.7 %collective-permute-start.11 = (bf16[256,768]{1,0:T(8,128)(2,1)S(1)}, bf16[256,768]{1,0:T(8,128)(2,1)S(1)}, u32[]{:S(2)}, u32[]{:S(2)}) collective-permute-start(bf16[256,768]{1,0:T(8,128)(2,1)S(1)} %get-tuple-element.65.refs_0_), channel_id=1, source_target_pairs={{0,4},{1,5},{2,6},{3,7},{4,0},{5,1},{6,2},{7,3},{8,12},{9,13},{10,... | collective-permute-start | bytes 1179656 | tf_op jit(solution)/shard_map/ppermute | solution.py:56
  59.3 17.1 %all-gather = bf16[512,768]{1,0:T(8,128)(2,1)} all-gather(bf16[128,768]{1,0:T(8,128)(2,1)S(1)} %get-tuple-element.64), channel_id=2, replica_groups={{0,8,16,24},{1,9,17,25},{2,10,18,26},{3,11,19,27},{4,12,20,28},{5,13,21..., dimensions={0}, use_global_device_ids=true | all-gather | bytes 983040 | tf_op jit(solution)/shard_map/all_gather | solution.py:70
  76.4 2.5 %collective-permute-start.10 = (bf16[256,768]{1,0:T(8,128)(2,1)S(1)}, bf16[256,768]{1,0:T(8,128)(2,1)S(1)}, u32[]{:S(2)}, u32[]{:S(2)}) collective-permute-start(bf16[256,768]{1,0:T(8,128)(2,1)S(1)} %collective-permute-done.8.refs_1_), channel_id=1, source_target_pairs={{0,1},{1,0},{2,3},{3,2},{4,5},{5,4},{6,7},{7,6},{8,9},{9,8},{10,11... | collective-permute-start | bytes 1179656 | tf_op jit(solution)/shard_map/ppermute | solution.py:74
  79.0 1.3 collective-permute-done.10.refs_3_
  80.3 0.7 copy-done.11
  81.0 11.5 %attention_first.1 = (bf16[128,768]{1,0:T(8,128)(2,1)}, bf16[128,768]{1,0:T(8,128)(2,1)}, bf16[128,768]{1,0:T(8,128)(2,1)}, bf16[128,768]{1,0:T(8,128)(2,1)}, f3...) custom-call(s32[5]{0:T(128)S(1)} %stack.72.pos, ...), custom_call_target="tpu_custom_call" | custom-call | tf_op jit(solution)/shard_map/attention_first/pallas_call | solution.py:352
  92.6 0.5 collective-permute-start.13
  93.1 0.1 collective-permute-start.14
  93.4 0.7 slice.72
  94.1 0.1 slice_reduce_fusion
  94.2 0.7 pad_maximum_fusion.cond
  95.0 0.7 copy-done.9
  95.7 0.2 copy-done.10
  95.9 12.1 %attention_last.1 = (bf16[128,896]{1,0:T(8,128)(2,1)S(1)}, bf16[128,896]{1,0:T(8,128)(2,1)S(1)}, bf16[128,896]{1,0:T(8,128)(2,1)S(1)}, bf16[128,896]{1,0:T(8,128)(2,1)S(1)}) custom-call(s32[5]{0:T(128)S(1)} %stack.64.pos, bf16[4,128,768]{2,1,0:T(8,128)(2,1)} %bitcast.32, bf16[256,768]{1,0:T(8,128)(2,1)} %copy-done.5, bf16[256,768]{1,0:T(8,128)(2,1)} %copy-done.6, ...), custom_call_target="tpu_custom_call" | custom-call | tf_op jit(solution)/shard_map/attention_last/pallas_call | solution.py:352
  108.0 0.7 collective-permute-start.15
  108.7 0.7 collective-permute-start.16
  109.4 0.4 collective-permute-start.17
  109.9 3.2 %atom_first.1 = (bf16[7,128,128]{2,1,0:T(8,128)(2,1)}, bf16[768,128]{1,0:T(8,128)(2,1)}, f32[1120,128]{1,0:T(8,128)}, f32[1120,128]{1,0:T(8,128)}, bf16[1120,128]{1,0:T(8,128)(2,1)}) custom-call(s32[10]{0:T(128)S(1)} %multiply_minimum_fusion.starts, bf16[4,1184,128]{2,1,0:T(8,128)(2,1)} %bitcast.33, bf16[1120,128]{1,0:T(8,128)(2,1)} %pad_maximum_fusion.cond, ...), custom_call_target="tpu_custom_call" | custom-call | flops 73400320 | bytes 3145728 | tf_op jit(solution)/shard_map/atom_first/pallas_call | solution.py:105
  113.1 4.4 %hidden.1.refs_5_ = f32[512,768]{1,0:T(8,128)} custom-call(s32[1]{0:T(128)} %bitcast.5.pos, bf16[2,768,384]{2,1,0:T(8,128)(2,1)S(1)} %copy-done, bf16[384,768]{1,0:T(8,128)(2,1)S(1)} %copy-done.1, bf16[4,1184,128]{2,1,0:T(8,128)(2,1)} %bitcast.34), custom_call_target="tpu_custom_call" | custom-call | flops 905969664 | bytes 6291456 | tf_op jit(solution)/shard_map/hidden/pallas_call | solution.py:105
  117.5 5.1 %collective-permute-done.17.refs_3_ = bf16[128,896]{1,0:T(8,128)(2,1)S(1)} collective-permute-done((bf16[128,896]{1,0:T(8,128)(2,1)S(1)}, bf16[128,896]{1,0:T(8,128)(2,1)S(1)}, u32[]{:S(2)}, u32[]{:S(2)}) %collective-permute-start.17) | collective-permute-done | bytes 229408 | tf_op jit(solution)/shard_map/ppermute | solution.py:44
  122.6 3.4 %combine.1 = (f32[128,768]{1,0:T(8,128)}, bf16[128,768]{1,0:T(8,128)(2,1)S(1)}, bf16[128,768]{1,0:T(8,128)(2,1)S(1)}, bf16[128,768]{1,0:T(8,128)(2,1)S(1)}, f32[...) custom-call(bf16[128,896]{1,0:T(8,128)(2,1)S(1)} %get-tuple-element., ...), custom_call_target="tpu_custom_call" | custom-call | flops 452984832 | bytes 5242880 | tf_op jit(solution)/shard_map/combine/pallas_call | solution.py:105
  126.0 0.8 collective-permute-start.20
  126.9 2.5 %collective-permute-start.19 = (bf16[128,128]{1,0:T(8,128)(2,1)S(1)}, bf16[128,128]{1,0:T(8,128)(2,1)S(1)}, u32[]{:S(2)}, u32[]{:S(2)}) collective-permute-start(bf16[128,128]{1,0:T(8,128)(2,1)S(1)} %get-tuple-element.90), channel_id=1, source_target_pairs={{0,64},{32,96},{64,0},{96,32},{1,65},{33,97},{65,1},{97,33},{2,66}... | collective-permute-start | bytes 98312 | tf_op jit(solution)/shard_map/ppermute | solution.py:38
  129.3 1.2 collective-permute-start.18
  130.5 0.8 collective-permute-done.19
  131.3 1.2 collective-permute-done.18
  132.6 0.8 collective-permute-start.22
  133.4 2.0 %collective-permute-start.23 = (bf16[128,128]{1,0:T(8,128)(2,1)S(1)}, bf16[128,128]{1,0:T(8,128)(2,1)S(1)}, u32[]{:S(2)}, u32[]{:S(2)}) collective-permute-start(bf16[128,128]{1,0:T(8,128)(2,1)S(1)} %get-tuple-element.109), channel_id=1, source_target_pairs={{0,24},{1,25},{2,26},{3,27},{4,28},{5,29},{6,30},{7,31},{8,0},{9,1... | collective-permute-start | bytes 98312 | tf_op jit(solution)/shard_map/ppermute | solution.py:44
  135.4 1.2 collective-permute-done.21
  136.5 0.4 collective-permute-done.22
  136.9 0.5 collective-permute-done.23
  137.5 1.6 collective-permute-start.24
  139.1 3.2 %collective-permute-start.25 = (bf16[512,128]{1,0:T(8,128)(2,1)S(1)}, bf16[512,128]{1,0:T(8,128)(2,1)S(1)}, u32[]{:S(2)}, u32[]{:S(2)}) collective-permute-start(bf16[512,128]{1,0:T(8,128)(2,1)S(1)} %pad_maximum_fusion.1), channel_id=1, source_target_pairs={{0,4},{1,5},{2,6},{3,7},{4,0},{5,1},{6,2},{7,3},{8,12},{9,13},{10,... | collective-permute-start | bytes 393224 | tf_op jit(solution)/shard_map/ppermute | solution.py:52
  142.2 0.5 collective-permute-start.26
  142.7 1.7 collective-permute-done.24
  144.4 6.2 %collective-permute-done.25 = bf16[512,128]{1,0:T(8,128)(2,1)S(1)} collective-permute-done((bf16[512,128]{1,0:T(8,128)(2,1)S(1)}, bf16[512,128]{1,0:T(8,128)(2,1)S(1)}, u32[]{:S(2)}, u32[]{:S(2)}) %collective-permute-start.25) | collective-permute-done | bytes 131104 | tf_op jit(solution)/shard_map/ppermute | solution.py:52
  150.7 2.6 %collective-permute-start.27 = (bf16[2048,128]{1,0:T(8,128)(2,1)S(1)}, bf16[2048,128]{1,0:T(8,128)(2,1)S(1)}, u32[]{:S(2)}, u32[]{:S(2)}) collective-permute-start(bf16[2048,128]{1,0:T(8,128)(2,1)S(1)} %constant_dynamic-update-slice_fusion.near), channel_id=1, source_target_pairs={{0,1},{1,0},{2,3},{3,2},{4,5},{5,4},{6,7},{7,6},{8,9},{9,8},{10,11... | collective-permute-start | bytes 1572872 | tf_op jit(solution)/shard_map/ppermute | solution.py:74
  153.3 2.5 %collective-permute-start.28 = (bf16[128,768]{1,0:T(8,128)(2,1)S(1)}, bf16[128,768]{1,0:T(8,128)(2,1)S(1)}, u32[]{:S(2)}, u32[]{:S(2)}) collective-permute-start(bf16[128,768]{1,0:T(8,128)(2,1)S(1)} %get-tuple-element.101), channel_id=1, source_target_pairs={{0,96},{32,0},{64,32},{96,64},{1,97},{33,1},{65,33},{97,65},{2,98}... | collective-permute-start | bytes 589832 | tf_op jit(solution)/shard_map/ppermute | solution.py:38
  155.8 0.6 collective-permute-start.30
  156.5 12.8 %atoms.1 = f32[3,1,1024]{2,1,0:T(1,128)} custom-call(s32[4]{0:T(128)S(1)} %pad_add_fusion.pos, s32[10]{0:T(128)S(1)} %multiply_minimum_fusion.starts, s32[2,32]{1,0:T(2,128)S(1)} %bitcast.30, bf16[2048,128]{1,0:T(8,128)(2,1)S(1)} %constant_dynamic-update-slice_fusion.near, bf16[2048,128]{1,0:T(8,128)(2,1)S(1)} %collective-permute-done.27.far, ...), custom_call_target="tpu_custom_call" | custom-call | flops 367001600 | bytes 6291456 | tf_op jit(solution)/shard_map/atoms/pallas_call | solution.py:105
  169.4 0.8 fusion
  (89 shorter events, 0.8 us)
Async XLA Ops:
  12.8 10.8 %copy-start.18 = (s32[1024]{0:T(1024)S(1)}, s32[1024]{0:T(1024)}, u32[]{:S(2)}) copy-start(s32[1024]{0:T(1024)} %param.33) | copy-start | bytes 12292
  12.8 11.0 %copy-start.16 = (bf16[7,128,32]{1,2,0:T(8,128)(2,1)S(1)}, bf16[7,128,32]{1,2,0:T(8,128)(2,1)}, u32[]{:S(2)}) copy-start(bf16[7,128,32]{1,2,0:T(8,128)(2,1)} %param.34) | copy-start | bytes 172036
  12.8 11.0 %copy-start.17 = (bf16[192,128]{1,0:T(8,128)(2,1)S(1)}, bf16[192,128]{1,0:T(8,128)(2,1)}, u32[]{:S(2)}) copy-start(bf16[192,128]{1,0:T(8,128)(2,1)} %param.35) | copy-start | bytes 147460
  12.8 67.5 %all-to-all-start = ((bf16[4,4,128,1024]{3,2,1,0:T(8,128)(2,1)}), bf16[4,4,128,1024]{3,2,1,0:T(8,128)(2,1)}, u32[]{:S(2)}, u32[]{:S(2)}) async-start(bf16[4,4,128,1024]{3,2,1,0:T(8,128)(2,1)} %get-tuple-element.68), calls=%async_computation | async-start | bytes 8388608 | tf_op jit(solution)/shard_map/all_to_all | solution.py:62
  18.0 91.9 %all-gather.4.cloned.1.call-start = ((), (), s32[]{:S(2)}) async-start(), calls=%async_computation.1 | async-start | bytes 1515520 | tf_op jit(solution)/shard_map/all_gather | solution.py:622
  18.0 9.0 %collective-permute-start = (bf16[128,960]{1,0:T(8,128)(2,1)}, bf16[128,960]{1,0:T(8,128)(2,1)S(1)}, u32[]{:S(2)}, u32[]{:S(2)}) collective-permute-start(bf16[128,960]{1,0:T(8,128)(2,1)} %get-tuple-element.56), channel_id=1, source_target_pairs={{0,32},{32,64},{64,96},{96,0},{1,33},{33,65},{65,97},{97,1},{2,34}... | collective-permute-start | bytes 737288 | tf_op jit(solution)/shard_map/ppermute | solution.py:38
  20.0 14.0 %collective-permute-start.1 = (bf16[128,960]{1,0:T(8,128)(2,1)S(1)}, bf16[128,960]{1,0:T(8,128)(2,1)S(1)}, u32[]{:S(2)}, u32[]{:S(2)}) collective-permute-start(bf16[128,960]{1,0:T(8,128)(2,1)S(1)} %get-tuple-element.57), channel_id=1, source_target_pairs={{0,64},{32,96},{64,0},{96,32},{1,65},{33,97},{65,1},{97,33},{2,66}... | collective-permute-start | bytes 737288 | tf_op jit(solution)/shard_map/ppermute | solution.py:38
  22.5 11.5 %collective-permute-start.2 = (bf16[128,960]{1,0:T(8,128)(2,1)S(1)}, bf16[128,960]{1,0:T(8,128)(2,1)S(1)}, u32[]{:S(2)}, u32[]{:S(2)}) collective-permute-start(bf16[128,960]{1,0:T(8,128)(2,1)S(1)} %get-tuple-element.58), channel_id=1, source_target_pairs={{0,96},{32,0},{64,32},{96,64},{1,97},{33,1},{65,33},{97,65},{2,98}... | collective-permute-start | bytes 737288 | tf_op jit(solution)/shard_map/ppermute | solution.py:38
  35.9 14.4 %copy-start.19 = (s32[128]{0:T(128)S(1)}, s32[128]{0:T(128)}, u32[]{:S(2)}) copy-start(s32[128]{0:T(128)} %param.22) | copy-start | bytes 1540
  35.9 15.7 %collective-permute-start.3 = (bf16[128,768]{1,0:T(8,128)(2,1)S(1)}, bf16[128,768]{1,0:T(8,128)(2,1)S(1)}, u32[]{:S(2)}, u32[]{:S(2)}) collective-permute-start(bf16[128,768]{1,0:T(8,128)(2,1)S(1)} %get-tuple-element.59.a0), channel_id=1, source_target_pairs={{0,32},{32,64},{64,96},{96,0},{1,33},{33,65},{65,97},{97,1},{2,34}... | collective-permute-start | bytes 589832 | tf_op jit(solution)/shard_map/ppermute | solution.py:38
  37.0 14.6 %collective-permute-start.4 = (bf16[128,768]{1,0:T(8,128)(2,1)S(1)}, bf16[128,768]{1,0:T(8,128)(2,1)S(1)}, u32[]{:S(2)}, u32[]{:S(2)}) collective-permute-start(bf16[128,768]{1,0:T(8,128)(2,1)S(1)} %get-tuple-element.59.a0), channel_id=1, source_target_pairs={{0,64},{32,96},{64,0},{96,32},{1,65},{33,97},{65,1},{97,33},{2,66}... | collective-permute-start | bytes 589832 | tf_op jit(solution)/shard_map/ppermute | solution.py:38
  39.3 12.3 %collective-permute-start.5 = (bf16[128,768]{1,0:T(8,128)(2,1)S(1)}, bf16[128,768]{1,0:T(8,128)(2,1)S(1)}, u32[]{:S(2)}, u32[]{:S(2)}) collective-permute-start(bf16[128,768]{1,0:T(8,128)(2,1)S(1)} %get-tuple-element.59.a0), channel_id=1, source_target_pairs={{0,96},{32,0},{64,32},{96,64},{1,97},{33,1},{65,33},{97,65},{2,98}... | collective-permute-start | bytes 589832 | tf_op jit(solution)/shard_map/ppermute | solution.py:38
  40.0 10.5 %collective-permute-start.6 = (bf16[112,128]{1,0:T(8,128)(2,1)S(1)}, bf16[112,128]{1,0:T(8,128)(2,1)S(1)}, u32[]{:S(2)}, u32[]{:S(2)}) collective-permute-start(bf16[112,128]{1,0:T(8,128)(2,1)S(1)} %pad_maximum_fusion.3), channel_id=1, source_target_pairs={{0,1},{1,2},{2,3},{3,4},{4,5},{5,6},{6,7},{7,8},{8,9},{9,10},{10,1... | collective-permute-start | bytes 86024 | tf_op jit(solution)/shard_map/ppermute | solution.py:578
  46.0 5.6 %collective-permute-start.7 = (bf16[112,128]{1,0:T(8,128)(2,1)S(1)}, bf16[112,128]{1,0:T(8,128)(2,1)S(1)}, u32[]{:S(2)}, u32[]{:S(2)}) collective-permute-start(bf16[112,128]{1,0:T(8,128)(2,1)S(1)} %pad_maximum_fusion.4), channel_id=1, source_target_pairs={{1,0},{2,1},{3,2},{4,3},{5,4},{6,5},{7,6},{8,7},{9,8},{10,9},{11,1... | collective-permute-start | bytes 86024 | tf_op jit(solution)/shard_map/ppermute | solution.py:579
  50.4 43.7 %copy-start.14 = (bf16[112,128]{1,0:T(8,128)(2,1)}, bf16[112,128]{1,0:T(8,128)(2,1)S(1)}, u32[]{:S(2)}) copy-start(bf16[112,128]{1,0:T(8,128)(2,1)S(1)} %collective-permute-done.6.before) | copy-start | bytes 86020
  51.6 41.0 %copy-start.15 = (bf16[112,128]{1,0:T(8,128)(2,1)}, bf16[112,128]{1,0:T(8,128)(2,1)S(1)}, u32[]{:S(2)}) copy-start(bf16[112,128]{1,0:T(8,128)(2,1)S(1)} %collective-permute-done.7.after) | copy-start | bytes 86020
  53.7 26.6 %copy-start.2 = (bf16[256,768]{1,0:T(8,128)(2,1)}, bf16[256,768]{1,0:T(8,128)(2,1)S(1)}, u32[]{:S(2)}) copy-start(bf16[256,768]{1,0:T(8,128)(2,1)S(1)} %get-tuple-element.65.refs_0_) | copy-start | bytes 1179652
  53.9 22.5 %collective-permute-start.8 = (bf16[256,768]{1,0:T(8,128)(2,1)S(1)}, bf16[256,768]{1,0:T(8,128)(2,1)S(1)}, u32[]{:S(2)}, u32[]{:S(2)}) collective-permute-start(bf16[256,768]{1,0:T(8,128)(2,1)S(1)} %get-tuple-element.65.refs_0_), channel_id=1, source_target_pairs={{0,2},{1,3},{2,0},{3,1},{4,6},{5,7},{6,4},{7,5},{8,10},{9,11},{10,... | collective-permute-start | bytes 1179656 | tf_op jit(solution)/shard_map/ppermute | solution.py:56
  55.6 23.4 %collective-permute-start.9 = (bf16[256,768]{1,0:T(8,128)(2,1)S(1)}, bf16[256,768]{1,0:T(8,128)(2,1)S(1)}, u32[]{:S(2)}, u32[]{:S(2)}) collective-permute-start(bf16[256,768]{1,0:T(8,128)(2,1)S(1)} %get-tuple-element.65.refs_0_), channel_id=1, source_target_pairs={{0,1},{1,0},{2,3},{3,2},{4,5},{5,4},{6,7},{7,6},{8,9},{9,8},{10,11... | collective-permute-start | bytes 1179656 | tf_op jit(solution)/shard_map/ppermute | solution.py:74
  55.6 37.0 %collective-permute-start.11 = (bf16[256,768]{1,0:T(8,128)(2,1)S(1)}, bf16[256,768]{1,0:T(8,128)(2,1)S(1)}, u32[]{:S(2)}, u32[]{:S(2)}) collective-permute-start(bf16[256,768]{1,0:T(8,128)(2,1)S(1)} %get-tuple-element.65.refs_0_), channel_id=1, source_target_pairs={{0,4},{1,5},{2,6},{3,7},{4,0},{5,1},{6,2},{7,3},{8,12},{9,13},{10,... | collective-permute-start | bytes 1179656 | tf_op jit(solution)/shard_map/ppermute | solution.py:56
  59.3 33.3 %collective-permute-start.12 = (bf16[256,768]{1,0:T(8,128)(2,1)S(1)}, bf16[256,768]{1,0:T(8,128)(2,1)S(1)}, u32[]{:S(2)}, u32[]{:S(2)}) collective-permute-start(bf16[256,768]{1,0:T(8,128)(2,1)S(1)} %get-tuple-element.65.refs_0_), channel_id=1, source_target_pairs={{0,6},{1,7},{2,4},{3,5},{4,2},{5,3},{6,0},{7,1},{8,14},{9,15},{10,... | collective-permute-start | bytes 1179656 | tf_op jit(solution)/shard_map/ppermute | solution.py:56
  76.4 3.9 %copy-start.7 = (bf16[256,768]{1,0:T(8,128)(2,1)}, bf16[256,768]{1,0:T(8,128)(2,1)S(1)}, u32[]{:S(2)}) copy-start(bf16[256,768]{1,0:T(8,128)(2,1)S(1)} %collective-permute-done.8.refs_1_) | copy-start | bytes 1179652
  76.4 3.8 %collective-permute-start.10 = (bf16[256,768]{1,0:T(8,128)(2,1)S(1)}, bf16[256,768]{1,0:T(8,128)(2,1)S(1)}, u32[]{:S(2)}, u32[]{:S(2)}) collective-permute-start(bf16[256,768]{1,0:T(8,128)(2,1)S(1)} %collective-permute-done.8.refs_1_), channel_id=1, source_target_pairs={{0,1},{1,0},{2,3},{3,2},{4,5},{5,4},{6,7},{7,6},{8,9},{9,8},{10,11... | collective-permute-start | bytes 1179656 | tf_op jit(solution)/shard_map/ppermute | solution.py:74
  78.9 15.3 %copy-start.12 = (bf16[1024,128]{1,0:T(8,128)(2,1)S(1)}, bf16[1024,128]{1,0:T(8,128)(2,1)}, u32[]{:S(2)}) copy-start(bf16[1024,128]{1,0:T(8,128)(2,1)} %param.30) | copy-start | bytes 786436
  79.0 1.3 copy-start.8
  80.3 0.8 copy-start.11
  92.6 2.4 %copy-start.5 = (bf16[256,768]{1,0:T(8,128)(2,1)}, bf16[256,768]{1,0:T(8,128)(2,1)S(1)}, u32[]{:S(2)}) copy-start(bf16[256,768]{1,0:T(8,128)(2,1)S(1)} %collective-permute-done.11.refs_0_) | copy-start | bytes 1179652
  92.6 2.4 %copy-start.6 = (bf16[256,768]{1,0:T(8,128)(2,1)}, bf16[256,768]{1,0:T(8,128)(2,1)S(1)}, u32[]{:S(2)}) copy-start(bf16[256,768]{1,0:T(8,128)(2,1)S(1)} %collective-permute-done.12.refs_1_) | copy-start | bytes 1179652
  92.6 2.3 %collective-permute-start.13 = (bf16[256,768]{1,0:T(8,128)(2,1)S(1)}, bf16[256,768]{1,0:T(8,128)(2,1)S(1)}, u32[]{:S(2)}, u32[]{:S(2)}) collective-permute-start(bf16[256,768]{1,0:T(8,128)(2,1)S(1)} %collective-permute-done.11.refs_0_), channel_id=1, source_target_pairs={{0,1},{1,0},{2,3},{3,2},{4,5},{5,4},{6,7},{7,6},{8,9},{9,8},{10,11... | collective-permute-start | bytes 1179656 | tf_op jit(solution)/shard_map/ppermute | solution.py:74
  93.1 1.9 %collective-permute-start.14 = (bf16[256,768]{1,0:T(8,128)(2,1)S(1)}, bf16[256,768]{1,0:T(8,128)(2,1)S(1)}, u32[]{:S(2)}, u32[]{:S(2)}) collective-permute-start(bf16[256,768]{1,0:T(8,128)(2,1)S(1)} %collective-permute-done.12.refs_1_), channel_id=1, source_target_pairs={{0,1},{1,0},{2,3},{3,2},{4,5},{5,4},{6,7},{7,6},{8,9},{9,8},{10,11... | collective-permute-start | bytes 1179656 | tf_op jit(solution)/shard_map/ppermute | solution.py:74
  93.4 14.6 %copy-start.13 = (s32[10,112]{1,0:T(8,128)}, s32[10,112]{1,0:T(8,128)S(1)}, u32[]{:S(2)}) copy-start(s32[10,112]{1,0:T(8,128)S(1)} %reshape.25.tokens) | copy-start | bytes 13444
  95.0 0.7 copy-start.9
  95.0 0.9 copy-start.10
  95.9 17.2 %copy-start.1 = (bf16[384,768]{1,0:T(8,128)(2,1)S(1)}, bf16[384,768]{1,0:T(8,128)(2,1)}, u32[]{:S(2)}) copy-start(bf16[384,768]{1,0:T(8,128)(2,1)} %w_out.1) | copy-start | bytes 1769476
  107.9 5.2 %copy-start = (bf16[2,768,384]{2,1,0:T(8,128)(2,1)S(1)}, bf16[2,768,384]{2,1,0:T(8,128)(2,1)}, u32[]{:S(2)}) copy-start(bf16[2,768,384]{2,1,0:T(8,128)(2,1)} %w_in.1) | copy-start | bytes 3538948
  108.0 9.5 %collective-permute-start.15 = (bf16[128,896]{1,0:T(8,128)(2,1)S(1)}, bf16[128,896]{1,0:T(8,128)(2,1)S(1)}, u32[]{:S(2)}, u32[]{:S(2)}) collective-permute-start(bf16[128,896]{1,0:T(8,128)(2,1)S(1)} %get-tuple-element.80), channel_id=1, source_target_pairs={{0,24},{1,25},{2,26},{3,27},{4,28},{5,29},{6,30},{7,31},{8,0},{9,1... | collective-permute-start | bytes 688136 | tf_op jit(solution)/shard_map/ppermute | solution.py:44
  108.7 8.8 %collective-permute-start.16 = (bf16[128,896]{1,0:T(8,128)(2,1)S(1)}, bf16[128,896]{1,0:T(8,128)(2,1)S(1)}, u32[]{:S(2)}, u32[]{:S(2)}) collective-permute-start(bf16[128,896]{1,0:T(8,128)(2,1)S(1)} %get-tuple-element.81), channel_id=1, source_target_pairs={{0,16},{1,17},{2,18},{3,19},{4,20},{5,21},{6,22},{7,23},{8,24},{9,... | collective-permute-start | bytes 688136 | tf_op jit(solution)/shard_map/ppermute | solution.py:44
  109.4 13.2 %collective-permute-start.17 = (bf16[128,896]{1,0:T(8,128)(2,1)S(1)}, bf16[128,896]{1,0:T(8,128)(2,1)S(1)}, u32[]{:S(2)}, u32[]{:S(2)}) collective-permute-start(bf16[128,896]{1,0:T(8,128)(2,1)S(1)} %get-tuple-element.82), channel_id=1, source_target_pairs={{0,8},{1,9},{2,10},{3,11},{4,12},{5,13},{6,14},{7,15},{8,16},{9,17... | collective-permute-start | bytes 688136 | tf_op jit(solution)/shard_map/ppermute | solution.py:44
  122.6 33.8 %copy-start.3 = (s32[32,2]{0,1:T(2,128)S(1)}, s32[32,2]{0,1:T(2,128)}, u32[]{:S(2)}) copy-start(s32[32,2]{0,1:T(2,128)} %param.32) | copy-start | bytes 772
  126.0 4.5 %collective-permute-start.20 = (bf16[128,128]{1,0:T(8,128)(2,1)S(1)}, bf16[128,128]{1,0:T(8,128)(2,1)S(1)}, u32[]{:S(2)}, u32[]{:S(2)}) collective-permute-start(bf16[128,128]{1,0:T(8,128)(2,1)S(1)} %get-tuple-element.91), channel_id=1, source_target_pairs={{0,32},{32,64},{64,96},{96,0},{1,33},{33,65},{65,97},{97,1},{2,34}... | collective-permute-start | bytes 98312 | tf_op jit(solution)/shard_map/ppermute | solution.py:38
  126.9 4.4 %collective-permute-start.19 = (bf16[128,128]{1,0:T(8,128)(2,1)S(1)}, bf16[128,128]{1,0:T(8,128)(2,1)S(1)}, u32[]{:S(2)}, u32[]{:S(2)}) collective-permute-start(bf16[128,128]{1,0:T(8,128)(2,1)S(1)} %get-tuple-element.90), channel_id=1, source_target_pairs={{0,64},{32,96},{64,0},{96,32},{1,65},{33,97},{65,1},{97,33},{2,66}... | collective-permute-start | bytes 98312 | tf_op jit(solution)/shard_map/ppermute | solution.py:38
  129.3 3.1 %collective-permute-start.18 = (bf16[128,128]{1,0:T(8,128)(2,1)S(1)}, bf16[128,128]{1,0:T(8,128)(2,1)S(1)}, u32[]{:S(2)}, u32[]{:S(2)}) collective-permute-start(bf16[128,128]{1,0:T(8,128)(2,1)S(1)} %get-tuple-element.89), channel_id=1, source_target_pairs={{0,96},{32,0},{64,32},{96,64},{1,97},{33,1},{65,33},{97,65},{2,98}... | collective-permute-start | bytes 98312 | tf_op jit(solution)/shard_map/ppermute | solution.py:38
  132.5 4.1 %collective-permute-start.21 = (bf16[128,128]{1,0:T(8,128)(2,1)S(1)}, bf16[128,128]{1,0:T(8,128)(2,1)S(1)}, u32[]{:S(2)}, u32[]{:S(2)}) collective-permute-start(bf16[128,128]{1,0:T(8,128)(2,1)S(1)} %get-tuple-element.109), channel_id=1, source_target_pairs={{0,8},{1,9},{2,10},{3,11},{4,12},{5,13},{6,14},{7,15},{8,16},{9,17... | collective-permute-start | bytes 98312 | tf_op jit(solution)/shard_map/ppermute | solution.py:44
  132.6 4.4 %collective-permute-start.22 = (bf16[128,128]{1,0:T(8,128)(2,1)S(1)}, bf16[128,128]{1,0:T(8,128)(2,1)S(1)}, u32[]{:S(2)}, u32[]{:S(2)}) collective-permute-start(bf16[128,128]{1,0:T(8,128)(2,1)S(1)} %get-tuple-element.109), channel_id=1, source_target_pairs={{0,16},{1,17},{2,18},{3,19},{4,20},{5,21},{6,22},{7,23},{8,24},{9,... | collective-permute-start | bytes 98312 | tf_op jit(solution)/shard_map/ppermute | solution.py:44
  133.4 4.1 %collective-permute-start.23 = (bf16[128,128]{1,0:T(8,128)(2,1)S(1)}, bf16[128,128]{1,0:T(8,128)(2,1)S(1)}, u32[]{:S(2)}, u32[]{:S(2)}) collective-permute-start(bf16[128,128]{1,0:T(8,128)(2,1)S(1)} %get-tuple-element.109), channel_id=1, source_target_pairs={{0,24},{1,25},{2,26},{3,27},{4,28},{5,29},{6,30},{7,31},{8,0},{9,1... | collective-permute-start | bytes 98312 | tf_op jit(solution)/shard_map/ppermute | solution.py:44
  137.5 6.9 %collective-permute-start.24 = (bf16[512,128]{1,0:T(8,128)(2,1)S(1)}, bf16[512,128]{1,0:T(8,128)(2,1)S(1)}, u32[]{:S(2)}, u32[]{:S(2)}) collective-permute-start(bf16[512,128]{1,0:T(8,128)(2,1)S(1)} %pad_maximum_fusion.1), channel_id=1, source_target_pairs={{0,2},{1,3},{2,4},{3,5},{4,6},{5,7},{6,0},{7,1},{8,10},{9,11},{10,... | collective-permute-start | bytes 393224 | tf_op jit(solution)/shard_map/ppermute | solution.py:52
  139.1 11.5 %collective-permute-start.25 = (bf16[512,128]{1,0:T(8,128)(2,1)S(1)}, bf16[512,128]{1,0:T(8,128)(2,1)S(1)}, u32[]{:S(2)}, u32[]{:S(2)}) collective-permute-start(bf16[512,128]{1,0:T(8,128)(2,1)S(1)} %pad_maximum_fusion.1), channel_id=1, source_target_pairs={{0,4},{1,5},{2,6},{3,7},{4,0},{5,1},{6,2},{7,3},{8,12},{9,13},{10,... | collective-permute-start | bytes 393224 | tf_op jit(solution)/shard_map/ppermute | solution.py:52
  142.2 8.4 %collective-permute-start.26 = (bf16[512,128]{1,0:T(8,128)(2,1)S(1)}, bf16[512,128]{1,0:T(8,128)(2,1)S(1)}, u32[]{:S(2)}, u32[]{:S(2)}) collective-permute-start(bf16[512,128]{1,0:T(8,128)(2,1)S(1)} %pad_maximum_fusion.1), channel_id=1, source_target_pairs={{0,6},{1,7},{2,0},{3,1},{4,2},{5,3},{6,4},{7,5},{8,14},{9,15},{10,... | collective-permute-start | bytes 393224 | tf_op jit(solution)/shard_map/ppermute | solution.py:52
  150.7 5.8 %collective-permute-start.27 = (bf16[2048,128]{1,0:T(8,128)(2,1)S(1)}, bf16[2048,128]{1,0:T(8,128)(2,1)S(1)}, u32[]{:S(2)}, u32[]{:S(2)}) collective-permute-start(bf16[2048,128]{1,0:T(8,128)(2,1)S(1)} %constant_dynamic-update-slice_fusion.near), channel_id=1, source_target_pairs={{0,1},{1,0},{2,3},{3,2},{4,5},{5,4},{6,7},{7,6},{8,9},{9,8},{10,11... | collective-permute-start | bytes 1572872 | tf_op jit(solution)/shard_map/ppermute | solution.py:74
  153.3 16.0 %collective-permute-start.28 = (bf16[128,768]{1,0:T(8,128)(2,1)S(1)}, bf16[128,768]{1,0:T(8,128)(2,1)S(1)}, u32[]{:S(2)}, u32[]{:S(2)}) collective-permute-start(bf16[128,768]{1,0:T(8,128)(2,1)S(1)} %get-tuple-element.101), channel_id=1, source_target_pairs={{0,96},{32,0},{64,32},{96,64},{1,97},{33,1},{65,33},{97,65},{2,98}... | collective-permute-start | bytes 589832 | tf_op jit(solution)/shard_map/ppermute | solution.py:38
  155.8 13.5 %collective-permute-start.29 = (bf16[128,768]{1,0:T(8,128)(2,1)S(1)}, bf16[128,768]{1,0:T(8,128)(2,1)S(1)}, u32[]{:S(2)}, u32[]{:S(2)}) collective-permute-start(bf16[128,768]{1,0:T(8,128)(2,1)S(1)} %get-tuple-element.102), channel_id=1, source_target_pairs={{0,64},{32,96},{64,0},{96,32},{1,65},{33,97},{65,1},{97,33},{2,66}... | collective-permute-start | bytes 589832 | tf_op jit(solution)/shard_map/ppermute | solution.py:38
  155.8 13.5 %collective-permute-start.30 = (bf16[128,768]{1,0:T(8,128)(2,1)S(1)}, bf16[128,768]{1,0:T(8,128)(2,1)S(1)}, u32[]{:S(2)}, u32[]{:S(2)}) collective-permute-start(bf16[128,768]{1,0:T(8,128)(2,1)S(1)} %get-tuple-element.103), channel_id=1, source_target_pairs={{0,32},{32,64},{64,96},{96,0},{1,33},{33,65},{65,97},{97,1},{2,34}... | collective-permute-start | bytes 589832 | tf_op jit(solution)/shard_map/ppermute | solution.py:38
  156.5 12.9 %copy-start.4 = (f32[128,768]{1,0:T(8,128)S(1)}, f32[128,768]{1,0:T(8,128)}, u32[]{:S(2)}) copy-start(f32[128,768]{1,0:T(8,128)} %get-tuple-element.87) | copy-start | bytes 1179652
Sparse Core Ops, SparseCore 0:
  53.8 28.2 all-gather.3

commit v3 on v2

--- a/solution.py
+++ b/solution.py
@@ -92,7 +92,7 @@
     return lax.dot_general(a, b, (((1,), (1,)), ((), ())), preferred_element_type=F32)
 
 
-def kernel_call(body, name, out_shape, args, scalars=(), scratch=(), flops=0, size=0, free=0, late=0):
+def kernel_call(body, name, out_shape, args, scalars=(), scratch=(), flops=0, size=0, free=0, late=0, here=0):
     def whole(a):
         return pl.BlockSpec(
             a.shape, lambda i, n=len(a.shape): (0,) * n, pipeline_mode=pl.Buffered(1)
@@ -107,7 +107,8 @@
         grid=(1,),
         out_shape=out_shape,
         in_specs=[pl.BlockSpec(memory_space=pltpu.SMEM)] * len(scalars)
-        + [whole(a) for a in args[: len(args) - late]]
+        + [pl.BlockSpec(memory_space=pltpu.VMEM)] * here
+        + [whole(a) for a in args[here : len(args) - late]]
         + [pl.BlockSpec(memory_space=pltpu.HBM)] * late,
         out_specs=jax.tree.map(whole, out_shape),
         scratch_shapes=list(scratch),
@@ -596,6 +597,7 @@
         "adaptive",
         [sent_shape((ROWS, DIM)), shape((DIM + COLS + 7 * 32, CA))],
         (*normed, ada_weights, offsets[0:2], own_maps),
+        here=4,
         free=7,
         flops=4 * 2 * 512 * 768 * 192,
         size=3 << 20,
@@ -606,6 +608,7 @@
         project_body,
         "project",
         [sent_shape((ROWS, DIM)), sent_shape((2 * ROWS, DIM)), shape((ROWS, DIM))],
+        here=4,
         free=7,
         args=(*attend_all, attention_in, offsets[2:3], token_mask.reshape(ROWS, 1)),
         scalars=(f_pos,),
@@ -663,6 +666,7 @@
         + [sent_shape((ROWS, CA), F32)]
         + [sent_shape((ROWS, CA))] * 3,
         (*parts, gate, ffn, attention_out, project_full, act),
+        here=4,
         free=4,
         flops=4 * 2 * 128 * 768 * (192 + 128) + 8 * 2 * 128 * 128 * 768,
         size=5 << 20,
@@ -700,6 +704,7 @@
             atom_bias,
         ),
         scalars,
+        here=2,
         free=2,
         scratch=[
             pltpu.VMEM((token_count, CA), BF16),

time: 178 us -> 178 us (level)
  no operation moved by 1% of the time
where the time goes in v3:
time: 178 us; the launch traced here: 177 us
  Pallas kernels  57.1 us (32%)
  starting transfers between devices  51.4 us (29%)
  waiting for transfers between devices  26.7 us (15%)
  blocking collectives  17.1 us (10%)
  between operations  14.4 us (8%)
  local copies, waits for them, and re-layouts  8.6 us (5%)
    pallas_call x6, Pallas kernels, kernel_call(): pl.pallas_call(body, grid=(1,), out_shape=out_shape, in_specs=[pl.BlockSp...  27.8 us
    pallas_call x2, Pallas kernels, attention(): pl.pallas_call(functools.partial(attention_body, merge), grid=(HEADS,), o...  23.6 us
    ppermute x12, starting transfers between devices, x_shift(): return lax.ppermute(a, 'fsdp', [(i, (i + k) % NX) for i in range(NX)])  17.3 us
    all_gather x1, blocking collectives, y_collect(): return lax.all_gather(a, 'seq', axis=0, axis_index_groups=groups)  17.1 us
    ppermute x12, waiting for transfers between devices, x_shift(): return lax.ppermute(a, 'fsdp', [(i, (i + k) % NX) for i in range(NX)])  9.05 us
    ppermute x3, waiting for transfers between devices, z_shift(): return lax.ppermute(a, 'seq', pairs)  7.83 us
    ppermute x6, waiting for transfers between devices, y_shift(): return lax.ppermute(a, 'seq', pairs)  7.26 us
    ppermute x1, starting transfers between devices, per_device(): before = lax.ppermute(edge(ATOMS - RIM, ATOMS), 'seq', up)  5.98 us
  transfers between devices with their start and end apart: 33, of which 11 were waited for; matrix products, arithmetic and copies ran while one was open for 4% of the time, Pallas kernels for 27%

profile of v3, /device:TPU:1, one launch (start us, length us, event | category | flops | bytes accessed | tf_op | source)
XLA Modules:
  0.0 177.0 jit_solution(8921047245242796572)
XLA Ops:
  7.2 5.6 %prepare.1 = (bf16[128,960]{1,0:T(8,128)(2,1)S(1)}, bf16[128,960]{1,0:T(8,128)(2,1)}, bf16[128,960]{1,0:T(8,128)(2,1)S(1)}, bf16[128,960]{1,0:T(8,128)(2,1)S(1)}, bf16[4,4,128,1024]{3,2,1,0:T(8,128)(2,1)}) custom-call(s32[1]{0:T(128)} %bitcast.5.pos, bf16[128,768]{1,0:T(8,128)(2,1)} %bitcast.35, bf16[128,768]{1,0:T(8,128)(2,1)} %bitcast.39, ...), custom_call_target="tpu_custom_call" | custom-call | tf_op jit(solution)/shard_map/prepare/pallas_call | solution.py:542
  12.8 5.2 %all-to-all-start = ((bf16[4,4,128,1024]{3,2,1,0:T(8,128)(2,1)}), bf16[4,4,128,1024]{3,2,1,0:T(8,128)(2,1)}, u32[]{:S(2)}, u32[]{:S(2)}) async-start(bf16[4,4,128,1024]{3,2,1,0:T(8,128)(2,1)} %get-tuple-element.68), calls=%async_computation | async-start | bytes 8388608 | tf_op jit(solution)/shard_map/all_to_all | solution.py:62
  18.0 2.1 %collective-permute-start = (bf16[128,960]{1,0:T(8,128)(2,1)}, bf16[128,960]{1,0:T(8,128)(2,1)S(1)}, u32[]{:S(2)}, u32[]{:S(2)}) collective-permute-start(bf16[128,960]{1,0:T(8,128)(2,1)} %get-tuple-element.56), channel_id=1, source_target_pairs={{0,32},{32,64},{64,96},{96,0},{1,33},{33,65},{65,97},{97,1},{2,34}... | collective-permute-start | bytes 737288 | tf_op jit(solution)/shard_map/ppermute | solution.py:38
  20.0 2.5 %collective-permute-start.1 = (bf16[128,960]{1,0:T(8,128)(2,1)S(1)}, bf16[128,960]{1,0:T(8,128)(2,1)S(1)}, u32[]{:S(2)}, u32[]{:S(2)}) collective-permute-start(bf16[128,960]{1,0:T(8,128)(2,1)S(1)} %get-tuple-element.57), channel_id=1, source_target_pairs={{0,64},{32,96},{64,0},{96,32},{1,65},{33,97},{65,1},{97,33},{2,66}... | collective-permute-start | bytes 737288 | tf_op jit(solution)/shard_map/ppermute | solution.py:38
  22.5 1.2 collective-permute-start.2
  23.8 0.8 constant_dynamic-slice_fusion.offset
  24.6 1.6 copy.24.ada
  26.2 0.8 fusion.16
  27.0 7.1 %collective-permute-done.1.m2 = bf16[128,960]{1,0:T(8,128)(2,1)S(1)} collective-permute-done((bf16[128,960]{1,0:T(8,128)(2,1)S(1)}, bf16[128,960]{1,0:T(8,128)(2,1)S(1)}, u32[]{:S(2)}, u32[]{:S(2)}) %collective-permute-start.1) | collective-permute-done | bytes 245792 | tf_op jit(solution)/shard_map/ppermute | solution.py:38
  34.0 1.9 %adaptive.1 = (bf16[128,768]{1,0:T(8,128)(2,1)S(1)}, bf16[1184,128]{1,0:T(8,128)(2,1)}) custom-call(bf16[128,960]{1,0:T(8,128)(2,1)S(1)} %get-tuple-element.55.m0, bf16[128,960]{1,0:T(8,128)(2,1)S(1)} %collective-permute-done.m1, bf16[128,960]{1,0:T(8,128)(2,1)S(1)} %collective-permute-done.1.m2, bf16[128,960]{1,0:T(8,128)(2,1)S(1)} %collective-permute-done.2.m3, ...), custom_call_target="tpu_custom_call" | custom-call | flops 603979776 | bytes 3145728 | tf_op jit(solution)/shard_map/adaptive/pallas_call | solution.py:105
  35.9 1.1 collective-permute-start.3
  37.0 2.3 %collective-permute-start.4 = (bf16[128,768]{1,0:T(8,128)(2,1)S(1)}, bf16[128,768]{1,0:T(8,128)(2,1)S(1)}, u32[]{:S(2)}, u32[]{:S(2)}) collective-permute-start(bf16[128,768]{1,0:T(8,128)(2,1)S(1)} %get-tuple-element.59.a0), channel_id=1, source_target_pairs={{0,64},{32,96},{64,0},{96,32},{1,65},{33,97},{65,1},{97,33},{2,66}... | collective-permute-start | bytes 589832 | tf_op jit(solution)/shard_map/ppermute | solution.py:38
  39.3 0.7 collective-permute-start.5
  40.0 6.0 %collective-permute-start.6 = (bf16[112,128]{1,0:T(8,128)(2,1)S(1)}, bf16[112,128]{1,0:T(8,128)(2,1)S(1)}, u32[]{:S(2)}, u32[]{:S(2)}) collective-permute-start(bf16[112,128]{1,0:T(8,128)(2,1)S(1)} %pad_maximum_fusion.3), channel_id=1, source_target_pairs={{0,1},{1,2},{2,3},{3,4},{4,5},{5,6},{6,7},{7,8},{8,9},{9,10},{10,1... | collective-permute-start | bytes 86024 | tf_op jit(solution)/shard_map/ppermute | solution.py:579
  46.0 1.9 %collective-permute-start.7 = (bf16[112,128]{1,0:T(8,128)(2,1)S(1)}, bf16[112,128]{1,0:T(8,128)(2,1)S(1)}, u32[]{:S(2)}, u32[]{:S(2)}) collective-permute-start(bf16[112,128]{1,0:T(8,128)(2,1)S(1)} %pad_maximum_fusion.4), channel_id=1, source_target_pairs={{1,0},{2,1},{3,2},{4,3},{5,4},{6,5},{7,6},{8,7},{9,8},{10,9},{11,1... | collective-permute-start | bytes 86024 | tf_op jit(solution)/shard_map/ppermute | solution.py:580
  47.9 1.6 copy.25.weights
  49.5 0.8 dynamic-slice.1.offset
  50.3 0.1 copy.26.mask
  50.4 1.1 collective-permute-done.7.after
  51.6 2.1 %project.1 = (bf16[128,768]{1,0:T(8,128)(2,1)S(1)}, bf16[256,768]{1,0:T(8,128)(2,1)S(1)}, bf16[128,768]{1,0:T(8,128)(2,1)}) custom-call(s32[1]{0:T(128)} %bitcast.5.pos, bf16[128,768]{1,0:T(8,128)(2,1)S(1)} %get-tuple-element.59.a0, bf16[128,768]{1,0:T(8,128)(2,1)S(1)} %collective-permute-done.3.a1, bf16[128,768]{1,0:T(8,128)(2,1)S(1)} %collective-permute-done.4.a2, ...), custom_call_target="tpu_custom_call" | custom-call | flops 603979776 | bytes 4194304 | tf_op jit(solution)/shard_map/project/pallas_call | solution.py:105
  53.8 0.1 stack.64.pos
  53.9 0.1 stack.72.pos
  53.9 1.7 collective-permute-start.8
  55.6 3.7 %collective-permute-start.11 = (bf16[256,768]{1,0:T(8,128)(2,1)S(1)}, bf16[256,768]{1,0:T(8,128)(2,1)S(1)}, u32[]{:S(2)}, u32[]{:S(2)}) collective-permute-start(bf16[256,768]{1,0:T(8,128)(2,1)S(1)} %get-tuple-element.65.refs_0_), channel_id=1, source_target_pairs={{0,4},{1,5},{2,6},{3,7},{4,0},{5,1},{6,2},{7,3},{8,12},{9,13},{10,... | collective-permute-start | bytes 1179656 | tf_op jit(solution)/shard_map/ppermute | solution.py:56
  59.3 17.1 %all-gather = bf16[512,768]{1,0:T(8,128)(2,1)} all-gather(bf16[128,768]{1,0:T(8,128)(2,1)S(1)} %get-tuple-element.64), channel_id=2, replica_groups={{0,8,16,24},{1,9,17,25},{2,10,18,26},{3,11,19,27},{4,12,20,28},{5,13,21..., dimensions={0}, use_global_device_ids=true | all-gather | bytes 983040 | tf_op jit(solution)/shard_map/all_gather | solution.py:70
  76.4 2.5 %collective-permute-start.10 = (bf16[256,768]{1,0:T(8,128)(2,1)S(1)}, bf16[256,768]{1,0:T(8,128)(2,1)S(1)}, u32[]{:S(2)}, u32[]{:S(2)}) collective-permute-start(bf16[256,768]{1,0:T(8,128)(2,1)S(1)} %collective-permute-done.8.refs_1_), channel_id=1, source_target_pairs={{0,1},{1,0},{2,3},{3,2},{4,5},{5,4},{6,7},{7,6},{8,9},{9,8},{10,11... | collective-permute-start | bytes 1179656 | tf_op jit(solution)/shard_map/ppermute | solution.py:74
  79.0 1.3 collective-permute-done.10.refs_3_
  80.3 0.7 copy-done.11
  81.0 11.5 %attention_first.1 = (bf16[128,768]{1,0:T(8,128)(2,1)}, bf16[128,768]{1,0:T(8,128)(2,1)}, bf16[128,768]{1,0:T(8,128)(2,1)}, bf16[128,768]{1,0:T(8,128)(2,1)}, f3...) custom-call(s32[5]{0:T(128)S(1)} %stack.72.pos, ...), custom_call_target="tpu_custom_call" | custom-call | tf_op jit(solution)/shard_map/attention_first/pallas_call | solution.py:353
  92.6 0.5 collective-permute-start.13
  93.1 0.1 collective-permute-start.14
  93.4 0.7 slice.72
  94.1 0.1 slice_reduce_fusion
  94.2 0.7 pad_maximum_fusion.cond
  95.0 0.7 copy-done.9
  95.7 0.2 copy-done.10
  95.9 12.1 %attention_last.1 = (bf16[128,896]{1,0:T(8,128)(2,1)S(1)}, bf16[128,896]{1,0:T(8,128)(2,1)S(1)}, bf16[128,896]{1,0:T(8,128)(2,1)S(1)}, bf16[128,896]{1,0:T(8,128)(2,1)S(1)}) custom-call(s32[5]{0:T(128)S(1)} %stack.64.pos, bf16[4,128,768]{2,1,0:T(8,128)(2,1)} %bitcast.32, bf16[256,768]{1,0:T(8,128)(2,1)} %copy-done.5, bf16[256,768]{1,0:T(8,128)(2,1)} %copy-done.6, ...), custom_call_target="tpu_custom_call" | custom-call | tf_op jit(solution)/shard_map/attention_last/pallas_call | solution.py:353
  108.0 0.7 collective-permute-start.15
  108.7 0.7 collective-permute-start.16
  109.4 0.4 collective-permute-start.17
  109.9 3.2 %atom_first.1 = (bf16[7,128,128]{2,1,0:T(8,128)(2,1)}, bf16[768,128]{1,0:T(8,128)(2,1)}, f32[1120,128]{1,0:T(8,128)}, f32[1120,128]{1,0:T(8,128)}, bf16[1120,128]{1,0:T(8,128)(2,1)}) custom-call(s32[10]{0:T(128)S(1)} %multiply_minimum_fusion.starts, bf16[4,1184,128]{2,1,0:T(8,128)(2,1)} %bitcast.33, bf16[1120,128]{1,0:T(8,128)(2,1)} %pad_maximum_fusion.cond, ...), custom_call_target="tpu_custom_call" | custom-call | flops 73400320 | bytes 3145728 | tf_op jit(solution)/shard_map/atom_first/pallas_call | solution.py:105
  113.1 4.4 %hidden.1.refs_5_ = f32[512,768]{1,0:T(8,128)} custom-call(s32[1]{0:T(128)} %bitcast.5.pos, bf16[2,768,384]{2,1,0:T(8,128)(2,1)S(1)} %copy-done, bf16[384,768]{1,0:T(8,128)(2,1)S(1)} %copy-done.1, bf16[4,1184,128]{2,1,0:T(8,128)(2,1)} %bitcast.34), custom_call_target="tpu_custom_call" | custom-call | flops 905969664 | bytes 6291456 | tf_op jit(solution)/shard_map/hidden/pallas_call | solution.py:105
  117.5 5.1 %collective-permute-done.17.refs_3_ = bf16[128,896]{1,0:T(8,128)(2,1)S(1)} collective-permute-done((bf16[128,896]{1,0:T(8,128)(2,1)S(1)}, bf16[128,896]{1,0:T(8,128)(2,1)S(1)}, u32[]{:S(2)}, u32[]{:S(2)}) %collective-permute-start.17) | collective-permute-done | bytes 229408 | tf_op jit(solution)/shard_map/ppermute | solution.py:44
  122.6 3.4 %combine.1 = (f32[128,768]{1,0:T(8,128)}, bf16[128,768]{1,0:T(8,128)(2,1)S(1)}, bf16[128,768]{1,0:T(8,128)(2,1)S(1)}, bf16[128,768]{1,0:T(8,128)(2,1)S(1)}, f32[...) custom-call(bf16[128,896]{1,0:T(8,128)(2,1)S(1)} %get-tuple-element., ...), custom_call_target="tpu_custom_call" | custom-call | flops 452984832 | bytes 5242880 | tf_op jit(solution)/shard_map/combine/pallas_call | solution.py:105
  126.0 0.8 collective-permute-start.20
  126.9 2.5 %collective-permute-start.19 = (bf16[128,128]{1,0:T(8,128)(2,1)S(1)}, bf16[128,128]{1,0:T(8,128)(2,1)S(1)}, u32[]{:S(2)}, u32[]{:S(2)}) collective-permute-start(bf16[128,128]{1,0:T(8,128)(2,1)S(1)} %get-tuple-element.90), channel_id=1, source_target_pairs={{0,64},{32,96},{64,0},{96,32},{1,65},{33,97},{65,1},{97,33},{2,66}... | collective-permute-start | bytes 98312 | tf_op jit(solution)/shard_map/ppermute | solution.py:38
  129.3 1.2 collective-permute-start.18
  130.5 0.8 collective-permute-done.19
  131.3 1.2 collective-permute-done.18
  132.6 0.8 collective-permute-start.22
  133.4 2.0 %collective-permute-start.23 = (bf16[128,128]{1,0:T(8,128)(2,1)S(1)}, bf16[128,128]{1,0:T(8,128)(2,1)S(1)}, u32[]{:S(2)}, u32[]{:S(2)}) collective-permute-start(bf16[128,128]{1,0:T(8,128)(2,1)S(1)} %get-tuple-element.109), channel_id=1, source_target_pairs={{0,24},{1,25},{2,26},{3,27},{4,28},{5,29},{6,30},{7,31},{8,0},{9,1... | collective-permute-start | bytes 98312 | tf_op jit(solution)/shard_map/ppermute | solution.py:44
  135.4 1.2 collective-permute-done.21
  136.5 0.4 collective-permute-done.22
  136.9 0.5 collective-permute-done.23
  137.5 1.6 collective-permute-start.24
  139.1 3.2 %collective-permute-start.25 = (bf16[512,128]{1,0:T(8,128)(2,1)S(1)}, bf16[512,128]{1,0:T(8,128)(2,1)S(1)}, u32[]{:S(2)}, u32[]{:S(2)}) collective-permute-start(bf16[512,128]{1,0:T(8,128)(2,1)S(1)} %pad_maximum_fusion.1), channel_id=1, source_target_pairs={{0,4},{1,5},{2,6},{3,7},{4,0},{5,1},{6,2},{7,3},{8,12},{9,13},{10,... | collective-permute-start | bytes 393224 | tf_op jit(solution)/shard_map/ppermute | solution.py:52
  142.2 0.5 collective-permute-start.26
  142.7 1.7 collective-permute-done.24
  144.4 6.2 %collective-permute-done.25 = bf16[512,128]{1,0:T(8,128)(2,1)S(1)} collective-permute-done((bf16[512,128]{1,0:T(8,128)(2,1)S(1)}, bf16[512,128]{1,0:T(8,128)(2,1)S(1)}, u32[]{:S(2)}, u32[]{:S(2)}) %collective-permute-start.25) | collective-permute-done | bytes 131104 | tf_op jit(solution)/shard_map/ppermute | solution.py:52
  150.7 2.6 %collective-permute-start.27 = (bf16[2048,128]{1,0:T(8,128)(2,1)S(1)}, bf16[2048,128]{1,0:T(8,128)(2,1)S(1)}, u32[]{:S(2)}, u32[]{:S(2)}) collective-permute-start(bf16[2048,128]{1,0:T(8,128)(2,1)S(1)} %constant_dynamic-update-slice_fusion.near), channel_id=1, source_target_pairs={{0,1},{1,0},{2,3},{3,2},{4,5},{5,4},{6,7},{7,6},{8,9},{9,8},{10,11... | collective-permute-start | bytes 1572872 | tf_op jit(solution)/shard_map/ppermute | solution.py:74
  153.3 2.5 %collective-permute-start.28 = (bf16[128,768]{1,0:T(8,128)(2,1)S(1)}, bf16[128,768]{1,0:T(8,128)(2,1)S(1)}, u32[]{:S(2)}, u32[]{:S(2)}) collective-permute-start(bf16[128,768]{1,0:T(8,128)(2,1)S(1)} %get-tuple-element.101), channel_id=1, source_target_pairs={{0,96},{32,0},{64,32},{96,64},{1,97},{33,1},{65,33},{97,65},{2,98}... | collective-permute-start | bytes 589832 | tf_op jit(solution)/shard_map/ppermute | solution.py:38
  155.8 0.6 collective-permute-start.30
  156.5 12.8 %atoms.1 = f32[3,1,1024]{2,1,0:T(1,128)} custom-call(s32[4]{0:T(128)S(1)} %pad_add_fusion.pos, s32[10]{0:T(128)S(1)} %multiply_minimum_fusion.starts, s32[2,32]{1,0:T(2,128)S(1)} %bitcast.30, bf16[2048,128]{1,0:T(8,128)(2,1)S(1)} %constant_dynamic-update-slice_fusion.near, bf16[2048,128]{1,0:T(8,128)(2,1)S(1)} %collective-permute-done.27.far, ...), custom_call_target="tpu_custom_call" | custom-call | flops 367001600 | bytes 6291456 | tf_op jit(solution)/shard_map/atoms/pallas_call | solution.py:105
  169.4 0.8 fusion
  (89 shorter events, 0.8 us)
Async XLA Ops:
  12.8 10.8 %copy-start.18 = (s32[1024]{0:T(1024)S(1)}, s32[1024]{0:T(1024)}, u32[]{:S(2)}) copy-start(s32[1024]{0:T(1024)} %param.33) | copy-start | bytes 12292
  12.8 11.0 %copy-start.16 = (bf16[7,128,32]{1,2,0:T(8,128)(2,1)S(1)}, bf16[7,128,32]{1,2,0:T(8,128)(2,1)}, u32[]{:S(2)}) copy-start(bf16[7,128,32]{1,2,0:T(8,128)(2,1)} %param.34) | copy-start | bytes 172036
  12.8 11.0 %copy-start.17 = (bf16[192,128]{1,0:T(8,128)(2,1)S(1)}, bf16[192,128]{1,0:T(8,128)(2,1)}, u32[]{:S(2)}) copy-start(bf16[192,128]{1,0:T(8,128)(2,1)} %param.35) | copy-start | bytes 147460
  12.8 67.5 %all-to-all-start = ((bf16[4,4,128,1024]{3,2,1,0:T(8,128)(2,1)}), bf16[4,4,128,1024]{3,2,1,0:T(8,128)(2,1)}, u32[]{:S(2)}, u32[]{:S(2)}) async-start(bf16[4,4,128,1024]{3,2,1,0:T(8,128)(2,1)} %get-tuple-element.68), calls=%async_computation | async-start | bytes 8388608 | tf_op jit(solution)/shard_map/all_to_all | solution.py:62
  18.0 91.9 %all-gather.4.cloned.1.call-start = ((), (), s32[]{:S(2)}) async-start(), calls=%async_computation.1 | async-start | bytes 1515520 | tf_op jit(solution)/shard_map/all_gather | solution.py:625
  18.0 9.0 %collective-permute-start = (bf16[128,960]{1,0:T(8,128)(2,1)}, bf16[128,960]{1,0:T(8,128)(2,1)S(1)}, u32[]{:S(2)}, u32[]{:S(2)}) collective-permute-start(bf16[128,960]{1,0:T(8,128)(2,1)} %get-tuple-element.56), channel_id=1, source_target_pairs={{0,32},{32,64},{64,96},{96,0},{1,33},{33,65},{65,97},{97,1},{2,34}... | collective-permute-start | bytes 737288 | tf_op jit(solution)/shard_map/ppermute | solution.py:38
  20.0 14.0 %collective-permute-start.1 = (bf16[128,960]{1,0:T(8,128)(2,1)S(1)}, bf16[128,960]{1,0:T(8,128)(2,1)S(1)}, u32[]{:S(2)}, u32[]{:S(2)}) collective-permute-start(bf16[128,960]{1,0:T(8,128)(2,1)S(1)} %get-tuple-element.57), channel_id=1, source_target_pairs={{0,64},{32,96},{64,0},{96,32},{1,65},{33,97},{65,1},{97,33},{2,66}... | collective-permute-start | bytes 737288 | tf_op jit(solution)/shard_map/ppermute | solution.py:38
  22.5 11.5 %collective-permute-start.2 = (bf16[128,960]{1,0:T(8,128)(2,1)S(1)}, bf16[128,960]{1,0:T(8,128)(2,1)S(1)}, u32[]{:S(2)}, u32[]{:S(2)}) collective-permute-start(bf16[128,960]{1,0:T(8,128)(2,1)S(1)} %get-tuple-element.58), channel_id=1, source_target_pairs={{0,96},{32,0},{64,32},{96,64},{1,97},{33,1},{65,33},{97,65},{2,98}... | collective-permute-start | bytes 737288 | tf_op jit(solution)/shard_map/ppermute | solution.py:38
  35.9 14.4 %copy-start.19 = (s32[128]{0:T(128)S(1)}, s32[128]{0:T(128)}, u32[]{:S(2)}) copy-start(s32[128]{0:T(128)} %param.22) | copy-start | bytes 1540
  35.9 15.7 %collective-permute-start.3 = (bf16[128,768]{1,0:T(8,128)(2,1)S(1)}, bf16[128,768]{1,0:T(8,128)(2,1)S(1)}, u32[]{:S(2)}, u32[]{:S(2)}) collective-permute-start(bf16[128,768]{1,0:T(8,128)(2,1)S(1)} %get-tuple-element.59.a0), channel_id=1, source_target_pairs={{0,32},{32,64},{64,96},{96,0},{1,33},{33,65},{65,97},{97,1},{2,34}... | collective-permute-start | bytes 589832 | tf_op jit(solution)/shard_map/ppermute | solution.py:38
  37.0 14.6 %collective-permute-start.4 = (bf16[128,768]{1,0:T(8,128)(2,1)S(1)}, bf16[128,768]{1,0:T(8,128)(2,1)S(1)}, u32[]{:S(2)}, u32[]{:S(2)}) collective-permute-start(bf16[128,768]{1,0:T(8,128)(2,1)S(1)} %get-tuple-element.59.a0), channel_id=1, source_target_pairs={{0,64},{32,96},{64,0},{96,32},{1,65},{33,97},{65,1},{97,33},{2,66}... | collective-permute-start | bytes 589832 | tf_op jit(solution)/shard_map/ppermute | solution.py:38
  39.3 12.3 %collective-permute-start.5 = (bf16[128,768]{1,0:T(8,128)(2,1)S(1)}, bf16[128,768]{1,0:T(8,128)(2,1)S(1)}, u32[]{:S(2)}, u32[]{:S(2)}) collective-permute-start(bf16[128,768]{1,0:T(8,128)(2,1)S(1)} %get-tuple-element.59.a0), channel_id=1, source_target_pairs={{0,96},{32,0},{64,32},{96,64},{1,97},{33,1},{65,33},{97,65},{2,98}... | collective-permute-start | bytes 589832 | tf_op jit(solution)/shard_map/ppermute | solution.py:38
  40.0 10.5 %collective-permute-start.6 = (bf16[112,128]{1,0:T(8,128)(2,1)S(1)}, bf16[112,128]{1,0:T(8,128)(2,1)S(1)}, u32[]{:S(2)}, u32[]{:S(2)}) collective-permute-start(bf16[112,128]{1,0:T(8,128)(2,1)S(1)} %pad_maximum_fusion.3), channel_id=1, source_target_pairs={{0,1},{1,2},{2,3},{3,4},{4,5},{5,6},{6,7},{7,8},{8,9},{9,10},{10,1... | collective-permute-start | bytes 86024 | tf_op jit(solution)/shard_map/ppermute | solution.py:579
  46.0 5.6 %collective-permute-start.7 = (bf16[112,128]{1,0:T(8,128)(2,1)S(1)}, bf16[112,128]{1,0:T(8,128)(2,1)S(1)}, u32[]{:S(2)}, u32[]{:S(2)}) collective-permute-start(bf16[112,128]{1,0:T(8,128)(2,1)S(1)} %pad_maximum_fusion.4), channel_id=1, source_target_pairs={{1,0},{2,1},{3,2},{4,3},{5,4},{6,5},{7,6},{8,7},{9,8},{10,9},{11,1... | collective-permute-start | bytes 86024 | tf_op jit(solution)/shard_map/ppermute | solution.py:580
  50.4 43.7 %copy-start.14 = (bf16[112,128]{1,0:T(8,128)(2,1)}, bf16[112,128]{1,0:T(8,128)(2,1)S(1)}, u32[]{:S(2)}) copy-start(bf16[112,128]{1,0:T(8,128)(2,1)S(1)} %collective-permute-done.6.before) | copy-start | bytes 86020
  51.6 41.0 %copy-start.15 = (bf16[112,128]{1,0:T(8,128)(2,1)}, bf16[112,128]{1,0:T(8,128)(2,1)S(1)}, u32[]{:S(2)}) copy-start(bf16[112,128]{1,0:T(8,128)(2,1)S(1)} %collective-permute-done.7.after) | copy-start | bytes 86020
  53.7 26.6 %copy-start.2 = (bf16[256,768]{1,0:T(8,128)(2,1)}, bf16[256,768]{1,0:T(8,128)(2,1)S(1)}, u32[]{:S(2)}) copy-start(bf16[256,768]{1,0:T(8,128)(2,1)S(1)} %get-tuple-element.65.refs_0_) | copy-start | bytes 1179652
  53.9 22.5 %collective-permute-start.8 = (bf16[256,768]{1,0:T(8,128)(2,1)S(1)}, bf16[256,768]{1,0:T(8,128)(2,1)S(1)}, u32[]{:S(2)}, u32[]{:S(2)}) collective-permute-start(bf16[256,768]{1,0:T(8,128)(2,1)S(1)} %get-tuple-element.65.refs_0_), channel_id=1, source_target_pairs={{0,2},{1,3},{2,0},{3,1},{4,6},{5,7},{6,4},{7,5},{8,10},{9,11},{10,... | collective-permute-start | bytes 1179656 | tf_op jit(solution)/shard_map/ppermute | solution.py:56
  55.6 23.4 %collective-permute-start.9 = (bf16[256,768]{1,0:T(8,128)(2,1)S(1)}, bf16[256,768]{1,0:T(8,128)(2,1)S(1)}, u32[]{:S(2)}, u32[]{:S(2)}) collective-permute-start(bf16[256,768]{1,0:T(8,128)(2,1)S(1)} %get-tuple-element.65.refs_0_), channel_id=1, source_target_pairs={{0,1},{1,0},{2,3},{3,2},{4,5},{5,4},{6,7},{7,6},{8,9},{9,8},{10,11... | collective-permute-start | bytes 1179656 | tf_op jit(solution)/shard_map/ppermute | solution.py:74
  55.6 37.0 %collective-permute-start.11 = (bf16[256,768]{1,0:T(8,128)(2,1)S(1)}, bf16[256,768]{1,0:T(8,128)(2,1)S(1)}, u32[]{:S(2)}, u32[]{:S(2)}) collective-permute-start(bf16[256,768]{1,0:T(8,128)(2,1)S(1)} %get-tuple-element.65.refs_0_), channel_id=1, source_target_pairs={{0,4},{1,5},{2,6},{3,7},{4,0},{5,1},{6,2},{7,3},{8,12},{9,13},{10,... | collective-permute-start | bytes 1179656 | tf_op jit(solution)/shard_map/ppermute | solution.py:56
  59.3 33.3 %collective-permute-start.12 = (bf16[256,768]{1,0:T(8,128)(2,1)S(1)}, bf16[256,768]{1,0:T(8,128)(2,1)S(1)}, u32[]{:S(2)}, u32[]{:S(2)}) collective-permute-start(bf16[256,768]{1,0:T(8,128)(2,1)S(1)} %get-tuple-element.65.refs_0_), channel_id=1, source_target_pairs={{0,6},{1,7},{2,4},{3,5},{4,2},{5,3},{6,0},{7,1},{8,14},{9,15},{10,... | collective-permute-start | bytes 1179656 | tf_op jit(solution)/shard_map/ppermute | solution.py:56
  76.4 3.9 %copy-start.7 = (bf16[256,768]{1,0:T(8,128)(2,1)}, bf16[256,768]{1,0:T(8,128)(2,1)S(1)}, u32[]{:S(2)}) copy-start(bf16[256,768]{1,0:T(8,128)(2,1)S(1)} %collective-permute-done.8.refs_1_) | copy-start | bytes 1179652
  76.4 3.8 %collective-permute-start.10 = (bf16[256,768]{1,0:T(8,128)(2,1)S(1)}, bf16[256,768]{1,0:T(8,128)(2,1)S(1)}, u32[]{:S(2)}, u32[]{:S(2)}) collective-permute-start(bf16[256,768]{1,0:T(8,128)(2,1)S(1)} %collective-permute-done.8.refs_1_), channel_id=1, source_target_pairs={{0,1},{1,0},{2,3},{3,2},{4,5},{5,4},{6,7},{7,6},{8,9},{9,8},{10,11... | collective-permute-start | bytes 1179656 | tf_op jit(solution)/shard_map/ppermute | solution.py:74
  78.9 15.3 %copy-start.12 = (bf16[1024,128]{1,0:T(8,128)(2,1)S(1)}, bf16[1024,128]{1,0:T(8,128)(2,1)}, u32[]{:S(2)}) copy-start(bf16[1024,128]{1,0:T(8,128)(2,1)} %param.30) | copy-start | bytes 786436
  79.0 1.3 copy-start.8
  80.3 0.8 copy-start.11
  92.6 2.4 %copy-start.5 = (bf16[256,768]{1,0:T(8,128)(2,1)}, bf16[256,768]{1,0:T(8,128)(2,1)S(1)}, u32[]{:S(2)}) copy-start(bf16[256,768]{1,0:T(8,128)(2,1)S(1)} %collective-permute-done.11.refs_0_) | copy-start | bytes 1179652
  92.6 2.4 %copy-start.6 = (bf16[256,768]{1,0:T(8,128)(2,1)}, bf16[256,768]{1,0:T(8,128)(2,1)S(1)}, u32[]{:S(2)}) copy-start(bf16[256,768]{1,0:T(8,128)(2,1)S(1)} %collective-permute-done.12.refs_1_) | copy-start | bytes 1179652
  92.6 2.3 %collective-permute-start.13 = (bf16[256,768]{1,0:T(8,128)(2,1)S(1)}, bf16[256,768]{1,0:T(8,128)(2,1)S(1)}, u32[]{:S(2)}, u32[]{:S(2)}) collective-permute-start(bf16[256,768]{1,0:T(8,128)(2,1)S(1)} %collective-permute-done.11.refs_0_), channel_id=1, source_target_pairs={{0,1},{1,0},{2,3},{3,2},{4,5},{5,4},{6,7},{7,6},{8,9},{9,8},{10,11... | collective-permute-start | bytes 1179656 | tf_op jit(solution)/shard_map/ppermute | solution.py:74
  93.1 1.9 %collective-permute-start.14 = (bf16[256,768]{1,0:T(8,128)(2,1)S(1)}, bf16[256,768]{1,0:T(8,128)(2,1)S(1)}, u32[]{:S(2)}, u32[]{:S(2)}) collective-permute-start(bf16[256,768]{1,0:T(8,128)(2,1)S(1)} %collective-permute-done.12.refs_1_), channel_id=1, source_target_pairs={{0,1},{1,0},{2,3},{3,2},{4,5},{5,4},{6,7},{7,6},{8,9},{9,8},{10,11... | collective-permute-start | bytes 1179656 | tf_op jit(solution)/shard_map/ppermute | solution.py:74
  93.4 14.6 %copy-start.13 = (s32[10,112]{1,0:T(8,128)}, s32[10,112]{1,0:T(8,128)S(1)}, u32[]{:S(2)}) copy-start(s32[10,112]{1,0:T(8,128)S(1)} %reshape.25.tokens) | copy-start | bytes 13444
  95.0 0.7 copy-start.9
  95.0 0.9 copy-start.10
  95.9 17.2 %copy-start.1 = (bf16[384,768]{1,0:T(8,128)(2,1)S(1)}, bf16[384,768]{1,0:T(8,128)(2,1)}, u32[]{:S(2)}) copy-start(bf16[384,768]{1,0:T(8,128)(2,1)} %w_out.1) | copy-start | bytes 1769476
  107.9 5.2 %copy-start = (bf16[2,768,384]{2,1,0:T(8,128)(2,1)S(1)}, bf16[2,768,384]{2,1,0:T(8,128)(2,1)}, u32[]{:S(2)}) copy-start(bf16[2,768,384]{2,1,0:T(8,128)(2,1)} %w_in.1) | copy-start | bytes 3538948
  108.0 9.5 %collective-permute-start.15 = (bf16[128,896]{1,0:T(8,128)(2,1)S(1)}, bf16[128,896]{1,0:T(8,128)(2,1)S(1)}, u32[]{:S(2)}, u32[]{:S(2)}) collective-permute-start(bf16[128,896]{1,0:T(8,128)(2,1)S(1)} %get-tuple-element.80), channel_id=1, source_target_pairs={{0,24},{1,25},{2,26},{3,27},{4,28},{5,29},{6,30},{7,31},{8,0},{9,1... | collective-permute-start | bytes 688136 | tf_op jit(solution)/shard_map/ppermute | solution.py:44
  108.7 8.8 %collective-permute-start.16 = (bf16[128,896]{1,0:T(8,128)(2,1)S(1)}, bf16[128,896]{1,0:T(8,128)(2,1)S(1)}, u32[]{:S(2)}, u32[]{:S(2)}) collective-permute-start(bf16[128,896]{1,0:T(8,128)(2,1)S(1)} %get-tuple-element.81), channel_id=1, source_target_pairs={{0,16},{1,17},{2,18},{3,19},{4,20},{5,21},{6,22},{7,23},{8,24},{9,... | collective-permute-start | bytes 688136 | tf_op jit(solution)/shard_map/ppermute | solution.py:44
  109.4 13.2 %collective-permute-start.17 = (bf16[128,896]{1,0:T(8,128)(2,1)S(1)}, bf16[128,896]{1,0:T(8,128)(2,1)S(1)}, u32[]{:S(2)}, u32[]{:S(2)}) collective-permute-start(bf16[128,896]{1,0:T(8,128)(2,1)S(1)} %get-tuple-element.82), channel_id=1, source_target_pairs={{0,8},{1,9},{2,10},{3,11},{4,12},{5,13},{6,14},{7,15},{8,16},{9,17... | collective-permute-start | bytes 688136 | tf_op jit(solution)/shard_map/ppermute | solution.py:44
  122.6 33.8 %copy-start.3 = (s32[32,2]{0,1:T(2,128)S(1)}, s32[32,2]{0,1:T(2,128)}, u32[]{:S(2)}) copy-start(s32[32,2]{0,1:T(2,128)} %param.32) | copy-start | bytes 772
  126.0 4.5 %collective-permute-start.20 = (bf16[128,128]{1,0:T(8,128)(2,1)S(1)}, bf16[128,128]{1,0:T(8,128)(2,1)S(1)}, u32[]{:S(2)}, u32[]{:S(2)}) collective-permute-start(bf16[128,128]{1,0:T(8,128)(2,1)S(1)} %get-tuple-element.91), channel_id=1, source_target_pairs={{0,32},{32,64},{64,96},{96,0},{1,33},{33,65},{65,97},{97,1},{2,34}... | collective-permute-start | bytes 98312 | tf_op jit(solution)/shard_map/ppermute | solution.py:38
  126.9 4.4 %collective-permute-start.19 = (bf16[128,128]{1,0:T(8,128)(2,1)S(1)}, bf16[128,128]{1,0:T(8,128)(2,1)S(1)}, u32[]{:S(2)}, u32[]{:S(2)}) collective-permute-start(bf16[128,128]{1,0:T(8,128)(2,1)S(1)} %get-tuple-element.90), channel_id=1, source_target_pairs={{0,64},{32,96},{64,0},{96,32},{1,65},{33,97},{65,1},{97,33},{2,66}... | collective-permute-start | bytes 98312 | tf_op jit(solution)/shard_map/ppermute | solution.py:38
  129.3 3.1 %collective-permute-start.18 = (bf16[128,128]{1,0:T(8,128)(2,1)S(1)}, bf16[128,128]{1,0:T(8,128)(2,1)S(1)}, u32[]{:S(2)}, u32[]{:S(2)}) collective-permute-start(bf16[128,128]{1,0:T(8,128)(2,1)S(1)} %get-tuple-element.89), channel_id=1, source_target_pairs={{0,96},{32,0},{64,32},{96,64},{1,97},{33,1},{65,33},{97,65},{2,98}... | collective-permute-start | bytes 98312 | tf_op jit(solution)/shard_map/ppermute | solution.py:38
  132.5 4.1 %collective-permute-start.21 = (bf16[128,128]{1,0:T(8,128)(2,1)S(1)}, bf16[128,128]{1,0:T(8,128)(2,1)S(1)}, u32[]{:S(2)}, u32[]{:S(2)}) collective-permute-start(bf16[128,128]{1,0:T(8,128)(2,1)S(1)} %get-tuple-element.109), channel_id=1, source_target_pairs={{0,8},{1,9},{2,10},{3,11},{4,12},{5,13},{6,14},{7,15},{8,16},{9,17... | collective-permute-start | bytes 98312 | tf_op jit(solution)/shard_map/ppermute | solution.py:44
  132.6 4.4 %collective-permute-start.22 = (bf16[128,128]{1,0:T(8,128)(2,1)S(1)}, bf16[128,128]{1,0:T(8,128)(2,1)S(1)}, u32[]{:S(2)}, u32[]{:S(2)}) collective-permute-start(bf16[128,128]{1,0:T(8,128)(2,1)S(1)} %get-tuple-element.109), channel_id=1, source_target_pairs={{0,16},{1,17},{2,18},{3,19},{4,20},{5,21},{6,22},{7,23},{8,24},{9,... | collective-permute-start | bytes 98312 | tf_op jit(solution)/shard_map/ppermute | solution.py:44
  133.4 4.1 %collective-permute-start.23 = (bf16[128,128]{1,0:T(8,128)(2,1)S(1)}, bf16[128,128]{1,0:T(8,128)(2,1)S(1)}, u32[]{:S(2)}, u32[]{:S(2)}) collective-permute-start(bf16[128,128]{1,0:T(8,128)(2,1)S(1)} %get-tuple-element.109), channel_id=1, source_target_pairs={{0,24},{1,25},{2,26},{3,27},{4,28},{5,29},{6,30},{7,31},{8,0},{9,1... | collective-permute-start | bytes 98312 | tf_op jit(solution)/shard_map/ppermute | solution.py:44
  137.5 6.9 %collective-permute-start.24 = (bf16[512,128]{1,0:T(8,128)(2,1)S(1)}, bf16[512,128]{1,0:T(8,128)(2,1)S(1)}, u32[]{:S(2)}, u32[]{:S(2)}) collective-permute-start(bf16[512,128]{1,0:T(8,128)(2,1)S(1)} %pad_maximum_fusion.1), channel_id=1, source_target_pairs={{0,2},{1,3},{2,4},{3,5},{4,6},{5,7},{6,0},{7,1},{8,10},{9,11},{10,... | collective-permute-start | bytes 393224 | tf_op jit(solution)/shard_map/ppermute | solution.py:52
  139.1 11.5 %collective-permute-start.25 = (bf16[512,128]{1,0:T(8,128)(2,1)S(1)}, bf16[512,128]{1,0:T(8,128)(2,1)S(1)}, u32[]{:S(2)}, u32[]{:S(2)}) collective-permute-start(bf16[512,128]{1,0:T(8,128)(2,1)S(1)} %pad_maximum_fusion.1), channel_id=1, source_target_pairs={{0,4},{1,5},{2,6},{3,7},{4,0},{5,1},{6,2},{7,3},{8,12},{9,13},{10,... | collective-permute-start | bytes 393224 | tf_op jit(solution)/shard_map/ppermute | solution.py:52
  142.2 8.4 %collective-permute-start.26 = (bf16[512,128]{1,0:T(8,128)(2,1)S(1)}, bf16[512,128]{1,0:T(8,128)(2,1)S(1)}, u32[]{:S(2)}, u32[]{:S(2)}) collective-permute-start(bf16[512,128]{1,0:T(8,128)(2,1)S(1)} %pad_maximum_fusion.1), channel_id=1, source_target_pairs={{0,6},{1,7},{2,0},{3,1},{4,2},{5,3},{6,4},{7,5},{8,14},{9,15},{10,... | collective-permute-start | bytes 393224 | tf_op jit(solution)/shard_map/ppermute | solution.py:52
  150.7 5.8 %collective-permute-start.27 = (bf16[2048,128]{1,0:T(8,128)(2,1)S(1)}, bf16[2048,128]{1,0:T(8,128)(2,1)S(1)}, u32[]{:S(2)}, u32[]{:S(2)}) collective-permute-start(bf16[2048,128]{1,0:T(8,128)(2,1)S(1)} %constant_dynamic-update-slice_fusion.near), channel_id=1, source_target_pairs={{0,1},{1,0},{2,3},{3,2},{4,5},{5,4},{6,7},{7,6},{8,9},{9,8},{10,11... | collective-permute-start | bytes 1572872 | tf_op jit(solution)/shard_map/ppermute | solution.py:74
  153.3 16.0 %collective-permute-start.28 = (bf16[128,768]{1,0:T(8,128)(2,1)S(1)}, bf16[128,768]{1,0:T(8,128)(2,1)S(1)}, u32[]{:S(2)}, u32[]{:S(2)}) collective-permute-start(bf16[128,768]{1,0:T(8,128)(2,1)S(1)} %get-tuple-element.101), channel_id=1, source_target_pairs={{0,96},{32,0},{64,32},{96,64},{1,97},{33,1},{65,33},{97,65},{2,98}... | collective-permute-start | bytes 589832 | tf_op jit(solution)/shard_map/ppermute | solution.py:38
  155.8 13.5 %collective-permute-start.29 = (bf16[128,768]{1,0:T(8,128)(2,1)S(1)}, bf16[128,768]{1,0:T(8,128)(2,1)S(1)}, u32[]{:S(2)}, u32[]{:S(2)}) collective-permute-start(bf16[128,768]{1,0:T(8,128)(2,1)S(1)} %get-tuple-element.102), channel_id=1, source_target_pairs={{0,64},{32,96},{64,0},{96,32},{1,65},{33,97},{65,1},{97,33},{2,66}... | collective-permute-start | bytes 589832 | tf_op jit(solution)/shard_map/ppermute | solution.py:38
  155.8 13.5 %collective-permute-start.30 = (bf16[128,768]{1,0:T(8,128)(2,1)S(1)}, bf16[128,768]{1,0:T(8,128)(2,1)S(1)}, u32[]{:S(2)}, u32[]{:S(2)}) collective-permute-start(bf16[128,768]{1,0:T(8,128)(2,1)S(1)} %get-tuple-element.103), channel_id=1, source_target_pairs={{0,32},{32,64},{64,96},{96,0},{1,33},{33,65},{65,97},{97,1},{2,34}... | collective-permute-start | bytes 589832 | tf_op jit(solution)/shard_map/ppermute | solution.py:38
  156.5 12.9 %copy-start.4 = (f32[128,768]{1,0:T(8,128)S(1)}, f32[128,768]{1,0:T(8,128)}, u32[]{:S(2)}) copy-start(f32[128,768]{1,0:T(8,128)} %get-tuple-element.87) | copy-start | bytes 1179652
Sparse Core Ops, SparseCore 0:
  53.8 28.2 all-gather.3
